TPU v7x, 32 devices: a whole 2x2x4 slice. The times are simulated.
32 devices in a mesh: band: 4 (over y, core), pw: 8 (over z, x).
Axes of the slice: x: 2, y: 2, z: 4, core: 2. Of those that a mesh axis runs over, the one named last changes fastest.
Arguments:
- response: bfloat16 [4, 2, 62464], P('band', None, 'pw'), may hold values from -6 to 6
- panel: bfloat16 [256, 2, 62464], P('band', None, 'pw'), may hold values from -0.0234375 to 0.0234375
- energies: float32 [256], replicated, may hold values from -1 to 0
- offset: int32 [1], replicated, may hold values from 0 to 252
- grid_map: int32 [62464], P('pw'), may hold values from 0 to 511999, as said below
- potential: float32 [160, 160, 160], P(None, 'pw'), may hold values from -6 to 2
- contact: float32 [160, 160, 160], P(None, 'pw'), may hold values from -10240 to 10240
Outputs:
- residual: bfloat16 [4, 2, 62464], P('band', None, 'pw')
- response_next: bfloat16 [4, 2, 62464], P('band', None, 'pw')
Inputs may be any that keep to these rules, and one draw needn't show every extreme that they name: `grid_map`: within each aligned block of 7808 entries (the plane waves of block p) the entries are distinct cells lx * 160 * 160 + ly * 160 + lz of the 20 grid planes gx = p + lx * 8; they are the 7808 cells of those planes with the smallest fx^2 + fy^2 + fz^2 in folded coordinates, ties among equal radii taken in any way.
All inputs are finite; a program needn't handle non-finite values.
Results may differ from a plain program's by a relative error of at most 0.015.
Values may be sent and summed in bfloat16 or wider, within the bound.
No kernel may reach another device: no remote copies, remote signals or barrier semaphores. Data moves between devices by JAX's collectives and lax.ppermute only.
A program may use at most 256 MiB of HBM per device.

v0:
```python
import math

import jax
import jax.numpy as jnp
from jax import lax
from jax.sharding import PartitionSpec as P


def fourier_table(length, sign_value):
    indices = jnp.arange(length, dtype=jnp.int32)
    products = indices[:, None] * indices[None, :] % length
    angles = products.astype(jnp.float32) * (2.0 * math.pi / length)
    scaling = 1.0 / math.sqrt(length)
    cosine = jnp.cos(angles) * scaling
    sine_part = sign_value * jnp.sin(angles) * scaling
    factor = jnp.stack([jnp.stack([cosine, sine_part]), jnp.stack([-sine_part, cosine])])
    return factor.astype(jnp.bfloat16)


def along_z(field, factor):
    return jnp.einsum("bcxyk,cdkw->bdxyw", field, factor, preferred_element_type=jnp.float32)


def along_y(field, factor):
    return jnp.einsum("bcxky,cdkw->bdxwy", field, factor, preferred_element_type=jnp.float32)


def along_x(field, factor):
    return jnp.einsum("bckyz,cdkw->bdwyz", field, factor, preferred_element_type=jnp.float32)


def folded_square(coord, grid_size):
    half_grid = grid_size // 2
    folded = jnp.where(coord >= half_grid, coord - grid_size, coord)
    return folded * folded


def slab_planes(coeffs, grid_map, factor, slab_size, grid_size):
    row_total = coeffs.shape[0]
    flat = (
        jnp.zeros((row_total, 2, slab_size * grid_size * grid_size), jnp.bfloat16)
        .at[:, :, grid_map]
        .set(coeffs)
    )
    field = flat.reshape(row_total, 2, slab_size, grid_size, grid_size)
    field = along_z(field, factor).astype(jnp.bfloat16)
    return along_y(field, factor).astype(jnp.bfloat16)


def correlation_of(panel, terms):
    other = jnp.stack([terms[:, 1], -terms[:, 0]], axis=1)
    swapped = jnp.stack([terms, other])
    return jnp.einsum("mcj,dncj->dmn", panel, swapped, preferred_element_type=jnp.float32)


def on_device(response, panel, energies, offset, grid_map, potential, contact):
    bands_here = response.shape[0]
    rows_here = panel.shape[0]
    grid_size = potential.shape[0]
    slab_size = potential.shape[1]
    block_count = lax.axis_size("pw")
    bands_all = bands_here * lax.axis_size("band")
    band_me = lax.axis_index("band")
    first_row = offset[0]
    local_rows = first_row + jnp.arange(bands_all, dtype=jnp.int32) - band_me * rows_here
    inside = (local_rows >= 0) & (local_rows < rows_here)
    picked = jnp.take(panel, jnp.clip(local_rows, 0, rows_here - 1), axis=0).astype(jnp.float32)
    partner_terms = jnp.where(inside[:, None, None], picked, 0.0)
    partner = lax.psum_scatter(
        partner_terms.astype(jnp.bfloat16), "band", scatter_dimension=0, tiled=True
    )
    shifts = lax.dynamic_slice_in_dim(energies, first_row + band_me * bands_here, bands_here, 0)
    plane_size = grid_size * grid_size
    grid_x = lax.axis_index("pw") + block_count * (grid_map // plane_size)
    grid_y = grid_map // grid_size % grid_size
    grid_z = grid_map % grid_size
    squares = (
        folded_square(grid_x, grid_size)
        + folded_square(grid_y, grid_size)
        + folded_square(grid_z, grid_size)
    )
    kinetic = 1.5 * squares.astype(jnp.float32) / float(grid_size // 2 * (grid_size // 2))
    own_term = (
        (kinetic[None, None, :] - shifts[:, None, None]) * response.astype(jnp.float32)
    ).astype(jnp.bfloat16)
    forward = fourier_table(grid_size, 1.0)
    backward = fourier_table(grid_size, -1.0)
    gathered_order = jnp.arange(grid_size, dtype=jnp.int32)
    plane_order = gathered_order // slab_size + block_count * (gathered_order % slab_size)
    forward_x = jnp.take(forward, plane_order, axis=2)
    backward_x = jnp.take(backward, plane_order, axis=3)

    def finish_x(piece):
        return along_x(piece, forward_x).astype(jnp.bfloat16)

    section_resp = slab_planes(response, grid_map, forward, slab_size, grid_size)
    space_resp = finish_x(
        lax.all_to_all(section_resp, "pw", split_axis=3, concat_axis=2, tiled=True)
    )
    section_part = slab_planes(partner, grid_map, forward, slab_size, grid_size)
    space_part = finish_x(
        lax.all_to_all(section_part, "pw", split_axis=3, concat_axis=2, tiled=True)
    )
    mixed_field = potential * space_resp.astype(jnp.float32) + contact * space_part.astype(
        jnp.float32
    )
    mixed_field = mixed_field.astype(jnp.bfloat16)
    returned = along_x(mixed_field, backward_x).astype(jnp.bfloat16)
    combed = along_y(
        lax.all_to_all(returned, "pw", split_axis=2, concat_axis=3, tiled=True), backward
    ).astype(jnp.bfloat16)
    final_field = along_z(combed, backward)
    field_term = final_field.reshape(bands_here, 2, slab_size * plane_size)[:, :, grid_map].astype(
        jnp.bfloat16
    )
    own_all, field_all = (
        lax.all_gather(own_term, "band", axis=0, tiled=True),
        lax.all_gather(field_term, "band", axis=0, tiled=True),
    )
    correlation = lax.psum(correlation_of(panel, own_all) + correlation_of(panel, field_all), "pw")
    correlation_low = correlation.astype(jnp.bfloat16)
    spread = jnp.stack(
        [
            jnp.stack([correlation_low[0], -correlation_low[1]]),
            jnp.stack([correlation_low[1], correlation_low[0]]),
        ]
    )
    correction = lax.psum_scatter(
        jnp.einsum("mcj,dcmn->ndj", panel, spread, preferred_element_type=jnp.float32).astype(
            jnp.bfloat16
        ),
        "band",
        scatter_dimension=0,
        tiled=True,
    ).astype(jnp.float32)
    summed = own_term.astype(jnp.float32) + field_term.astype(jnp.float32) - correction
    residual = summed.astype(jnp.bfloat16)
    response_next = (response.astype(jnp.float32) - summed / (1.0 + kinetic)[None, None, :]).astype(
        jnp.bfloat16
    )
    return (residual, response_next)


def solution(mesh):
    return jax.shard_map(
        on_device,
        mesh=mesh,
        in_specs=(
            P("band", None, "pw"),
            P("band", None, "pw"),
            P(),
            P(),
            P("pw"),
            P(None, "pw", None),
            P(None, "pw", None),
        ),
        out_specs=(P("band", None, "pw"), P("band", None, "pw")),
        check_vma=False,
    )
```

profile of v0, /device:TPU:0, one launch (start us, length us, event | category | flops | bytes accessed | tf_op | source)
XLA Modules:
  0.0 927.8 jit_solution(613314010680141836)
XLA Ops:
  11.9 6.0 sort
  20.3 143.9 %scatter_custom_fusion = bf16[2,512000]{0,1:T(8,128)(2,1)} fusion(s32[7808]{0:T(1024)S(1)} %get-tuple-element.6, bf16[]{:T(256)} %constant.135.clone.1, bf16[7808,2]{1,0:T(8,128)(2,1)S(1)} %copy.97, s32[8192]{0:T(1024)S(1)} %pad_clamp_fusion.1), kind=kCustom, calls=%fused_computation.10 | custom fusion | bytes 2048002 | tf_op jit(solution)/shard_map/scatter | solution.py:43
  164.2 108.1 %copy.98 = bf16[2,20,160,160]{3,2,0,1:T(8,128)(2,1)S(1)} copy(bf16[2,20,160,160]{0,3,2,1:T(8,128)(2,1)} %bitcast.19) | data formatting | bytes 4096000 | tf_op jit(solution)/shard_map/reshape.7
  274.2 6.2 fusion.19
  280.4 7.0 copy.100
  287.4 7.4 all-to-all-start
  295.5 3.0 gather_fusion.2
  301.0 32.0 %all-reduce.5.cloned.1.call-done = bf16[4,2,7808]{2,1,0:T(2,128)(2,1)} async-done(((bf16[4,2,7808]{2,1,0:T(2,128)(2,1)}), bf16[4,2,7808]{2,1,0:T(2,128)(2,1)}) %all-reduce.5.cloned.1.call-update) | async-done | bytes 124944
  336.4 169.0 %scatter_custom_fusion.1 = bf16[2,512000]{0,1:T(8,128)(2,1)} fusion(s32[7808]{0:T(1024)} %copy-done.7, bf16[]{:T(256)} %constant.135.clone.1, bf16[7808,2]{1,0:T(8,128)(2,1)} %copy.105, s32[8192]{0:T(1024)S(1)} %pad_clamp_fusion.1), kind=kCustom, calls=%fused_computation.8 | custom fusion | bytes 2048512 | tf_op jit(solution)/shard_map/scatter | solution.py:43
  505.3 108.6 %copy.106 = bf16[2,20,160,160]{3,2,0,1:T(8,128)(2,1)} copy(bf16[2,20,160,160]{0,3,2,1:T(8,128)(2,1)} %bitcast.41) | data formatting | bytes 4096000 | tf_op jit(solution)/shard_map/reshape.18
  613.9 7.4 fusion.20
  621.3 7.0 copy.108
  628.3 5.5 all-to-all-start.1
  640.4 3.2 gather_fusion.1
  643.5 3.2 gather_fusion
  646.7 2.6 fusion.96
  653.1 3.2 copy.101
  658.6 48.1 %all-to-all-done.1 = bf16[1,2,20,160,160]{4,1,2,0,3:T(2,128)(2,1)} async-done(((bf16[1,2,20,160,160]{4,1,2,0,3:T(2,128)(2,1)}), bf16[1,2,20,160,160]{4,1,2,0,3:T(2,128)(2,1)}, u32[]{:S(2)}, u32[]{:S(2)}) %all-to-all-start.1) | async-done | bytes 2048032 | tf_op jit(solution)/shard_map/all_to_all | solution.py:102
  706.6 5.1 copy.109
  714.0 4.0 fusion.25
  718.0 10.3 %fusion.17 = bf16[1,2,160,20,160]{4,2,3,1,0:T(8,128)(2,1)} fusion(bf16[2,160,20,160,1]{3,1,4,0,2:T(8,128)(2,1)} %fusion.25, f32[160,20,160]{2,0,1:T(8,128)} %param.13, f32[160,20,160]{2,0,1:T(8,128)} %param.12, bf16[2,160,20,160,1]{3,0,2,1,4:T(2,128)(2,1)S(1)} %bitcast.271, bf16[2,2,160,160]{2,3,0,1:T(8,128)(2,1)} %copy.103, ...), kind=kOutput, calls=%fused_computation.30 | convolution fusion | flops 1318912000 | bytes 10649600 | tf_op jit(solution)/shard_map/bckyz,cdkw->bdwyz/dot_general | solution.py:29
  728.3 7.0 copy.114
  735.3 3.8 all-to-all-start.2
  739.2 5.4 all_gather.6
  747.2 65.7 %all-to-all-done.2 = bf16[1,2,160,20,160]{4,1,3,0,2:T(2,128)(2,1)S(1)} async-done(((bf16[1,2,160,20,160]{4,1,3,0,2:T(2,128)(2,1)}), bf16[1,2,160,20,160]{4,1,3,0,2:T(2,128)(2,1)S(1)}, u32[]{:S(2)}, u32[]{:S(2)}) %all-to-all-start.2) | async-done | bytes 2048032 | tf_op jit(solution)/shard_map/all_to_all | solution.py:110
  812.8 3.2 copy.115
  819.9 4.0 copy.120
  823.8 6.8 reshape.317
  830.7 31.3 %gather_fusion.3 = bf16[7808,2]{0,1:T(2,128)(2,1)S(1)} fusion(bf16[2,512000]{1,0:T(2,128)(2,1)S(1)} %reshape.317, s32[8192]{0:T(1024)S(1)} %pad_clamp_fusion), kind=kCustom, calls=%fused_computation.3 | custom fusion | bytes 93696 | tf_op jit(solution)/shard_map/gather | solution.py:113
  861.9 5.5 all-gather.1
  870.0 19.5 %psum.7 = bf16[2,64,4]{1,2,0:T(4,128)(2,1)S(1)} all-reduce(f32[2,64,4]{1,2,0:T(4,128)S(1)} %fusion.83), channel_id=1, replica_groups=mesh['band'=4,'pw'=8] {'pw'}, use_global_device_ids=true, to_apply=%region_3.4 | all-reduce | flops 512 | bytes 3072 | tf_op jit(solution)/shard_map/psum | solution.py:120
  890.7 27.9 %all-reduce.7.cloned.1.call-done = bf16[4,2,7808]{2,1,0:T(2,128)(2,1)} async-done(((bf16[4,2,7808]{2,1,0:T(2,128)(2,1)}), bf16[4,2,7808]{2,1,0:T(2,128)(2,1)}) %all-reduce.7.cloned.1.call-update) | async-done | bytes 124944
  (70 shorter events, 41.8 us)
Async XLA Ops:
  11.9 6.0 copy-start.3
  17.9 146.3 %copy-start.7 = (s32[7808]{0:T(1024)}, s32[7808]{0:T(1024)S(1)}, u32[]{:S(2)}) copy-start(s32[7808]{0:T(1024)S(1)} %get-tuple-element.6) | copy-start | bytes 93700
  287.4 12.9 %copy-start.9 = (u32[32]{0:T(128)S(1)}, u32[32]{0:T(128)}, u32[]{:S(2)}) copy-start(u32[32]{0:T(128)} %constant.146) | copy-start | bytes 388
  287.4 340.9 %all-to-all-start = ((bf16[1,2,20,160,160]{4,1,2,0,3:T(2,128)(2,1)}), bf16[1,2,20,160,160]{4,1,2,0,3:T(2,128)(2,1)S(1)}, u32[]{:S(2)}, u32[]{:S(2)}) async-start(bf16[1,2,20,160,160]{4,1,2,0,3:T(2,128)(2,1)} %copy.100), calls=%async_computation | async-start | bytes 6553600 | tf_op jit(solution)/shard_map/all_to_all | solution.py:98
  294.8 38.2 %all-reduce.5.cloned.1.call-start = ((), (), s32[]{:S(2)}) async-start(), calls=%async_computation.3 | async-start | bytes 249856
  628.3 78.3 %all-to-all-start.1 = ((bf16[1,2,20,160,160]{4,1,2,0,3:T(2,128)(2,1)}), bf16[1,2,20,160,160]{4,1,2,0,3:T(2,128)(2,1)}, u32[]{:S(2)}, u32[]{:S(2)}) async-start(bf16[1,2,20,160,160]{4,1,2,0,3:T(2,128)(2,1)} %copy.108), calls=%async_computation.1 | async-start | bytes 6553600 | tf_op jit(solution)/shard_map/all_to_all | solution.py:102
  633.8 17.9 %copy-start.8 = (f32[256]{0:T(256)S(1)}, f32[256]{0:T(256)}, u32[]{:S(2)}) copy-start(f32[256]{0:T(256)} %param.9) | copy-start | bytes 3076
  633.8 18.5 %copy-start.6 = (s32[7808]{0:T(1024)S(1)}, s32[7808]{0:T(1024)}, u32[]{:S(2)}) copy-start(s32[7808]{0:T(1024)} %param.11) | copy-start | bytes 93700
  711.8 2.3 copy-start.1
  735.3 3.9 copy-start.5
  735.3 9.4 %copy-start.4 = (s32[7808]{0:T(1024)S(1)}, s32[7808]{0:T(1024)}, u32[]{:S(2)}) copy-start(s32[7808]{0:T(1024)} %copy-done.3) | copy-start | bytes 93700
  735.3 77.5 %all-to-all-start.2 = ((bf16[1,2,160,20,160]{4,1,3,0,2:T(2,128)(2,1)}), bf16[1,2,160,20,160]{4,1,3,0,2:T(2,128)(2,1)S(1)}, u32[]{:S(2)}, u32[]{:S(2)}) async-start(bf16[1,2,160,20,160]{4,1,3,0,2:T(2,128)(2,1)} %copy.114), calls=%async_computation.2 | async-start | bytes 6553600 | tf_op jit(solution)/shard_map/all_to_all | solution.py:110
  739.1 179.5 %all-reduce.7.cloned.1.call-start = ((), (), s32[]{:S(2)}) async-start(), calls=%async_computation.4 | async-start | bytes 249856
  812.8 3.2 copy-start.2
  861.9 27.6 %copy-start = (bf16[64,2,7808]{2,1,0:T(2,128)(2,1)S(1)}, bf16[64,2,7808]{2,1,0:T(2,128)(2,1)}, u32[]{:S(2)}) copy-start(bf16[64,2,7808]{2,1,0:T(2,128)(2,1)} %param.8) | copy-start | bytes 5996548
Sparse Core Ops, SparseCore 0:
  300.4 32.5 all-reduce.4
  890.8 27.7 all-reduce.6
where the time goes:
time: 941 us; the launch traced here: 928 us
  local copies, waits for them, and re-layouts  631 us (67%)
  waiting for transfers between devices  174 us (18%)
  matrix products  36.8 us (4%)
  blocking collectives  30.4 us (3%)
  other arithmetic  23.8 us (3%)
  starting transfers between devices  16.8 us (2%)
  between operations  15.2 us (2%)
    scatter x3, local copies, waits for them, and re-layouts, slab_planes(): flat = jnp.zeros((row_total, 2, slab_size * grid_size * grid_size), jnp.b...  313 us
    another operation x2, local copies, waits for them, and re-layouts  217 us
    all_to_all x1, waiting for transfers between devices, on_device(): lax.all_to_all(returned, 'pw', split_axis=2, concat_axis=3, tiled=True)  65.7 us
    unnamed x4, waiting for transfers between devices  59.9 us
    all_to_all x1, waiting for transfers between devices, on_device(): lax.all_to_all(section_part, 'pw', split_axis=3, concat_axis=2, tiled=True)  48.1 us
    gather x1, local copies, waits for them, and re-layouts, on_device(): final_field.reshape(bands_here, 2, slab_size * plane_size)[:, :, grid_map]  31.3 us
    psum x1, blocking collectives, on_device(): lax.psum(correlation_of(panel, own_all) + correlation_of(panel, field_all...  19.5 us
  transfers between devices with their start and end apart: 5, of which 4 were waited for; matrix products, arithmetic and copies ran while one was open for 35% of the time, Pallas kernels for 0%

commit v1 on v0

v1 whole, which is shorter than its diff:
```python
import functools
import math

import jax
import jax.numpy as jnp
import numpy as np
from jax import lax
from jax.experimental import pallas as pl
from jax.experimental.pallas import tpu as pltpu
from jax.sharding import PartitionSpec as P

F32, BF16, I32 = jnp.float32, jnp.bfloat16, jnp.int32


def up(value, step):
    return -(-value // step) * step


class Box:
    def __init__(self, grid, blocks, count):
        self.grid, self.blocks, self.count = grid, blocks, count
        self.slab = grid // blocks
        folded = np.arange(grid)
        folded = np.where(folded >= grid // 2, folded - grid, folded)
        flat = np.sort((folded[:, None] ** 2 + folded[None, :] ** 2).ravel())
        used, half = set(), 0
        for block in range(blocks):
            planes = folded[block + blocks * np.arange(self.slab)] ** 2
            radii = np.sort((planes[:, None] + flat[None, :]).ravel())
            limit = int(radii[count - 1])
            used |= set(np.nonzero(planes <= limit)[0].tolist())
            half = max(half, math.isqrt(limit - int(planes.min())))
        self.low = 0
        while self.low in used and self.low < self.slab:
            self.low += 1
        self.slots = self.low + len([u for u in used if u >= self.low])
        if any(u in used for u in range(self.low, self.slab - (self.slots - self.low))):
            self.low = self.slots = self.slab
        self.planes = [s if s < self.low else s + self.slab - self.slots for s in range(self.slots)]
        self.half = min(half, grid // 2 - 1) if 2 * half + 1 <= grid else grid // 2
        self.width = min(2 * self.half + 1, grid)
        self.ypad = up(self.width, 8)
        self.zpad = 64 if self.width <= 64 else up(self.width, 128)
        self.rows = up(self.slots * self.slab, 16)
        self.spad = self.slots
        while self.spad * self.slab % 8 or self.spad * self.slab < self.rows:
            self.spad += 1

    def waves(self, first, other):
        products = (np.asarray(first)[:, None] * np.asarray(other)[None, :]) % self.grid
        angles = products.astype(np.float32) * np.float32(2.0 * math.pi / self.grid)
        scaling = np.float32(1.0 / math.sqrt(self.grid))
        return np.cos(angles) * scaling, np.sin(angles) * scaling

    def tables(self):
        grid, ypad, zpad = self.grid, self.ypad, self.zpad
        every = np.arange(grid)
        boxed = np.arange(self.width) - self.half

        def padded(part, rows, columns):
            return np.pad(part, ((0, rows - part.shape[0]), (0, columns - part.shape[1])))

        cos_y, sin_y = self.waves(every, boxed)
        up_y = np.concatenate([padded(cos_y, grid, ypad), padded(sin_y, grid, ypad)], 1)
        down_y = np.concatenate([padded(cos_y.T, ypad, grid), padded(-sin_y.T, ypad, grid)], 0)
        cos_z, sin_z = padded(cos_y, grid, zpad), padded(sin_y, grid, zpad)
        up_z = np.stack([np.concatenate([cos_z.T, -sin_z.T], 0), np.concatenate([sin_z.T, cos_z.T], 0)])
        down_z = np.stack([np.concatenate([cos_z, -sin_z], 1), np.concatenate([sin_z, cos_z], 1)])
        planes = np.array([p + self.blocks * x for p in range(self.blocks) for x in self.planes])
        cos_x, sin_x = self.waves(every, planes)

        def slotted(part):
            part = part.reshape(grid, self.blocks, self.slots)
            part = np.pad(part, ((0, 0), (0, 0), (0, self.spad - self.slots)))
            return part.reshape(grid, self.blocks * self.spad)

        cos_x, sin_x = slotted(cos_x), slotted(sin_x)
        up_x = np.concatenate([cos_x, sin_x], 1)
        down_x = np.concatenate([cos_x.T, -sin_x.T], 0)
        return [jnp.asarray(t, BF16) for t in (up_y, down_y, up_x, down_x, up_z, down_z)]


def quarter(field, zpad):
    pieces = []
    for start in range(0, field.shape[1], 2 * zpad):
        piece = field[:, start : start + 2 * zpad]
        if 2 * zpad == 128:
            lane = lax.broadcasted_iota(I32, piece.shape, 1)
            turned = pltpu.roll(piece, zpad, 1)
            pieces.append(jnp.where(lane < zpad, -turned, turned))
        else:
            pieces += [-piece[:, zpad:], piece[:, :zpad]]
    return pieces[0] if len(pieces) == 1 else jnp.concatenate(pieces, 1)


def chunks(total, step):
    return [(start, min(step, total - start)) for start in range(0, total, step)]


def dot(left, right, dims=((1,), (0,))):
    return lax.dot_general(left, right, (dims, ((), ())), preferred_element_type=F32)


def pick_rows(rows, index):
    return lax.broadcasted_iota(I32, (rows, index.shape[1]), 0) == index


def scatter_kernel(box, row_ref, z_ref, resp_ref, part_ref, up_y_ref, out_ref, space_ref):
    zpad, ypad, slab = box.zpad, box.ypad, box.slab
    total = None
    for start, size in chunks(box.count, 1024):
        span = slice(start, start + size)
        chosen = jnp.where(pick_rows(box.slots * ypad, row_ref[:, span]), 1.0, 0.0).astype(BF16)
        at_z = pick_rows(zpad, z_ref[:, span])
        values = []
        for ref in (resp_ref, part_ref):
            pair = ref[0, :, span].astype(F32)
            values += [jnp.where(at_z, pair[c : c + 1], 0.0).astype(BF16) for c in range(2)]
        piece = dot(chosen, jnp.concatenate(values, 0), ((1,), (1,)))
        total = piece if total is None else total + piece
    for s in range(box.slots):
        plane = total[s * ypad : (s + 1) * ypad]
        both = jnp.concatenate([plane, quarter(plane, zpad)], 0).astype(BF16)
        lines = dot(up_y_ref[...], both)
        for q in range(box.blocks):
            space_ref[q, s * slab : (s + 1) * slab, :] = lines[q * slab : (q + 1) * slab]
    used = box.slots * slab
    for q in range(box.blocks):
        if used < box.rows:
            space_ref[q, used:, :] = jnp.zeros((box.rows - used, space_ref.shape[2]), F32)
        out_ref[q] = space_ref[q].astype(BF16)


def mix_kernel(
    box, lines, in_ref, pot_ref, con_ref, up_x_ref, down_x_ref, up_z_ref, down_z_ref, out_ref, from_ref, to_ref
):
    zpad, slab, stride = box.zpad, box.slab, box.spad * box.slab
    planes, tiles = box.blocks * box.spad, 2 * zpad // 128
    step = pl.program_id(0)

    @pl.when(step == 0)
    def _():
        for p in range(box.blocks):
            for t in range(2 * tiles):
                from_ref[t, p * stride : p * stride + box.rows, :] = in_ref[
                    p, :, t * 128 : (t + 1) * 128
                ].astype(F32)
                if box.rows < stride:
                    from_ref[t, p * stride + box.rows : (p + 1) * stride, :] = jnp.zeros(
                        (stride - box.rows, 128), F32
                    )

    for i in range(lines):
        line = step * lines + i
        space = []
        for f in range(2):
            plane = jnp.concatenate(
                [
                    from_ref[f * tiles + t, pl.ds(line, planes, stride=slab), :]
                    for t in range(tiles)
                ],
                1,
            )
            both = jnp.concatenate([plane, quarter(plane, zpad)], 0).astype(BF16)
            wide = dot(up_x_ref[...], both).astype(BF16)
            space.append([dot(wide, up_z_ref[d]) for d in range(2)])
        potential, contact = pot_ref[i], con_ref[i]
        mixed = [(potential * space[0][d] + contact * space[1][d]).astype(BF16) for d in range(2)]
        back = (dot(mixed[0], down_z_ref[0]) + dot(mixed[1], down_z_ref[1])).astype(BF16)
        parts = dot(down_x_ref[...], back)
        lined = parts[:planes] + quarter(parts[planes:], zpad)
        for t in range(tiles):
            to_ref[t, pl.ds(line, planes, stride=slab), :] = lined[:, t * 128 : (t + 1) * 128]

    @pl.when(step == pl.num_programs(0) - 1)
    def _():
        for p in range(box.blocks):
            for t in range(tiles):
                out_ref[p, :, t * 128 : (t + 1) * 128] = to_ref[
                    t, p * stride : p * stride + box.rows, :
                ].astype(BF16)


def term_kernel(
    box, in_ref, row_ref, z_ref, resp_ref, factor_ref, down_y_ref, low_ref, term_ref, space_ref
):
    zpad, ypad, slab = box.zpad, box.ypad, box.slab
    for q in range(box.blocks):
        space_ref[q] = in_ref[q].astype(F32)
    fields = []
    for s in range(box.slots):
        plane = jnp.concatenate(
            [space_ref[q, s * slab : (s + 1) * slab, :] for q in range(box.blocks)], 0
        ).astype(BF16)
        parts = dot(down_y_ref[...], plane)
        fields.append(parts[:ypad] + quarter(parts[ypad:], zpad))
    field = jnp.concatenate(fields, 0).T.astype(BF16)
    for start, size in chunks(box.count, 1024):
        span = slice(start, start + size)
        chosen = jnp.where(pick_rows(box.slots * ypad, row_ref[:, span]), 1.0, 0.0).astype(BF16)
        at_z = pick_rows(zpad, z_ref[:, span])
        found = dot(field, chosen)
        pair = resp_ref[0, :, span].astype(F32)
        rows = []
        for c in range(2):
            value = jnp.sum(jnp.where(at_z, found[c * zpad : (c + 1) * zpad], 0.0), 0, keepdims=True)
            own = (factor_ref[:, span] * pair[c : c + 1]).astype(BF16).astype(F32)
            rows.append(own + value)
        both = jnp.concatenate(rows, 0)
        term_ref[0, :, span] = both
        low_ref[0, :, span] = both.astype(BF16)


def whole_call(kernel, out_shape, scratch, args, cost):
    return pl.pallas_call(
        kernel,
        out_shape=out_shape,
        in_specs=[pl.BlockSpec(memory_space=pltpu.VMEM)] * len(args),
        out_specs=jax.tree.map(lambda _: pl.BlockSpec(memory_space=pltpu.VMEM), out_shape),
        scratch_shapes=scratch,
        compiler_params=pltpu.CompilerParams(vmem_limit_bytes=48 << 20),
        cost_estimate=pl.CostEstimate(flops=cost, bytes_accessed=1 << 20, transcendentals=0),
    )(*args)


def mix_call(box, received, potential, contact, tables):
    grid, slab = box.grid, box.slab
    steps = 5 if slab % 5 == 0 else slab
    lines = slab // steps
    full = lambda shape: pl.BlockSpec(shape, lambda g: (0,) * len(shape))
    height = box.blocks * box.spad * slab
    block = pl.BlockSpec((lines, grid, grid), lambda g: (g, 0, 0))
    return pl.pallas_call(
        functools.partial(mix_kernel, box, lines),
        out_shape=jax.ShapeDtypeStruct((box.blocks, box.rows, 2 * box.zpad), BF16),
        grid=(steps,),
        in_specs=[full(received.shape), block, block] + [full(t.shape) for t in tables],
        out_specs=full((box.blocks, box.rows, 2 * box.zpad)),
        scratch_shapes=[
            pltpu.VMEM((2 * box.zpad // 64, height, 128), F32),
            pltpu.VMEM((2 * box.zpad // 128, height, 128), F32),
        ],
        compiler_params=pltpu.CompilerParams(
            vmem_limit_bytes=48 << 20, dimension_semantics=("arbitrary",)
        ),
        cost_estimate=pl.CostEstimate(flops=1 << 32, bytes_accessed=8 << 20, transcendentals=0),
    )(received, potential, contact, *tables)


def folded_square(coord, grid_size):
    folded = jnp.where(coord >= grid_size // 2, coord - grid_size, coord)
    return folded * folded


def on_device(sizes, response, panel, energies, offset, grid_map, potential, contact):
    rows_here, count = panel.shape[0], grid_map.shape[0]
    grid = potential.shape[0]
    bands, blocks = sizes
    box = Box(grid, blocks, count)
    up_y, down_y, up_x, down_x, up_z, down_z = box.tables()
    band_me = lax.axis_index("band")
    first_row = offset[0]

    local = first_row - band_me * rows_here
    picked = jnp.concatenate(
        [
            lax.dynamic_slice_in_dim(panel, jnp.clip(local + n, 0, rows_here - 1), 1, 0)
            for n in range(bands)
        ],
        0,
    )
    arrived = lax.all_to_all(picked, "band", split_axis=0, concat_axis=0, tiled=True)
    owner = (first_row + band_me) // rows_here
    partner = lax.dynamic_slice_in_dim(arrived, owner, 1, 0)
    shift = lax.dynamic_slice_in_dim(energies, first_row + band_me, 1, 0)

    plane_size = grid * grid
    local_x = grid_map // plane_size
    grid_x = lax.axis_index("pw") + blocks * local_x
    grid_y = grid_map // grid % grid
    grid_z = grid_map % grid
    squares = folded_square(grid_x, grid) + folded_square(grid_y, grid) + folded_square(grid_z, grid)
    kinetic = 1.5 * squares.astype(F32) / float(grid // 2 * (grid // 2))
    slot = jnp.where(local_x < box.low, local_x, local_x - (box.slab - box.slots))
    row_index = (slot * box.ypad + (grid_y + box.half) % grid)[None, :]
    z_index = ((grid_z + box.half) % grid)[None, :]
    factor = (kinetic - shift[0])[None, :]

    sent = whole_call(
        functools.partial(scatter_kernel, box),
        jax.ShapeDtypeStruct((blocks, box.rows, 4 * box.zpad), BF16),
        [pltpu.VMEM((blocks, box.rows, 4 * box.zpad), F32)],
        (row_index, z_index, response, partner, up_y),
        1 << 32,
    )
    received = lax.all_to_all(sent, "pw", split_axis=0, concat_axis=0, tiled=True)
    returned = mix_call(
        box,
        received,
        jnp.transpose(potential, (1, 0, 2)),
        jnp.transpose(contact, (1, 0, 2)),
        (up_x, down_x, up_z, down_z),
    )
    combed = lax.all_to_all(returned, "pw", split_axis=0, concat_axis=0, tiled=True)
    term_low, term = whole_call(
        functools.partial(term_kernel, box),
        (
            jax.ShapeDtypeStruct((1, 2, count), BF16),
            jax.ShapeDtypeStruct((1, 2, count), F32),
        ),
        [pltpu.VMEM((blocks, box.rows, 2 * box.zpad), F32)],
        (combed, row_index, z_index, response, factor, down_y),
        1 << 32,
    )

    terms = lax.all_gather(term_low, "band", axis=0, tiled=True)
    other = jnp.stack([terms[:, 1], -terms[:, 0]], axis=1)
    swapped = jnp.stack([terms, other])
    correlation = jnp.einsum("mcj,dncj->dmn", panel, swapped, preferred_element_type=F32)
    near = 1
    while near < blocks:
        pairs = [(source, source ^ near) for source in range(blocks)]
        correlation = correlation + lax.ppermute(correlation, "pw", pairs)
        near *= 2
    low = correlation.astype(BF16)
    spread = jnp.stack([jnp.stack([low[0], -low[1]]), jnp.stack([low[1], low[0]])])
    shares = jnp.einsum("mcj,dcmn->ndj", panel, spread, preferred_element_type=F32).astype(BF16)
    parts = lax.all_to_all(shares, "band", split_axis=0, concat_axis=0, tiled=True)
    correction = jnp.sum(parts.astype(F32), axis=0, keepdims=True)
    summed = term - correction
    residual = summed.astype(BF16)
    response_next = (response.astype(F32) - summed / (1.0 + kinetic)[None, None, :]).astype(BF16)
    return (residual, response_next)


def solution(mesh):
    return jax.shard_map(
        functools.partial(on_device, (mesh.shape["band"], mesh.shape["pw"])),
        mesh=mesh,
        in_specs=(
            P("band", None, "pw"),
            P("band", None, "pw"),
            P(),
            P(),
            P("pw"),
            P(None, "pw", None),
            P(None, "pw", None),
        ),
        out_specs=(P("band", None, "pw"), P("band", None, "pw")),
        check_vma=False,
    )
```

time: 941 us -> 97 us (0.10); the launches traced: 928 us -> 96.3 us
  local copies, waits for them, and re-layouts: 631 us -> 3.41 us
  waiting for transfers between devices: 174 us -> 19.3 us
  matrix products: 36.8 us -> 1.2 us
  Pallas kernels: 0 us -> 21.7 us
  other arithmetic: 23.8 us -> 3.45 us
  between operations: 15.2 us -> 1.53 us
    scatter x3 -> x0, local copies, waits for them, and re-layouts: 313 us -> none  [slab_planes(): flat = jnp.zeros((row_total, 2, slab_size * grid_size * grid_size), jnp.b...]
    another operation x4 -> x0, local copies, waits for them, and re-layouts: 220 us -> none
    all_to_all x3 -> x2, waiting for transfers between devices: 114 us -> 10.9 us  [the longest x1 7.31 us: on_device(): lax.all_to_all(returned, 'pw', split_axis=0, concat_axis=0, tiled=True)]
    unnamed x4 -> x0, waiting for transfers between devices: 59.9 us -> none
    gather x4 -> x0, local copies, waits for them, and re-layouts: 40.6 us -> none  [the longest x1 31.3 us: on_device(): final_field.reshape(bands_here, 2, slab_size * plane_size)[:, :, grid_map]]
    dot_general x9 -> x2, matrix products: 36.8 us -> 1.2 us  [the longest x1 0.75 us: on_device(): jnp.einsum('mcj,dncj->dmn', panel, swapped, preferred_element_type=F32)]
    all_to_all x0 -> x2, blocking collectives: none -> 29.3 us  [the longest x1 22.3 us: on_device(): lax.all_to_all(sent, 'pw', split_axis=0, concat_axis=0, tiled=True)]
    pallas_call x0 -> x3, Pallas kernels: none -> 21.7 us  [the longest x1 16.5 us: mix_call(): pl.pallas_call(functools.partial(mix_kernel, box, lines), out_shape=jax.S...]
  transfers between devices with their start and end apart: 5 -> 5, of which waited for: 4 -> 5; matrix products, arithmetic and copies ran while one was open for 35% -> 2% of each run, Pallas kernels for 0% -> 0%
where the time goes in v1:
time: 97 us; the launch traced here: 96.3 us
  blocking collectives  34.7 us (36%)
  Pallas kernels  21.7 us (22%)
  waiting for transfers between devices  19.3 us (20%)
  starting transfers between devices  11.1 us (11%)
  other arithmetic  3.45 us (4%)
  local copies, waits for them, and re-layouts  3.41 us (4%)
  between operations  1.53 us (2%)
  matrix products  1.2 us (1%)
    all_to_all x1, blocking collectives, on_device(): lax.all_to_all(sent, 'pw', split_axis=0, concat_axis=0, tiled=True)  22.3 us
    pallas_call x1, Pallas kernels, mix_call(): pl.pallas_call(functools.partial(mix_kernel, box, lines), out_shape=jax.S...  16.5 us
    ppermute x3, waiting for transfers between devices, on_device(): correlation = correlation + lax.ppermute(correlation, 'pw', pairs)  8.36 us
    all_to_all x1, waiting for transfers between devices, on_device(): lax.all_to_all(returned, 'pw', split_axis=0, concat_axis=0, tiled=True)  7.31 us
    all_to_all x1, blocking collectives, on_device(): lax.all_to_all(shares, 'band', split_axis=0, concat_axis=0, tiled=True)  6.95 us
    all_gather x1, blocking collectives, on_device(): terms = lax.all_gather(term_low, 'band', axis=0, tiled=True)  5.41 us
    pallas_call x2, Pallas kernels, whole_call(): pl.pallas_call(kernel, out_shape=out_shape, in_specs=[pl.BlockSpec(memory...  5.15 us
    all_to_all x1, starting transfers between devices, on_device(): lax.all_to_all(picked, 'band', split_axis=0, concat_axis=0, tiled=True)  4.24 us
  transfers between devices with their start and end apart: 5, of which 5 were waited for; matrix products, arithmetic and copies ran while one was open for 2% of the time, Pallas kernels for 0%

profile of v1, /device:TPU:0, one launch (start us, length us, event | category | flops | bytes accessed | tf_op | source)
XLA Modules:
  0.0 96.3 jit_solution(14223966917266310133)
XLA Ops:
  1.3 1.0 %constant_dynamic-slice_fusion.4 = (bf16[1,2,7808]{2,1,0:T(2,128)(2,1)S(1)}, bf16[1,2,7808]{2,1,0:T(2,128)(2,1)S(1)}, bf16[1,2,7808]{2,1,0:T(2,128)(2,1)S(1)}, bf16[1,2,7808]{2,1,0:T(2,128)(2,1)S(1)}) fusion(bf16[64,2,7808]{2,1,0:T(2,128)(2,1)} %param.14, s32[]{:T(128)S(6)} %min.13, s32[]{:T(128)S(6)} %min.15, s32[]{:T(128)S(6)} %min.14, s32[]{:T(128)S(6)} %min.16), kind=kLoop, calls=%fused_computation.58 | loop fusion | bytes 249872 | tf_op jit(solution)/shard_map/dynamic_slice | solution.py:267
  2.3 0.9 pad_maximum_fusion
  3.2 4.2 %all-to-all-start = ((bf16[4,2,7808]{2,1,0:T(2,128)(2,1)}), bf16[4,2,7808]{2,1,0:T(2,128)(2,1)S(1)}, u32[]{:S(2)}, u32[]{:S(2)}) async-start(bf16[4,2,7808]{2,1,0:T(2,128)(2,1)} %pad_maximum_fusion), calls=%async_computation | async-start | bytes 249856 | tf_op jit(solution)/shard_map/all_to_all | solution.py:272
  7.4 0.9 add_select_fusion
  8.4 3.6 %all-to-all-done = bf16[4,2,7808]{2,1,0:T(2,128)(2,1)S(1)} async-done(((bf16[4,2,7808]{2,1,0:T(2,128)(2,1)}), bf16[4,2,7808]{2,1,0:T(2,128)(2,1)S(1)}, u32[]{:S(2)}, u32[]{:S(2)}) %all-to-all-start) | async-done | bytes 124960 | tf_op jit(solution)/shard_map/all_to_all | solution.py:272
  12.0 0.7 copy-done
  12.8 0.8 copy-done.8
  13.6 2.5 %shard_map.140 = bf16[8,144,256]{2,1,0:T(8,128)(2,1)S(1)} custom-call(s32[1,7808]{1,0:T(1,128)S(1)} %broadcast_in_dim.13.row_ref, s32[1,7808]{1,0:T(1,128)S(1)} %broadcast_in_dim.14.z_ref, bf16[1,2,7808]{2,1,0:T(2,128)(2,1)S(1)} %copy-done, bf16[1,2,7808]{2,1,0:T(2,128)(2,1)S(1)} %constant_dynamic-slice_fusion.part_ref, bf16[160,112]{1,0:T(8,128)(2,1)S(1)} %copy-done.8), custom_call_target="tpu_custom_call" | custom-call | flops 4294967296 | bytes 1048576 | tf_op jit(solution)/shard_map/pallas_call | solution.py:215
  16.0 22.3 %all_to_all.20.in_ref = bf16[8,144,256]{2,1,0:T(8,128)(2,1)S(1)} all-to-all(bf16[8,144,256]{2,1,0:T(8,128)(2,1)S(1)} %shard_map.140), channel_id=1, replica_groups=mesh['band'=4,'pw'=8] {'pw'}, dimensions={0} | all-to-all | bytes 1179648 | tf_op jit(solution)/shard_map/all_to_all | solution.py:296
  38.4 0.0 copy-start.6
  38.4 16.5 %shard_map.141 = bf16[8,144,128]{2,1,0:T(8,128)(2,1)} custom-call(bf16[8,144,256]{2,1,0:T(8,128)(2,1)S(1)} %all_to_all.20.in_ref, f32[20,160,160]{2,1,0:T(8,128)S(1)} %bitcast.43, f32[20,160,160]{2,1,0:T(8,128)} %bitcast.45, bf16[160,128]{1,0:T(8,128)(2,1)S(1)} %copy-done.7, bf16[128,160]{1,0:T(8,128)(2,1)S(1)} %copy-done.5, ...), custom_call_target="tpu_custom_call" | custom-call | flops 4294967296 | bytes 8388608 | tf_op jit(solution)/shard_map/pallas_call | solution.py:233
  55.0 3.4 %all-to-all-start.2 = ((bf16[8,144,128]{2,1,0:T(8,128)(2,1)}), bf16[8,144,128]{2,1,0:T(8,128)(2,1)S(1)}, u32[]{:S(2)}, u32[]{:S(2)}) async-start(bf16[8,144,128]{2,1,0:T(8,128)(2,1)} %shard_map.141), calls=%async_computation.2 | async-start | bytes 589824 | tf_op jit(solution)/shard_map/all_to_all | solution.py:304
  58.4 0.6 dynamic_slice.23
  59.0 0.1 broadcast_add_fusion
  59.1 0.7 broadcast_subtract_fusion
  59.8 7.3 %all-to-all-done.2.in_ref = bf16[8,144,128]{2,1,0:T(8,128)(2,1)S(1)} async-done(((bf16[8,144,128]{2,1,0:T(8,128)(2,1)}), bf16[8,144,128]{2,1,0:T(8,128)(2,1)S(1)}, u32[]{:S(2)}, u32[]{:S(2)}) %all-to-all-start.2) | async-done | bytes 294944 | tf_op jit(solution)/shard_map/all_to_all | solution.py:304
  67.1 2.7 %shard_map.142 = (bf16[1,2,7808]{2,1,0:T(2,128)(2,1)S(1)}, f32[1,2,7808]{2,1,0:T(2,128)S(1)}) custom-call(bf16[8,144,128]{2,1,0:T(8,128)(2,1)S(1)} %all-to-all-done.2.in_ref, s32[1,7808]{1,0:T(1,128)S(1)} %broadcast_in_dim.13.row_ref, s32[1,7808]{1,0:T(1,128)S(1)} %broadcast_in_dim.14.z_ref, bf16[1,2,7808]{2,1,0:T(2,128)(2,1)S(1)} %copy-done.1, ...), custom_call_target="tpu_custom_call" | custom-call | flops 4294967296 | bytes 1048576 | tf_op jit(solution)/shard_map/pallas_call | solution.py:215
  69.8 5.4 %all_gather.3 = bf16[4,2,7808]{2,1,0:T(2,128)(2,1)S(1)} all-gather(bf16[1,2,7808]{2,1,0:T(2,128)(2,1)S(1)} %get-tuple-element.5), channel_id=1, replica_groups=mesh['band'=4,'pw'=8] {'band'}, dimensions={0}, use_global_device_ids=true | all-gather | bytes 156160 | tf_op jit(solution)/shard_map/all_gather | solution.py:316
  75.3 0.1 fusion.32
  75.3 0.1 maximum_bitcast_fusion
  75.4 0.7 fusion.7
  76.2 1.4 %collective-permute-start = (f32[2,64,4]{1,2,0:T(4,128)S(1)}, f32[2,64,4]{1,2,0:T(4,128)S(1)}, u32[]{:S(2)}, u32[]{:S(2)}) collective-permute-start(f32[2,64,4]{1,2,0:T(4,128)S(1)} %fusion.7), channel_id=1, source_target_pairs={{0,1},{1,0},{2,3},{3,2},{4,5},{5,4},{6,7},{7,6},{8,9},{9,8},{10,11... | collective-permute-start | bytes 6152 | tf_op jit(solution)/shard_map/ppermute | solution.py:323
  77.6 2.2 %collective-permute-done = f32[2,64,4]{1,2,0:T(4,128)S(1)} collective-permute-done((f32[2,64,4]{1,2,0:T(4,128)S(1)}, f32[2,64,4]{1,2,0:T(4,128)S(1)}, u32[]{:S(2)}, u32[]{:S(2)}) %collective-permute-start) | collective-permute-done | bytes 2080 | tf_op jit(solution)/shard_map/ppermute | solution.py:323
  79.8 1.0 %collective-permute-start.1 = (f32[2,64,4]{1,2,0:T(4,128)S(1)}, f32[2,64,4]{1,2,0:T(4,128)S(1)}, u32[]{:S(2)}, u32[]{:S(2)}) collective-permute-start(f32[2,64,4]{1,2,0:T(4,128)S(1)} %add.101), channel_id=1, source_target_pairs={{0,2},{1,3},{2,0},{3,1},{4,6},{5,7},{6,4},{7,5},{8,10},{9,11},{10,... | collective-permute-start | bytes 6152 | tf_op jit(solution)/shard_map/ppermute | solution.py:323
  80.8 2.6 %collective-permute-done.1 = f32[2,64,4]{1,2,0:T(4,128)S(1)} collective-permute-done((f32[2,64,4]{1,2,0:T(4,128)S(1)}, f32[2,64,4]{1,2,0:T(4,128)S(1)}, u32[]{:S(2)}, u32[]{:S(2)}) %collective-permute-start.1) | collective-permute-done | bytes 2080 | tf_op jit(solution)/shard_map/ppermute | solution.py:323
  83.5 1.0 collective-permute-start.2
  84.4 3.5 %collective-permute-done.2 = f32[2,64,4]{1,2,0:T(4,128)S(1)} collective-permute-done((f32[2,64,4]{1,2,0:T(4,128)S(1)}, f32[2,64,4]{1,2,0:T(4,128)S(1)}, u32[]{:S(2)}, u32[]{:S(2)}) %collective-permute-start.2) | collective-permute-done | bytes 2080 | tf_op jit(solution)/shard_map/ppermute | solution.py:323
  88.0 0.4 fusion.1
  88.4 0.1 copy.23
  88.5 6.9 %all_to_all.21 = bf16[4,2,7808]{2,1,0:T(2,128)(2,1)S(1)} all-to-all(bf16[4,2,7808]{2,1,0:T(2,128)(2,1)S(1)} %copy.23), channel_id=1, replica_groups=mesh['band'=4,'pw'=8] {'band'}, dimensions={0} | all-to-all | bytes 249856 | tf_op jit(solution)/shard_map/all_to_all | solution.py:328
  95.5 0.1 convert_reduce_fusion
  95.6 0.7 fusion.13
  (31 shorter events, 0.2 us)
Async XLA Ops:
  3.2 8.8 %all-to-all-start = ((bf16[4,2,7808]{2,1,0:T(2,128)(2,1)}), bf16[4,2,7808]{2,1,0:T(2,128)(2,1)S(1)}, u32[]{:S(2)}, u32[]{:S(2)}) async-start(bf16[4,2,7808]{2,1,0:T(2,128)(2,1)} %pad_maximum_fusion), calls=%async_computation | async-start | bytes 249856 | tf_op jit(solution)/shard_map/all_to_all | solution.py:272
  12.0 0.8 copy-start
  12.8 0.8 copy-start.8
  13.5 24.8 %copy-start.2 = (f32[160,20,160]{2,0,1:T(8,128)S(1)}, f32[160,20,160]{2,0,1:T(8,128)}, u32[]{:S(2)}) copy-start(f32[160,20,160]{2,0,1:T(8,128)} %param.18) | copy-start | bytes 6144004
  13.5 24.8 %copy-start.3 = (bf16[2,128,160]{2,1,0:T(8,128)(2,1)S(1)}, bf16[2,128,160]{2,1,0:T(8,128)(2,1)}, u32[]{:S(2)}) copy-start(bf16[2,128,160]{2,1,0:T(8,128)(2,1)} %constant.114.clone.up_z_ref) | copy-start | bytes 245764
  13.5 24.8 %copy-start.4 = (bf16[2,160,128]{2,1,0:T(8,128)(2,1)S(1)}, bf16[2,160,128]{2,1,0:T(8,128)(2,1)}, u32[]{:S(2)}) copy-start(bf16[2,160,128]{2,1,0:T(8,128)(2,1)} %constant.115.clone.down_z_ref) | copy-start | bytes 245764
  13.5 24.8 %copy-start.5 = (bf16[128,160]{1,0:T(8,128)(2,1)S(1)}, bf16[128,160]{1,0:T(8,128)(2,1)}, u32[]{:S(2)}) copy-start(bf16[128,160]{1,0:T(8,128)(2,1)} %constant.113.clone.down_x_ref) | copy-start | bytes 122884
  13.5 24.8 %copy-start.7 = (bf16[160,128]{1,0:T(8,128)(2,1)S(1)}, bf16[160,128]{1,0:T(8,128)(2,1)}, u32[]{:S(2)}) copy-start(bf16[160,128]{1,0:T(8,128)(2,1)} %constant.112.clone.up_x_ref) | copy-start | bytes 122884
  38.4 20.0 %copy-start.11 = (f32[256]{0:T(256)S(1)}, f32[256]{0:T(256)}, u32[]{:S(2)}) copy-start(f32[256]{0:T(256)} %param.15) | copy-start | bytes 3076
  38.4 20.6 %copy-start.10 = (s32[7808]{0:T(1024)S(1)}, s32[7808]{0:T(1024)}, u32[]{:S(2)}) copy-start(s32[7808]{0:T(1024)} %param.17) | copy-start | bytes 93700
  38.4 28.7 %copy-start.1 = (bf16[1,2,7808]{2,1,0:T(2,128)(2,1)S(1)}, bf16[1,2,7808]{2,1,0:T(2,128)(2,1)}, u32[]{:S(2)}) copy-start(bf16[1,2,7808]{2,1,0:T(2,128)(2,1)} %resp_ref.3) | copy-start | bytes 93700
  38.4 28.7 %copy-start.6 = (bf16[112,160]{1,0:T(8,128)(2,1)S(1)}, bf16[112,160]{1,0:T(8,128)(2,1)}, u32[]{:S(2)}) copy-start(bf16[112,160]{1,0:T(8,128)(2,1)} %constant.111.clone.down_y_ref) | copy-start | bytes 107524
  55.0 12.1 %all-to-all-start.2 = ((bf16[8,144,128]{2,1,0:T(8,128)(2,1)}), bf16[8,144,128]{2,1,0:T(8,128)(2,1)S(1)}, u32[]{:S(2)}, u32[]{:S(2)}) async-start(bf16[8,144,128]{2,1,0:T(8,128)(2,1)} %shard_map.141), calls=%async_computation.2 | async-start | bytes 589824 | tf_op jit(solution)/shard_map/all_to_all | solution.py:304
  59.8 15.7 %copy-start.9 = (bf16[64,2,7808]{2,1,0:T(2,128)(2,1)S(1)}, bf16[64,2,7808]{2,1,0:T(2,128)(2,1)}, u32[]{:S(2)}) copy-start(bf16[64,2,7808]{2,1,0:T(2,128)(2,1)} %param.14) | copy-start | bytes 5996548
  76.2 3.7 %collective-permute-start = (f32[2,64,4]{1,2,0:T(4,128)S(1)}, f32[2,64,4]{1,2,0:T(4,128)S(1)}, u32[]{:S(2)}, u32[]{:S(2)}) collective-permute-start(f32[2,64,4]{1,2,0:T(4,128)S(1)} %fusion.7), channel_id=1, source_target_pairs={{0,1},{1,0},{2,3},{3,2},{4,5},{5,4},{6,7},{7,6},{8,9},{9,8},{10,11... | collective-permute-start | bytes 6152 | tf_op jit(solution)/shard_map/ppermute | solution.py:323
  79.8 3.6 %collective-permute-start.1 = (f32[2,64,4]{1,2,0:T(4,128)S(1)}, f32[2,64,4]{1,2,0:T(4,128)S(1)}, u32[]{:S(2)}, u32[]{:S(2)}) collective-permute-start(f32[2,64,4]{1,2,0:T(4,128)S(1)} %add.101), channel_id=1, source_target_pairs={{0,2},{1,3},{2,0},{3,1},{4,6},{5,7},{6,4},{7,5},{8,10},{9,11},{10,... | collective-permute-start | bytes 6152 | tf_op jit(solution)/shard_map/ppermute | solution.py:323
  83.5 4.5 %collective-permute-start.2 = (f32[2,64,4]{1,2,0:T(4,128)S(1)}, f32[2,64,4]{1,2,0:T(4,128)S(1)}, u32[]{:S(2)}, u32[]{:S(2)}) collective-permute-start(f32[2,64,4]{1,2,0:T(4,128)S(1)} %add.102), channel_id=1, source_target_pairs={{0,4},{1,5},{2,6},{3,7},{4,0},{5,1},{6,2},{7,3},{8,12},{9,13},{10,... | collective-permute-start | bytes 6152 | tf_op jit(solution)/shard_map/ppermute | solution.py:323

commit v2 on v1

v2 whole, which is shorter than its diff:
```python
import functools
import math

import jax
import jax.numpy as jnp
import numpy as np
from jax import lax
from jax.experimental import pallas as pl
from jax.experimental.layout import Layout, with_layout_constraint
from jax.experimental.pallas import tpu as pltpu
from jax.sharding import PartitionSpec as P

F32, BF16, I32 = jnp.float32, jnp.bfloat16, jnp.int32


def up(value, step):
    return -(-value // step) * step


class Box:
    def __init__(self, grid, blocks, count):
        self.grid, self.blocks, self.count = grid, blocks, count
        self.slab = grid // blocks
        folded = np.arange(grid)
        folded = np.where(folded >= grid // 2, folded - grid, folded)
        flat = np.sort((folded[:, None] ** 2 + folded[None, :] ** 2).ravel())
        used, half = set(), 0
        for block in range(blocks):
            planes = folded[block + blocks * np.arange(self.slab)] ** 2
            radii = np.sort((planes[:, None] + flat[None, :]).ravel())
            limit = int(radii[count - 1])
            used |= set(np.nonzero(planes <= limit)[0].tolist())
            half = max(half, math.isqrt(limit - int(planes.min())))
        self.low = 0
        while self.low in used and self.low < self.slab:
            self.low += 1
        self.slots = self.low + len([u for u in used if u >= self.low])
        if any(u in used for u in range(self.low, self.slab - (self.slots - self.low))):
            self.low = self.slots = self.slab
        self.planes = [s if s < self.low else s + self.slab - self.slots for s in range(self.slots)]
        self.half = min(half, grid // 2 - 1) if 2 * half + 1 <= grid else grid // 2
        self.width = min(2 * self.half + 1, grid)
        self.ypad = up(self.width, 8)
        self.zpad = 64 if self.width <= 64 else up(self.width, 128)
        self.rows = up(self.slots * self.slab, 16)
        self.spad = self.slots
        while self.spad * self.slab % 8 or self.spad * self.slab < self.rows:
            self.spad += 1

    def waves(self, first, other):
        products = (np.asarray(first)[:, None] * np.asarray(other)[None, :]) % self.grid
        angles = products.astype(np.float32) * np.float32(2.0 * math.pi / self.grid)
        scaling = np.float32(1.0 / math.sqrt(self.grid))
        return np.cos(angles) * scaling, np.sin(angles) * scaling

    def tables(self):
        grid, ypad, zpad = self.grid, self.ypad, self.zpad
        every = np.arange(grid)
        boxed = np.arange(self.width) - self.half

        def padded(part, rows, columns):
            return np.pad(part, ((0, rows - part.shape[0]), (0, columns - part.shape[1])))

        cos_y, sin_y = self.waves(every, boxed)
        up_y = np.concatenate([padded(cos_y, grid, ypad), padded(sin_y, grid, ypad)], 1)
        down_y = np.concatenate([padded(cos_y.T, ypad, grid), padded(-sin_y.T, ypad, grid)], 0)
        cos_z, sin_z = padded(cos_y, grid, zpad), padded(sin_y, grid, zpad)
        up_z = np.stack([np.concatenate([cos_z.T, -sin_z.T], 0), np.concatenate([sin_z.T, cos_z.T], 0)])
        down_z = np.stack([np.concatenate([cos_z, -sin_z], 1), np.concatenate([sin_z, cos_z], 1)])
        planes = np.array([p + self.blocks * x for p in range(self.blocks) for x in self.planes])
        cos_x, sin_x = self.waves(every, planes)

        def slotted(part):
            part = part.reshape(grid, self.blocks, self.slots)
            part = np.pad(part, ((0, 0), (0, 0), (0, self.spad - self.slots)))
            return part.reshape(grid, self.blocks * self.spad)

        cos_x, sin_x = slotted(cos_x), slotted(sin_x)
        up_x = np.concatenate([cos_x, sin_x], 1)
        down_x = np.concatenate([cos_x.T, -sin_x.T], 0)
        return [jnp.asarray(t, BF16) for t in (up_y, down_y, up_x, down_x, up_z, down_z)]


def quarter(field, zpad):
    pieces = []
    for start in range(0, field.shape[1], 2 * zpad):
        piece = field[:, start : start + 2 * zpad]
        if 2 * zpad == 128:
            lane = lax.broadcasted_iota(I32, piece.shape, 1)
            turned = pltpu.roll(piece, zpad, 1)
            pieces.append(jnp.where(lane < zpad, -turned, turned))
        else:
            pieces += [-piece[:, zpad:], piece[:, :zpad]]
    return pieces[0] if len(pieces) == 1 else jnp.concatenate(pieces, 1)


def chunks(total, step):
    return [(start, min(step, total - start)) for start in range(0, total, step)]


def dot(left, right, dims=((1,), (0,))):
    return lax.dot_general(left, right, (dims, ((), ())), preferred_element_type=F32)


def pick_rows(rows, index):
    return lax.broadcasted_iota(I32, (rows, index.shape[1]), 0) == index


def scattered(box, row_ref, z_ref, value_ref, up_y_ref, out_ref, space_ref):
    zpad, ypad, slab = box.zpad, box.ypad, box.slab
    total = None
    for start, size in chunks(box.count, 1024):
        span = slice(start, start + size)
        chosen = jnp.where(pick_rows(box.slots * ypad, row_ref[:, span]), 1.0, 0.0).astype(BF16)
        at_z = pick_rows(zpad, z_ref[:, span])
        pair = value_ref[0, :, span].astype(F32)
        values = [jnp.where(at_z, pair[c : c + 1], 0.0).astype(BF16) for c in range(2)]
        piece = dot(chosen, jnp.concatenate(values, 0), ((1,), (1,)))
        total = piece if total is None else total + piece
    for s in range(box.slots):
        plane = total[s * ypad : (s + 1) * ypad]
        both = jnp.concatenate([plane, quarter(plane, zpad)], 0).astype(BF16)
        lines = dot(up_y_ref[...], both)
        for q in range(box.blocks):
            space_ref[q, s * slab : (s + 1) * slab, :] = lines[q * slab : (q + 1) * slab]
    used = box.slots * slab
    for q in range(box.blocks):
        if used < box.rows:
            space_ref[q, used:, :] = jnp.zeros((box.rows - used, space_ref.shape[2]), F32)
        out_ref[q] = space_ref[q].astype(BF16)


def folded_square(coord, grid):
    folded = jnp.where(coord >= grid // 2, coord - grid, coord)
    return folded * folded


def first_kernel(box, map_ref, value_ref, up_y_ref, out_ref, row_ref, z_ref, kinetic_ref, space_ref):
    grid, cell = box.grid, map_ref[...][None, :].astype(F32)
    local_x = jnp.floor((cell + 0.5) * (1.0 / (grid * grid)))
    cell = cell - local_x * (grid * grid)
    grid_y = jnp.floor((cell + 0.5) * (1.0 / grid))
    grid_z = cell - grid_y * grid
    grid_x = lax.axis_index("pw").astype(F32) + box.blocks * local_x
    squares = folded_square(grid_x, grid) + folded_square(grid_y, grid) + folded_square(grid_z, grid)
    kinetic_ref[...] = 1.5 * squares / float(grid // 2 * (grid // 2))

    def boxed(coord):
        moved = coord + box.half
        return jnp.where(moved >= grid, moved - grid, moved)

    slot = jnp.where(local_x < box.low, local_x, local_x - (box.slab - box.slots))
    row_ref[...] = (slot * box.ypad + boxed(grid_y)).astype(I32)
    z_ref[...] = boxed(grid_z).astype(I32)
    scattered(box, row_ref, z_ref, value_ref, up_y_ref, out_ref, space_ref)


def spread_rows(box, in_ref, from_ref):
    stride = box.spad * box.slab
    for p in range(box.blocks):
        for t in range(2 * box.zpad // 128):
            from_ref[t, p * stride : p * stride + box.rows, :] = in_ref[
                p, :, t * 128 : (t + 1) * 128
            ].astype(F32)
            if box.rows < stride:
                from_ref[t, p * stride + box.rows : (p + 1) * stride, :] = jnp.zeros(
                    (stride - box.rows, 128), F32
                )


def along_x(box, from_ref, up_x_ref, wide_ref):
    zpad, planes = box.zpad, box.blocks * box.spad
    both = []
    for line in range(box.slab):
        plane = jnp.concatenate(
            [from_ref[t, pl.ds(line, planes, stride=box.slab), :] for t in range(2 * zpad // 128)], 1
        )
        both.append(jnp.concatenate([plane, quarter(plane, zpad)], 0).astype(BF16))
    wide = dot(up_x_ref[...], jnp.concatenate(both, 1)).astype(BF16)
    for line in range(box.slab):
        wide_ref[line] = wide[:, line * 2 * zpad : (line + 1) * 2 * zpad]


def line_groups(box):
    return [slice(start, start + size) for start, size in chunks(box.slab, 5)]


def response_kernel(
    box,
    in_ref,
    pot_ref,
    up_x_ref,
    up_z_ref,
    real_ref,
    imag_ref,
    from_ref,
    wide_ref,
    pot_held,
    real_held,
    imag_held,
    sems,
    out_sems,
):
    copies = {
        lines.start: pltpu.make_async_copy(pot_ref.at[lines], pot_held.at[lines], sems.at[n])
        for n, lines in enumerate(line_groups(box))
    }
    for copy in copies.values():
        copy.start()
    spread_rows(box, in_ref, from_ref)
    along_x(box, from_ref, up_x_ref, wide_ref)
    outs = []
    for n, lines in enumerate(line_groups(box)):
        copies[lines.start].wait()
        for line in range(lines.start, lines.stop):
            for d, held in enumerate((real_held, imag_held)):
                held[line] = (pot_held[line] * dot(wide_ref[line], up_z_ref[d])).astype(BF16)
        for d, (held, ref) in enumerate(((real_held, real_ref), (imag_held, imag_ref))):
            outs.append(pltpu.make_async_copy(held.at[lines], ref.at[lines], out_sems.at[n, d]))
            outs[-1].start()
    for copy in outs:
        copy.wait()


def mix_kernel(
    box,
    in_ref,
    real_ref,
    imag_ref,
    con_ref,
    up_x_ref,
    down_x_ref,
    up_z_ref,
    down_z_ref,
    out_ref,
    from_ref,
    to_ref,
    wide_ref,
    back_ref,
    real_held,
    imag_held,
    con_held,
    sems,
):
    zpad, stride = box.zpad, box.spad * box.slab
    planes, tiles = box.blocks * box.spad, 2 * zpad // 128
    pairs = ((real_ref, real_held), (imag_ref, imag_held), (con_ref, con_held))
    copies = [
        [
            pltpu.make_async_copy(ref.at[lines], held.at[lines], sems.at[n, k])
            for k, (ref, held) in enumerate(pairs)
        ]
        for n, lines in enumerate(line_groups(box))
    ]
    for copy in sum(copies[:2], []):
        copy.start()
    spread_rows(box, in_ref, from_ref)
    along_x(box, from_ref, up_x_ref, wide_ref)
    for n, lines in enumerate(line_groups(box)):
        for copy in copies[n]:
            copy.wait()
        for copy in sum(copies[n + 2 : n + 3], []):
            copy.start()
        for line in range(lines.start, lines.stop):
            contact = con_held[line].astype(F32)
            mixed = [
                (held[line].astype(F32) + contact * dot(wide_ref[line], up_z_ref[d])).astype(BF16)
                for d, held in enumerate((real_held, imag_held))
            ]
            back = dot(mixed[0], down_z_ref[0]) + dot(mixed[1], down_z_ref[1])
            back_ref[:, line * 2 * zpad : (line + 1) * 2 * zpad] = back.astype(BF16)
    parts = dot(down_x_ref[...], back_ref[...])
    lined = parts[:planes] + quarter(parts[planes:], zpad)
    for line in range(box.slab):
        for t in range(tiles):
            column = (line * tiles + t) * 128
            to_ref[t, pl.ds(line, planes, stride=box.slab), :] = lined[:, column : column + 128]
    for p in range(box.blocks):
        for t in range(tiles):
            out_ref[p, :, t * 128 : (t + 1) * 128] = to_ref[
                t, p * stride : p * stride + box.rows, :
            ].astype(BF16)


def gather_kernel(mine_ref, other_ref, out_ref, sems):
    rows = mine_ref.shape[0]
    copies = [
        pltpu.make_async_copy(ref, out_ref.at[n * rows : (n + 1) * rows], sems.at[n])
        for n, ref in enumerate((mine_ref, other_ref))
    ]
    for copy in copies:
        copy.start()
    for copy in copies:
        copy.wait()


def term_kernel(
    box, in_ref, row_ref, z_ref, resp_ref, factor_ref, down_y_ref, low_ref, term_ref, space_ref
):
    zpad, ypad, slab = box.zpad, box.ypad, box.slab
    for q in range(box.blocks):
        space_ref[q] = in_ref[q].astype(F32)
    fields = []
    for s in range(box.slots):
        plane = jnp.concatenate(
            [space_ref[q, s * slab : (s + 1) * slab, :] for q in range(box.blocks)], 0
        ).astype(BF16)
        parts = dot(down_y_ref[...], plane)
        fields.append(parts[:ypad] + quarter(parts[ypad:], zpad))
    field = jnp.concatenate(fields, 0).T.astype(BF16)
    for start, size in chunks(box.count, 1024):
        span = slice(start, start + size)
        chosen = jnp.where(pick_rows(box.slots * ypad, row_ref[:, span]), 1.0, 0.0).astype(BF16)
        at_z = pick_rows(zpad, z_ref[:, span])
        found = dot(field, chosen)
        pair = resp_ref[0, :, span].astype(F32)
        rows = []
        for c in range(2):
            value = jnp.sum(jnp.where(at_z, found[c * zpad : (c + 1) * zpad], 0.0), 0, keepdims=True)
            own = (factor_ref[:, span] * pair[c : c + 1]).astype(BF16).astype(F32)
            rows.append(own + value)
        both = jnp.concatenate(rows, 0)
        term_ref[0, :, span] = both
        low_ref[0, :, span] = both.astype(BF16)


def call(kernel, out_shape, scratch, args, flops, limit, left=(), out_left=False):
    return pl.pallas_call(
        kernel,
        out_shape=out_shape,
        in_specs=[
            pl.BlockSpec(memory_space=pltpu.HBM if n in left else None) for n in range(len(args))
        ],
        out_specs=jax.tree.map(
            lambda _: pl.BlockSpec(memory_space=pltpu.HBM if out_left else None), out_shape
        ),
        scratch_shapes=scratch,
        compiler_params=pltpu.CompilerParams(vmem_limit_bytes=limit << 20),
        cost_estimate=pl.CostEstimate(flops=flops, bytes_accessed=4 << 20, transcendentals=0),
    )(*args)


def xor_permute(value, axis, size, distance):
    return lax.ppermute(value, axis, [(source, source ^ distance) for source in range(size)])


def sum_over(value, axis, size):
    near = 1
    while near < size:
        radix = 2 if (size // near).bit_length() % 2 == 0 else 4
        if radix == 2:
            value = value + xor_permute(value, axis, size, near)
        else:
            one, two, three = [xor_permute(value, axis, size, near * k) for k in (1, 2, 3)]
            value = (value + one) + (two + three)
        near *= radix
    return value


def on_device(sizes, response, panel, energies, offset, grid_map, potential, contact):
    rows_here, count = panel.shape[0], grid_map.shape[0]
    grid = potential.shape[0]
    bands, blocks = sizes
    box = Box(grid, blocks, count)
    up_y, down_y, up_x, down_x, up_z, down_z = box.tables()
    band_me = lax.axis_index("band")
    first_row = offset[0]

    shape = (blocks, box.rows, 2 * box.zpad)
    tiles, height = 2 * box.zpad // 128, blocks * box.spad * box.slab
    index_shape = jax.ShapeDtypeStruct((1, count), I32)
    field, row_index, z_index, kinetic = call(
        functools.partial(first_kernel, box),
        (
            jax.ShapeDtypeStruct(shape, BF16),
            index_shape,
            index_shape,
            jax.ShapeDtypeStruct((1, count), F32),
        ),
        [pltpu.VMEM(shape, F32)],
        (grid_map, response, up_y),
        1 << 31,
        56,
    )
    field, panel, contact = lax.optimization_barrier((field, panel, contact))
    contact_low = jnp.transpose(contact, (1, 0, 2)).astype(BF16)
    field = lax.all_to_all(field, "pw", split_axis=0, concat_axis=0, tiled=True)

    local = first_row - band_me * rows_here
    candidates = []
    for distance in range(bands):
        row = jnp.clip(local + (band_me ^ distance), 0, rows_here - 1)
        row = lax.dynamic_slice_in_dim(panel, row, 1, 0)
        candidates.append(xor_permute(row, "band", bands, distance) if distance else row)
    owner = (first_row + band_me) // rows_here
    partner = candidates[0]
    for distance in range(1, bands):
        partner = jnp.where(owner == band_me ^ distance, candidates[distance], partner)
    beside = with_layout_constraint(xor_permute(panel, "band", bands, 1), Layout((0, 1, 2)))
    shift = lax.dynamic_slice_in_dim(energies, first_row + band_me, 1, 0)
    factor = kinetic - shift[0]

    other_field = call(
        functools.partial(scattered, box),
        jax.ShapeDtypeStruct(shape, BF16),
        [pltpu.VMEM(shape, F32)],
        (row_index, z_index, partner, up_y),
        1 << 31,
        16,
    )
    other_field = lax.all_to_all(other_field, "pw", split_axis=0, concat_axis=0, tiled=True)
    groups = len(line_groups(box))
    space = (box.slab, grid, grid)
    columns = pltpu.VMEM((tiles, height, 128), F32)
    wide = pltpu.VMEM((box.slab, grid, 2 * box.zpad), BF16)
    real, imag = call(
        functools.partial(response_kernel, box),
        (jax.ShapeDtypeStruct(space, BF16), jax.ShapeDtypeStruct(space, BF16)),
        [
            columns,
            wide,
            pltpu.VMEM(space, F32),
            pltpu.VMEM(space, BF16),
            pltpu.VMEM(space, BF16),
            pltpu.SemaphoreType.DMA((groups,)),
            pltpu.SemaphoreType.DMA((groups, 2)),
        ],
        (field, jnp.transpose(potential, (1, 0, 2)), up_x, up_z),
        1 << 32,
        60,
        (1,),
        True,
    )
    returned = call(
        functools.partial(mix_kernel, box),
        jax.ShapeDtypeStruct(shape, BF16),
        [
            columns,
            columns,
            wide,
            pltpu.VMEM((grid, box.slab * 2 * box.zpad), BF16),
            pltpu.VMEM(space, BF16),
            pltpu.VMEM(space, BF16),
            pltpu.VMEM(space, BF16),
            pltpu.SemaphoreType.DMA((groups, 3)),
        ],
        (other_field, real, imag, contact_low, up_x, down_x, up_z, down_z),
        1 << 32,
        60,
        (1, 2, 3),
    )
    returned, panel_late, beside = lax.optimization_barrier((returned, panel, beside))
    rows_both = pl.pallas_call(
        gather_kernel,
        out_shape=jax.ShapeDtypeStruct((2 * rows_here, 2, count), BF16),
        in_specs=[pl.BlockSpec(memory_space=pl.ANY)] * 2,
        out_specs=pl.BlockSpec(memory_space=pltpu.VMEM),
        scratch_shapes=[pltpu.SemaphoreType.DMA((2,))],
        compiler_params=pltpu.CompilerParams(vmem_limit_bytes=16 << 20),
        cost_estimate=pl.CostEstimate(flops=0, bytes_accessed=8 << 20, transcendentals=0),
    )(panel_late, beside)
    combed = lax.all_to_all(returned, "pw", split_axis=0, concat_axis=0, tiled=True)
    combed, rows_both = lax.optimization_barrier((combed, rows_both))
    term_low, term = call(
        functools.partial(term_kernel, box),
        (
            jax.ShapeDtypeStruct((1, 2, count), BF16),
            jax.ShapeDtypeStruct((1, 2, count), F32),
        ),
        [pltpu.VMEM(shape, F32)],
        (combed, row_index, z_index, response, factor, down_y),
        1 << 32,
        16,
    )

    far = range(2, bands, 2)
    terms = jnp.concatenate(
        [term_low] + [xor_permute(term_low, "band", bands, k) for k in far], 0
    )
    other = jnp.stack([terms[:, 1], -terms[:, 0]], axis=1)
    swapped = jnp.stack([terms, other])
    correlation = jnp.einsum("mcj,dncj->dmn", rows_both, swapped, preferred_element_type=F32)
    low = sum_over(correlation, "pw", blocks).astype(BF16)
    spread = jnp.stack([jnp.stack([low[0], -low[1]]), jnp.stack([low[1], low[0]])])
    shares = jnp.einsum("mcj,dcmn->ndj", rows_both, spread, preferred_element_type=F32)
    correction = shares[:1]
    for k, distance in enumerate(far):
        share = xor_permute(shares[k + 1 : k + 2].astype(BF16), "band", bands, distance)
        correction = correction + share.astype(F32)
    summed = term - correction
    residual = summed.astype(BF16)
    response_next = (response.astype(F32) - summed / (1.0 + kinetic)[None]).astype(BF16)
    return (residual, response_next)


def solution(mesh):
    return jax.shard_map(
        functools.partial(on_device, (mesh.shape["band"], mesh.shape["pw"])),
        mesh=mesh,
        in_specs=(
            P("band", None, "pw"),
            P("band", None, "pw"),
            P(),
            P(),
            P("pw"),
            P(None, "pw", None),
            P(None, "pw", None),
        ),
        out_specs=(P("band", None, "pw"), P("band", None, "pw")),
        check_vma=False,
    )
```

time: 97 us -> 83.9 us (0.86)
  blocking collectives: 34.7 us -> 0 us
  starting transfers between devices: 11.1 us -> 26.7 us
  other arithmetic: 3.45 us -> 5.25 us
  local copies, waits for them, and re-layouts: 3.41 us -> 4.9 us
  waiting for transfers between devices: 19.3 us -> 20.4 us
    all_to_all x2 -> x0, blocking collectives: 29.3 us -> none  [the longest x1 22.3 us: on_device(): lax.all_to_all(sent, 'pw', split_axis=0, concat_axis=0, tiled=True)]
    ppermute x3 -> x10, starting transfers between devices: 3.41 us -> 12.9 us  [xor_permute(): lax.ppermute(value, axis, [(source, source ^ distance) for source in rang...]
    all_gather x1 -> x0, blocking collectives: 5.41 us -> none  [on_device(): terms = lax.all_gather(term_low, 'band', axis=0, tiled=True)]
    all_to_all x1 -> x2, starting transfers between devices: 4.24 us -> 9.44 us  [the longest x1 5.81 us: on_device(): field = lax.all_to_all(field, 'pw', split_axis=0, concat_axis=0, tiled=True)]
    all_to_all x1 -> x2, waiting for transfers between devices: 3.6 us -> 7.07 us  [the longest x1 5.39 us: on_device(): field = lax.all_to_all(field, 'pw', split_axis=0, concat_axis=0, tiled=True)]
    all_to_all x1, waiting for transfers between devices: 7.31 us -> 3.96 us  [on_device(): lax.all_to_all(returned, 'pw', split_axis=0, concat_axis=0, tiled=True)]
    convert_element_type x2 -> x3, other arithmetic: 0.7 us -> 4.05 us  [the longest x1 3.34 us: on_device(): contact_low = jnp.transpose(contact, (1, 0, 2)).astype(BF16)]
    unnamed x24 -> x29, local copies, waits for them, and re-layouts: 1.58 us -> 4.18 us
  transfers between devices with their start and end apart: 5 -> 13, of which waited for: 5 -> 8; matrix products, arithmetic and copies ran while one was open for 2% -> 6% of each run, Pallas kernels for 0% -> 19%
where the time goes in v2:
time: 83.9 us; the launch traced here: 83.2 us
  starting transfers between devices  26.7 us (32%)
  Pallas kernels  22.5 us (27%)
  waiting for transfers between devices  20.4 us (24%)
  other arithmetic  5.25 us (6%)
  local copies, waits for them, and re-layouts  4.9 us (6%)
  matrix products  1.9 us (2%)
  between operations  1.54 us (2%)
    pallas_call x5, Pallas kernels, call(): pl.pallas_call(kernel, out_shape=out_shape, in_specs=[pl.BlockSpec(memory...  20.6 us
    ppermute x10, starting transfers between devices, xor_permute(): lax.ppermute(value, axis, [(source, source ^ distance) for source in rang...  12.9 us
    ppermute x10, waiting for transfers between devices, xor_permute(): lax.ppermute(value, axis, [(source, source ^ distance) for source in rang...  9.36 us
    all_to_all x1, starting transfers between devices, on_device(): field = lax.all_to_all(field, 'pw', split_axis=0, concat_axis=0, tiled=True)  5.81 us
    all_to_all x1, waiting for transfers between devices, on_device(): field = lax.all_to_all(field, 'pw', split_axis=0, concat_axis=0, tiled=True)  5.39 us
    all_to_all x1, starting transfers between devices, on_device(): lax.all_to_all(returned, 'pw', split_axis=0, concat_axis=0, tiled=True)  4.34 us
    unnamed x29, local copies, waits for them, and re-layouts  4.18 us
    all_to_all x1, waiting for transfers between devices, on_device(): lax.all_to_all(returned, 'pw', split_axis=0, concat_axis=0, tiled=True)  3.96 us
  transfers between devices with their start and end apart: 13, of which 8 were waited for; matrix products, arithmetic and copies ran while one was open for 6% of the time, Pallas kernels for 19%

profile of v2, /device:TPU:0, one launch (start us, length us, event | category | flops | bytes accessed | tf_op | source)
XLA Modules:
  0.0 83.2 jit_solution(17188171413283444212)
XLA Ops:
  1.3 4.0 %shard_map.140 = (bf16[8,144,128]{2,1,0:T(8,128)(2,1)}, s32[1,7808]{1,0:T(1,128)}, s32[1,7808]{1,0:T(1,128)}, f32[1,7808]{1,0:T(1,128)}) custom-call(s32[7808]{0:T(1024)} %map_ref.1, bf16[1,2,7808]{2,1,0:T(2,128)(2,1)} %resp_ref.1, bf16[160,112]{1,0:T(8,128)(2,1)} %constant.49.clone.up_y_ref), custom_call_target="tpu_custom_call" | custom-call | flops 2147483648 | bytes 4194304 | tf_op jit(solution)/shard_map/pallas_call | solution.py:328
  5.4 2.5 %collective-permute-start = (bf16[1,2,7808]{2,1,0:T(2,128)(2,1)S(1)}, bf16[1,2,7808]{2,1,0:T(2,128)(2,1)S(1)}, u32[]{:S(2)}, u32[]{:S(2)}) collective-permute-start(bf16[1,2,7808]{2,1,0:T(2,128)(2,1)S(1)} %get-tuple-element.36), channel_id=1, source_target_pairs={{0,24},{8,16},{16,8},{24,0},{1,25},{9,17},{17,9},{25,1},{2,26},{10... | collective-permute-start | bytes 93704 | tf_op jit(solution)/shard_map/ppermute | solution.py:344
  9.0 5.8 %all-to-all-start.1 = ((bf16[8,144,128]{2,1,0:T(8,128)(2,1)}), bf16[8,144,128]{2,1,0:T(8,128)(2,1)S(1)}, u32[]{:S(2)}, u32[]{:S(2)}) async-start(bf16[8,144,128]{2,1,0:T(8,128)(2,1)} %get-tuple-element.22), calls=%async_computation.1 | async-start | bytes 589824 | tf_op jit(solution)/shard_map/all_to_all | solution.py:387
  14.9 0.7 copy-done.6
  15.7 0.8 copy-done.8
  16.4 3.0 %shard_map.141 = bf16[8,144,128]{2,1,0:T(8,128)(2,1)} custom-call(s32[1,7808]{1,0:T(1,128)S(1)} %copy-done.6, s32[1,7808]{1,0:T(1,128)S(1)} %copy-done.8, bf16[1,2,7808]{2,1,0:T(2,128)(2,1)S(1)} %broadcast_select_fusion.2.value_ref, bf16[160,112]{1,0:T(8,128)(2,1)S(1)} %copy-done.5), custom_call_target="tpu_custom_call" | custom-call | flops 2147483648 | bytes 4194304 | tf_op jit(solution)/shard_map/pallas_call | solution.py:328
  19.4 5.4 %all-to-all-done.1.in_ref = bf16[8,144,128]{2,1,0:T(8,128)(2,1)S(1)} async-done(((bf16[8,144,128]{2,1,0:T(8,128)(2,1)}), bf16[8,144,128]{2,1,0:T(8,128)(2,1)S(1)}, u32[]{:S(2)}, u32[]{:S(2)}) %all-to-all-start.1) | async-done | bytes 294944 | tf_op jit(solution)/shard_map/all_to_all | solution.py:387
  24.8 3.6 %all-to-all-start = ((bf16[8,144,128]{2,1,0:T(8,128)(2,1)}), bf16[8,144,128]{2,1,0:T(8,128)(2,1)S(1)}, u32[]{:S(2)}, u32[]{:S(2)}) async-start(bf16[8,144,128]{2,1,0:T(8,128)(2,1)} %shard_map.141), calls=%async_computation | async-start | bytes 589824 | tf_op jit(solution)/shard_map/all_to_all | solution.py:411
  28.5 3.3 %convert_bitcast_fusion.con_ref = bf16[20,160,160]{2,1,0:T(8,128)(2,1)} fusion(f32[160,20,160]{2,0,1:T(8,128)} %param.19), kind=kLoop, calls=%fused_computation.6 | loop fusion | flops 512000 | bytes 3072000 | tf_op jit(solution)/shard_map/convert_element_type | solution.py:386
  31.8 4.7 %shard_map.142 = (bf16[20,160,160]{2,1,0:T(8,128)(2,1)}, bf16[20,160,160]{2,1,0:T(8,128)(2,1)}) custom-call(bf16[8,144,128]{2,1,0:T(8,128)(2,1)} %copy-done.10, f32[20,160,160]{2,1,0:T(8,128)} %bitcast.32, bf16[160,128]{1,0:T(8,128)(2,1)} %constant.51.clone.up_x_ref, bf16[2,128,160]{2,1,0:T(8,128)(2,1)} %constant.53.clone.up_z_ref), custom_call_target="tpu_custom_call" | custom-call | flops 4294967296 | bytes 4194304 | tf_op jit(solution)/shard_map/pallas_call | solution.py:328
  36.5 1.7 %all-to-all-done.in_ref = bf16[8,144,128]{2,1,0:T(8,128)(2,1)S(1)} async-done(((bf16[8,144,128]{2,1,0:T(8,128)(2,1)}), bf16[8,144,128]{2,1,0:T(8,128)(2,1)S(1)}, u32[]{:S(2)}, u32[]{:S(2)}) %all-to-all-start) | async-done | bytes 294944 | tf_op jit(solution)/shard_map/all_to_all | solution.py:411
  38.1 0.7 copy-done.11
  38.9 6.3 %shard_map.143 = bf16[8,144,128]{2,1,0:T(8,128)(2,1)} custom-call(bf16[8,144,128]{2,1,0:T(8,128)(2,1)} %copy-done.11, bf16[20,160,160]{2,1,0:T(8,128)(2,1)} %get-tuple-element.23.real_ref, bf16[20,160,160]{2,1,0:T(8,128)(2,1)} %get-tuple-element.24.imag_ref, bf16[20,160,160]{2,1,0:T(8,128)(2,1)} %convert_bitcast_fusion.con_ref, ...), custom_call_target="tpu_custom_call" | custom-call | flops 4294967296 | bytes 4194304 | tf_op jit(solution)/shard_map/pallas_call | solution.py:328
  45.2 4.3 %all-to-all-start.2 = ((bf16[8,144,128]{2,1,0:T(8,128)(2,1)}), bf16[8,144,128]{2,1,0:T(8,128)(2,1)S(1)}, u32[]{:S(2)}, u32[]{:S(2)}) async-start(bf16[8,144,128]{2,1,0:T(8,128)(2,1)} %shard_map.143), calls=%async_computation.2 | async-start | bytes 589824 | tf_op jit(solution)/shard_map/all_to_all | solution.py:462
  50.1 0.7 add_reduce_fusion
  50.8 1.9 %shard_map.144 = bf16[128,2,7808]{2,1,0:T(2,128)(2,1)S(1)} custom-call(bf16[64,2,7808]{2,1,0:T(2,128)(2,1)S(1)} %copy-done.2, bf16[64,2,7808]{2,1,0:T(2,128)(2,1)} %collective-permute-done.3.other_ref), custom_call_target="tpu_custom_call" | custom-call | bytes 8388608 | tf_op jit(solution)/shard_map/pallas_call | solution.py:453
  52.8 1.9 %copy-done = bf16[128,2,7808]{2,1,0:T(2,128)(2,1)} copy-done((bf16[128,2,7808]{2,1,0:T(2,128)(2,1)}, bf16[128,2,7808]{2,1,0:T(2,128)(2,1)S(1)}, u32[]{:S(2)}) %copy-start) | copy-done | bytes 3997720
  54.6 4.0 %all-to-all-done.2.in_ref = bf16[8,144,128]{2,1,0:T(8,128)(2,1)S(1)} async-done(((bf16[8,144,128]{2,1,0:T(8,128)(2,1)}), bf16[8,144,128]{2,1,0:T(8,128)(2,1)S(1)}, u32[]{:S(2)}, u32[]{:S(2)}) %all-to-all-start.2) | async-done | bytes 294944 | tf_op jit(solution)/shard_map/all_to_all | solution.py:462
  58.6 2.7 %shard_map.145 = (bf16[1,2,7808]{2,1,0:T(2,128)(2,1)S(1)}, f32[1,2,7808]{2,1,0:T(2,128)S(1)}) custom-call(bf16[8,144,128]{2,1,0:T(8,128)(2,1)S(1)} %all-to-all-done.2.in_ref, s32[1,7808]{1,0:T(1,128)S(1)} %copy-done.7, s32[1,7808]{1,0:T(1,128)S(1)} %copy-done.9, bf16[1,2,7808]{2,1,0:T(2,128)(2,1)S(1)} %copy-done.3, ...), custom_call_target="tpu_custom_call" | custom-call | flops 4294967296 | bytes 4194304 | tf_op jit(solution)/shard_map/pallas_call | solution.py:328
  61.3 1.7 %collective-permute-start.4 = (bf16[1,2,7808]{2,1,0:T(2,128)(2,1)S(1)}, bf16[1,2,7808]{2,1,0:T(2,128)(2,1)S(1)}, u32[]{:S(2)}, u32[]{:S(2)}) collective-permute-start(bf16[1,2,7808]{2,1,0:T(2,128)(2,1)S(1)} %get-tuple-element.32), channel_id=1, source_target_pairs={{0,16},{8,24},{16,0},{24,8},{1,17},{9,25},{17,1},{25,9},{2,18},{10... | collective-permute-start | bytes 93704 | tf_op jit(solution)/shard_map/ppermute | solution.py:344
  63.0 2.3 %collective-permute-done.4 = bf16[1,2,7808]{2,1,0:T(2,128)(2,1)S(1)} collective-permute-done((bf16[1,2,7808]{2,1,0:T(2,128)(2,1)S(1)}, bf16[1,2,7808]{2,1,0:T(2,128)(2,1)S(1)}, u32[]{:S(2)}, u32[]{:S(2)}) %collective-permute-start.4) | collective-permute-done | bytes 31264 | tf_op jit(solution)/shard_map/ppermute | solution.py:344
  65.8 1.2 %fusion.5 = f32[2,128,2]{1,2,0:T(2,128)S(1)} fusion(bf16[128,2,7808]{2,1,0:T(2,128)(2,1)S(1)} %copy-done.1, bf16[2,2,2,7808]{3,2,1,0:T(2,128)(2,1)S(1)} %pad_maximum_fusion), kind=kOutput, calls=%fused_computation.7 | convolution fusion | flops 15990784 | bytes 4124672 | tf_op jit(solution)/shard_map/mcj,dncj->dmn/dot_general | solution.py:482
  67.1 1.5 %collective-permute-start.5 = (f32[2,128,2]{1,2,0:T(2,128)S(1)}, f32[2,128,2]{1,2,0:T(2,128)S(1)}, u32[]{:S(2)}, u32[]{:S(2)}) collective-permute-start(f32[2,128,2]{1,2,0:T(2,128)S(1)} %fusion.5), channel_id=1, source_target_pairs={{0,1},{1,0},{2,3},{3,2},{4,5},{5,4},{6,7},{7,6},{8,9},{9,8},{10,11... | collective-permute-start | bytes 6152 | tf_op jit(solution)/shard_map/ppermute | solution.py:344
  68.6 2.1 %collective-permute-done.5 = f32[2,128,2]{1,2,0:T(2,128)S(1)} collective-permute-done((f32[2,128,2]{1,2,0:T(2,128)S(1)}, f32[2,128,2]{1,2,0:T(2,128)S(1)}, u32[]{:S(2)}, u32[]{:S(2)}) %collective-permute-start.5) | collective-permute-done | bytes 2080 | tf_op jit(solution)/shard_map/ppermute | solution.py:344
  70.7 1.1 %collective-permute-start.6 = (f32[2,128,2]{1,2,0:T(2,128)S(1)}, f32[2,128,2]{1,2,0:T(2,128)S(1)}, u32[]{:S(2)}, u32[]{:S(2)}) collective-permute-start(f32[2,128,2]{1,2,0:T(2,128)S(1)} %add.51), channel_id=1, source_target_pairs={{0,2},{1,3},{2,0},{3,1},{4,6},{5,7},{6,4},{7,5},{8,10},{9,11},{10,... | collective-permute-start | bytes 6152 | tf_op jit(solution)/shard_map/ppermute | solution.py:344
  72.4 2.6 %collective-permute-start.8 = (f32[2,128,2]{1,2,0:T(2,128)S(1)}, f32[2,128,2]{1,2,0:T(2,128)S(1)}, u32[]{:S(2)}, u32[]{:S(2)}) collective-permute-start(f32[2,128,2]{1,2,0:T(2,128)S(1)} %add.51), channel_id=1, source_target_pairs={{0,6},{1,7},{2,4},{3,5},{4,2},{5,3},{6,0},{7,1},{8,14},{9,15},{10,... | collective-permute-start | bytes 6152 | tf_op jit(solution)/shard_map/ppermute | solution.py:344
  75.1 1.2 %collective-permute-done.7 = f32[2,128,2]{1,2,0:T(2,128)S(1)} collective-permute-done((f32[2,128,2]{1,2,0:T(2,128)S(1)}, f32[2,128,2]{1,2,0:T(2,128)S(1)}, u32[]{:S(2)}, u32[]{:S(2)}) %collective-permute-start.7) | collective-permute-done | bytes 2080 | tf_op jit(solution)/shard_map/ppermute | solution.py:344
  76.3 1.5 %collective-permute-done.8 = f32[2,128,2]{1,2,0:T(2,128)S(1)} collective-permute-done((f32[2,128,2]{1,2,0:T(2,128)S(1)}, f32[2,128,2]{1,2,0:T(2,128)S(1)}, u32[]{:S(2)}, u32[]{:S(2)}) %collective-permute-start.8) | collective-permute-done | bytes 2080 | tf_op jit(solution)/shard_map/ppermute | solution.py:344
  77.8 0.6 convolution_bitcast_fusion
  78.5 1.7 %collective-permute-start.9 = (bf16[1,2,7808]{2,1,0:T(2,128)(2,1)S(1)}, bf16[1,2,7808]{2,1,0:T(2,128)(2,1)S(1)}, u32[]{:S(2)}, u32[]{:S(2)}) collective-permute-start(bf16[1,2,7808]{2,1,0:T(2,128)(2,1)S(1)} %slice.43), channel_id=1, source_target_pairs={{0,16},{8,24},{16,0},{24,8},{1,17},{9,25},{17,1},{25,9},{2,18},{10... | collective-permute-start | bytes 93704 | tf_op jit(solution)/shard_map/ppermute | solution.py:344
  80.2 2.3 %collective-permute-done.9 = bf16[1,2,7808]{2,1,0:T(2,128)(2,1)S(1)} collective-permute-done((bf16[1,2,7808]{2,1,0:T(2,128)(2,1)S(1)}, bf16[1,2,7808]{2,1,0:T(2,128)(2,1)S(1)}, u32[]{:S(2)}, u32[]{:S(2)}) %collective-permute-start.9) | collective-permute-done | bytes 31264 | tf_op jit(solution)/shard_map/ppermute | solution.py:344
  82.5 0.7 fusion.10
  (47 shorter events, 3.1 us)
Async XLA Ops:
  1.3 4.0 %copy-start.2 = (bf16[64,2,7808]{2,1,0:T(2,128)(2,1)S(1)}, bf16[64,2,7808]{2,1,0:T(2,128)(2,1)}, u32[]{:S(2)}) copy-start(bf16[64,2,7808]{2,1,0:T(2,128)(2,1)} %mine_ref) | copy-start | bytes 5996548
  1.3 13.6 %copy-start.5 = (bf16[160,112]{1,0:T(8,128)(2,1)S(1)}, bf16[160,112]{1,0:T(8,128)(2,1)}, u32[]{:S(2)}) copy-start(bf16[160,112]{1,0:T(8,128)(2,1)} %constant.49.clone.up_y_ref) | copy-start | bytes 107524
  5.4 9.4 %collective-permute-start = (bf16[1,2,7808]{2,1,0:T(2,128)(2,1)S(1)}, bf16[1,2,7808]{2,1,0:T(2,128)(2,1)S(1)}, u32[]{:S(2)}, u32[]{:S(2)}) collective-permute-start(bf16[1,2,7808]{2,1,0:T(2,128)(2,1)S(1)} %get-tuple-element.36), channel_id=1, source_target_pairs={{0,24},{8,16},{16,8},{24,0},{1,25},{9,17},{17,9},{25,1},{2,26},{10... | collective-permute-start | bytes 93704 | tf_op jit(solution)/shard_map/ppermute | solution.py:344
  7.9 7.0 %collective-permute-start.1 = (bf16[1,2,7808]{2,1,0:T(2,128)(2,1)S(1)}, bf16[1,2,7808]{2,1,0:T(2,128)(2,1)S(1)}, u32[]{:S(2)}, u32[]{:S(2)}) collective-permute-start(bf16[1,2,7808]{2,1,0:T(2,128)(2,1)S(1)} %get-tuple-element.35), channel_id=1, source_target_pairs={{0,16},{8,24},{16,0},{24,8},{1,17},{9,25},{17,1},{25,9},{2,18},{10... | collective-permute-start | bytes 93704 | tf_op jit(solution)/shard_map/ppermute | solution.py:344
  8.5 6.3 %collective-permute-start.2 = (bf16[1,2,7808]{2,1,0:T(2,128)(2,1)S(1)}, bf16[1,2,7808]{2,1,0:T(2,128)(2,1)S(1)}, u32[]{:S(2)}, u32[]{:S(2)}) collective-permute-start(bf16[1,2,7808]{2,1,0:T(2,128)(2,1)S(1)} %get-tuple-element.34), channel_id=1, source_target_pairs={{0,8},{8,0},{16,24},{24,16},{1,9},{9,1},{17,25},{25,17},{2,10},{10... | collective-permute-start | bytes 93704 | tf_op jit(solution)/shard_map/ppermute | solution.py:344
  8.5 36.6 %collective-permute-start.3 = (bf16[64,2,7808]{2,1,0:T(2,128)(2,1)S(1)}, bf16[64,2,7808]{2,1,0:T(2,128)(2,1)}, u32[]{:S(2)}, u32[]{:S(2)}) collective-permute-start(bf16[64,2,7808]{2,1,0:T(2,128)(2,1)S(1)} %copy-done.2), channel_id=1, source_target_pairs={{0,8},{8,0},{16,24},{24,16},{1,9},{9,1},{17,25},{25,17},{2,10},{10... | collective-permute-start | bytes 5996552 | tf_op jit(solution)/shard_map/ppermute | solution.py:344
  9.0 15.8 %all-to-all-start.1 = ((bf16[8,144,128]{2,1,0:T(8,128)(2,1)}), bf16[8,144,128]{2,1,0:T(8,128)(2,1)S(1)}, u32[]{:S(2)}, u32[]{:S(2)}) async-start(bf16[8,144,128]{2,1,0:T(8,128)(2,1)} %get-tuple-element.22), calls=%async_computation.1 | async-start | bytes 589824 | tf_op jit(solution)/shard_map/all_to_all | solution.py:387
  14.9 0.8 copy-start.6
  15.7 0.8 copy-start.8
  24.8 7.0 %copy-start.10 = (bf16[8,144,128]{2,1,0:T(8,128)(2,1)}, bf16[8,144,128]{2,1,0:T(8,128)(2,1)S(1)}, u32[]{:S(2)}) copy-start(bf16[8,144,128]{2,1,0:T(8,128)(2,1)S(1)} %all-to-all-done.1.in_ref) | copy-start | bytes 884740
  24.8 13.3 %all-to-all-start = ((bf16[8,144,128]{2,1,0:T(8,128)(2,1)}), bf16[8,144,128]{2,1,0:T(8,128)(2,1)S(1)}, u32[]{:S(2)}, u32[]{:S(2)}) async-start(bf16[8,144,128]{2,1,0:T(8,128)(2,1)} %shard_map.141), calls=%async_computation | async-start | bytes 589824 | tf_op jit(solution)/shard_map/all_to_all | solution.py:411
  38.1 0.7 copy-start.11
  38.9 10.7 %copy-start.13 = (f32[256]{0:T(256)S(1)}, f32[256]{0:T(256)}, u32[]{:S(2)}) copy-start(f32[256]{0:T(256)} %param.15) | copy-start | bytes 3076
  38.9 11.3 %copy-start.12 = (f32[1,7808]{1,0:T(1,128)S(1)}, f32[1,7808]{1,0:T(1,128)}, u32[]{:S(2)}) copy-start(f32[1,7808]{1,0:T(1,128)} %get-tuple-element.30) | copy-start | bytes 93700
  45.2 13.4 %all-to-all-start.2 = ((bf16[8,144,128]{2,1,0:T(8,128)(2,1)}), bf16[8,144,128]{2,1,0:T(8,128)(2,1)S(1)}, u32[]{:S(2)}, u32[]{:S(2)}) async-start(bf16[8,144,128]{2,1,0:T(8,128)(2,1)} %shard_map.143), calls=%async_computation.2 | async-start | bytes 589824 | tf_op jit(solution)/shard_map/all_to_all | solution.py:462
  50.8 7.8 %copy-start.3 = (bf16[1,2,7808]{2,1,0:T(2,128)(2,1)S(1)}, bf16[1,2,7808]{2,1,0:T(2,128)(2,1)}, u32[]{:S(2)}) copy-start(bf16[1,2,7808]{2,1,0:T(2,128)(2,1)} %resp_ref.1) | copy-start | bytes 93700
  50.8 7.8 %copy-start.4 = (bf16[112,160]{1,0:T(8,128)(2,1)S(1)}, bf16[112,160]{1,0:T(8,128)(2,1)}, u32[]{:S(2)}) copy-start(bf16[112,160]{1,0:T(8,128)(2,1)} %constant.50.clone.down_y_ref) | copy-start | bytes 107524
  50.8 7.8 %copy-start.7 = (s32[1,7808]{1,0:T(1,128)S(1)}, s32[1,7808]{1,0:T(1,128)}, u32[]{:S(2)}) copy-start(s32[1,7808]{1,0:T(1,128)} %get-tuple-element.18.row_ref) | copy-start | bytes 93700
  50.8 7.8 %copy-start.9 = (s32[1,7808]{1,0:T(1,128)S(1)}, s32[1,7808]{1,0:T(1,128)}, u32[]{:S(2)}) copy-start(s32[1,7808]{1,0:T(1,128)} %get-tuple-element.19.z_ref) | copy-start | bytes 93700
  52.8 1.9 %copy-start = (bf16[128,2,7808]{2,1,0:T(2,128)(2,1)}, bf16[128,2,7808]{2,1,0:T(2,128)(2,1)S(1)}, u32[]{:S(2)}) copy-start(bf16[128,2,7808]{2,1,0:T(2,128)(2,1)S(1)} %shard_map.144) | copy-start | bytes 11993092
  58.6 7.2 %copy-start.1 = (bf16[128,2,7808]{2,1,0:T(2,128)(2,1)S(1)}, bf16[128,2,7808]{2,1,0:T(2,128)(2,1)}, u32[]{:S(2)}) copy-start(bf16[128,2,7808]{2,1,0:T(2,128)(2,1)} %copy-done) | copy-start | bytes 11993092
  61.3 4.0 %collective-permute-start.4 = (bf16[1,2,7808]{2,1,0:T(2,128)(2,1)S(1)}, bf16[1,2,7808]{2,1,0:T(2,128)(2,1)S(1)}, u32[]{:S(2)}, u32[]{:S(2)}) collective-permute-start(bf16[1,2,7808]{2,1,0:T(2,128)(2,1)S(1)} %get-tuple-element.32), channel_id=1, source_target_pairs={{0,16},{8,24},{16,0},{24,8},{1,17},{9,25},{17,1},{25,9},{2,18},{10... | collective-permute-start | bytes 93704 | tf_op jit(solution)/shard_map/ppermute | solution.py:344
  67.1 3.6 %collective-permute-start.5 = (f32[2,128,2]{1,2,0:T(2,128)S(1)}, f32[2,128,2]{1,2,0:T(2,128)S(1)}, u32[]{:S(2)}, u32[]{:S(2)}) collective-permute-start(f32[2,128,2]{1,2,0:T(2,128)S(1)} %fusion.5), channel_id=1, source_target_pairs={{0,1},{1,0},{2,3},{3,2},{4,5},{5,4},{6,7},{7,6},{8,9},{9,8},{10,11... | collective-permute-start | bytes 6152 | tf_op jit(solution)/shard_map/ppermute | solution.py:344
  70.7 4.4 %collective-permute-start.6 = (f32[2,128,2]{1,2,0:T(2,128)S(1)}, f32[2,128,2]{1,2,0:T(2,128)S(1)}, u32[]{:S(2)}, u32[]{:S(2)}) collective-permute-start(f32[2,128,2]{1,2,0:T(2,128)S(1)} %add.51), channel_id=1, source_target_pairs={{0,2},{1,3},{2,0},{3,1},{4,6},{5,7},{6,4},{7,5},{8,10},{9,11},{10,... | collective-permute-start | bytes 6152 | tf_op jit(solution)/shard_map/ppermute | solution.py:344
  71.8 4.5 %collective-permute-start.7 = (f32[2,128,2]{1,2,0:T(2,128)S(1)}, f32[2,128,2]{1,2,0:T(2,128)S(1)}, u32[]{:S(2)}, u32[]{:S(2)}) collective-permute-start(f32[2,128,2]{1,2,0:T(2,128)S(1)} %add.51), channel_id=1, source_target_pairs={{0,4},{1,5},{2,6},{3,7},{4,0},{5,1},{6,2},{7,3},{8,12},{9,13},{10,... | collective-permute-start | bytes 6152 | tf_op jit(solution)/shard_map/ppermute | solution.py:344
  72.4 5.4 %collective-permute-start.8 = (f32[2,128,2]{1,2,0:T(2,128)S(1)}, f32[2,128,2]{1,2,0:T(2,128)S(1)}, u32[]{:S(2)}, u32[]{:S(2)}) collective-permute-start(f32[2,128,2]{1,2,0:T(2,128)S(1)} %add.51), channel_id=1, source_target_pairs={{0,6},{1,7},{2,4},{3,5},{4,2},{5,3},{6,0},{7,1},{8,14},{9,15},{10,... | collective-permute-start | bytes 6152 | tf_op jit(solution)/shard_map/ppermute | solution.py:344
  78.5 4.0 %collective-permute-start.9 = (bf16[1,2,7808]{2,1,0:T(2,128)(2,1)S(1)}, bf16[1,2,7808]{2,1,0:T(2,128)(2,1)S(1)}, u32[]{:S(2)}, u32[]{:S(2)}) collective-permute-start(bf16[1,2,7808]{2,1,0:T(2,128)(2,1)S(1)} %slice.43), channel_id=1, source_target_pairs={{0,16},{8,24},{16,0},{24,8},{1,17},{9,25},{17,1},{25,9},{2,18},{10... | collective-permute-start | bytes 93704 | tf_op jit(solution)/shard_map/ppermute | solution.py:344

commit v3 on v2

--- a/solution.py
+++ b/solution.py
@@ -11,6 +11,9 @@
 from jax.sharding import PartitionSpec as P
 
 F32, BF16, I32 = jnp.float32, jnp.bfloat16, jnp.int32
+
+
+SCATTER_LIMIT, MIX_LIMIT = 24, 16
 
 
 def up(value, step):
@@ -65,8 +68,11 @@
         up_y = np.concatenate([padded(cos_y, grid, ypad), padded(sin_y, grid, ypad)], 1)
         down_y = np.concatenate([padded(cos_y.T, ypad, grid), padded(-sin_y.T, ypad, grid)], 0)
         cos_z, sin_z = padded(cos_y, grid, zpad), padded(sin_y, grid, zpad)
+        cos_z, sin_z = (padded(part, up(grid, 128), zpad) for part in (cos_z, sin_z))
         up_z = np.stack([np.concatenate([cos_z.T, -sin_z.T], 0), np.concatenate([sin_z.T, cos_z.T], 0)])
-        down_z = np.stack([np.concatenate([cos_z, -sin_z], 1), np.concatenate([sin_z, cos_z], 1)])
+        down_z = np.concatenate(
+            [np.concatenate([cos_z, -sin_z], 1), np.concatenate([sin_z, cos_z], 1)], 0
+        )
         planes = np.array([p + self.blocks * x for p in range(self.blocks) for x in self.planes])
         cos_x, sin_x = self.waves(every, planes)
 
@@ -106,15 +112,22 @@
     return lax.broadcasted_iota(I32, (rows, index.shape[1]), 0) == index
 
 
-def scattered(box, row_ref, z_ref, value_ref, up_y_ref, out_ref, space_ref):
+def scatter_kernel(box, choice_ref, row_ref, z_ref, resp_ref, *refs):
+    *partner_refs, up_y_ref, out_ref, space_ref = refs
     zpad, ypad, slab = box.zpad, box.ypad, box.slab
-    total = None
+    choice, total = choice_ref[0], None
     for start, size in chunks(box.count, 1024):
         span = slice(start, start + size)
         chosen = jnp.where(pick_rows(box.slots * ypad, row_ref[:, span]), 1.0, 0.0).astype(BF16)
         at_z = pick_rows(zpad, z_ref[:, span])
-        pair = value_ref[0, :, span].astype(F32)
-        values = [jnp.where(at_z, pair[c : c + 1], 0.0).astype(BF16) for c in range(2)]
+        partner = partner_refs[0][0, :, span].astype(F32)
+        for k, ref in enumerate(partner_refs[1:]):
+            partner = jnp.where(choice == k + 1, ref[0, :, span].astype(F32), partner)
+        values = [
+            jnp.where(at_z, pair[c : c + 1], 0.0).astype(BF16)
+            for pair in (resp_ref[0, :, span].astype(F32), partner)
+            for c in range(2)
+        ]
         piece = dot(chosen, jnp.concatenate(values, 0), ((1,), (1,)))
         total = piece if total is None else total + piece
     for s in range(box.slots):
@@ -135,7 +148,7 @@
     return folded * folded
 
 
-def first_kernel(box, map_ref, value_ref, up_y_ref, out_ref, row_ref, z_ref, kinetic_ref, space_ref):
+def index_kernel(box, map_ref, resp_ref, table_ref, row_ref, z_ref, kinetic_ref, resp_out, table_out):
     grid, cell = box.grid, map_ref[...][None, :].astype(F32)
     local_x = jnp.floor((cell + 0.5) * (1.0 / (grid * grid)))
     cell = cell - local_x * (grid * grid)
@@ -152,13 +165,14 @@
     slot = jnp.where(local_x < box.low, local_x, local_x - (box.slab - box.slots))
     row_ref[...] = (slot * box.ypad + boxed(grid_y)).astype(I32)
     z_ref[...] = boxed(grid_z).astype(I32)
-    scattered(box, row_ref, z_ref, value_ref, up_y_ref, out_ref, space_ref)
+    resp_out[...] = resp_ref[...]
+    table_out[...] = table_ref[...]
 
 
 def spread_rows(box, in_ref, from_ref):
     stride = box.spad * box.slab
     for p in range(box.blocks):
-        for t in range(2 * box.zpad // 128):
+        for t in range(from_ref.shape[0]):
             from_ref[t, p * stride : p * stride + box.rows, :] = in_ref[
                 p, :, t * 128 : (t + 1) * 128
             ].astype(F32)
@@ -168,107 +182,52 @@
                 )
 
 
-def along_x(box, from_ref, up_x_ref, wide_ref):
+def along_x(box, from_ref, field, up_x_ref, wide_ref):
     zpad, planes = box.zpad, box.blocks * box.spad
+    tiles = 2 * zpad // 128
     both = []
     for line in range(box.slab):
         plane = jnp.concatenate(
-            [from_ref[t, pl.ds(line, planes, stride=box.slab), :] for t in range(2 * zpad // 128)], 1
+            [
+                from_ref[field * tiles + t, pl.ds(line, planes, stride=box.slab), :]
+                for t in range(tiles)
+            ],
+            1,
         )
         both.append(jnp.concatenate([plane, quarter(plane, zpad)], 0).astype(BF16))
     wide = dot(up_x_ref[...], jnp.concatenate(both, 1)).astype(BF16)
     for line in range(box.slab):
-        wide_ref[line] = wide[:, line * 2 * zpad : (line + 1) * 2 * zpad]
-
-
-def line_groups(box):
-    return [slice(start, start + size) for start, size in chunks(box.slab, 5)]
-
-
-def response_kernel(
-    box,
-    in_ref,
-    pot_ref,
-    up_x_ref,
-    up_z_ref,
-    real_ref,
-    imag_ref,
-    from_ref,
-    wide_ref,
-    pot_held,
-    real_held,
-    imag_held,
-    sems,
-    out_sems,
-):
-    copies = {
-        lines.start: pltpu.make_async_copy(pot_ref.at[lines], pot_held.at[lines], sems.at[n])
-        for n, lines in enumerate(line_groups(box))
-    }
-    for copy in copies.values():
-        copy.start()
+        wide_ref[field, line] = wide[:, line * 2 * zpad : (line + 1) * 2 * zpad]
+
+
+def x_kernel(box, in_ref, up_x_ref, wide_ref, from_ref):
     spread_rows(box, in_ref, from_ref)
-    along_x(box, from_ref, up_x_ref, wide_ref)
-    outs = []
-    for n, lines in enumerate(line_groups(box)):
-        copies[lines.start].wait()
-        for line in range(lines.start, lines.stop):
-            for d, held in enumerate((real_held, imag_held)):
-                held[line] = (pot_held[line] * dot(wide_ref[line], up_z_ref[d])).astype(BF16)
-        for d, (held, ref) in enumerate(((real_held, real_ref), (imag_held, imag_ref))):
-            outs.append(pltpu.make_async_copy(held.at[lines], ref.at[lines], out_sems.at[n, d]))
-            outs[-1].start()
-    for copy in outs:
-        copy.wait()
+    for field in range(2):
+        along_x(box, from_ref, field, up_x_ref, wide_ref)
 
 
 def mix_kernel(
-    box,
-    in_ref,
-    real_ref,
-    imag_ref,
-    con_ref,
-    up_x_ref,
-    down_x_ref,
-    up_z_ref,
-    down_z_ref,
-    out_ref,
-    from_ref,
-    to_ref,
-    wide_ref,
-    back_ref,
-    real_held,
-    imag_held,
-    con_held,
-    sems,
+    box, wide_ref, pot_ref, con_ref, down_x_ref, up_z_ref, down_z_ref, out_ref, to_ref, back_ref
 ):
     zpad, stride = box.zpad, box.spad * box.slab
     planes, tiles = box.blocks * box.spad, 2 * zpad // 128
-    pairs = ((real_ref, real_held), (imag_ref, imag_held), (con_ref, con_held))
-    copies = [
-        [
-            pltpu.make_async_copy(ref.at[lines], held.at[lines], sems.at[n, k])
-            for k, (ref, held) in enumerate(pairs)
+    pair = 2 if box.slab % 2 == 0 else 1
+    for first in range(0, box.slab, pair):
+        lines = range(first, first + pair)
+        potential, contact, resp, part = (
+            jnp.concatenate([ref[line] for line in lines], 0)
+            for ref in (pot_ref, con_ref, wide_ref.at[0], wide_ref.at[1])
+        )
+        potential, contact = potential.astype(F32), contact.astype(F32)
+        mixed = [
+            (potential * dot(resp, up_z_ref[d]) + contact * dot(part, up_z_ref[d])).astype(BF16)
+            for d in range(2)
         ]
-        for n, lines in enumerate(line_groups(box))
-    ]
-    for copy in sum(copies[:2], []):
-        copy.start()
-    spread_rows(box, in_ref, from_ref)
-    along_x(box, from_ref, up_x_ref, wide_ref)
-    for n, lines in enumerate(line_groups(box)):
-        for copy in copies[n]:
-            copy.wait()
-        for copy in sum(copies[n + 2 : n + 3], []):
-            copy.start()
-        for line in range(lines.start, lines.stop):
-            contact = con_held[line].astype(F32)
-            mixed = [
-                (held[line].astype(F32) + contact * dot(wide_ref[line], up_z_ref[d])).astype(BF16)
-                for d, held in enumerate((real_held, imag_held))
+        back = dot(jnp.concatenate(mixed, 1), down_z_ref[...]).astype(BF16)
+        for n, line in enumerate(lines):
+            back_ref[:, line * 2 * zpad : (line + 1) * 2 * zpad] = back[
+                n * box.grid : (n + 1) * box.grid
             ]
-            back = dot(mixed[0], down_z_ref[0]) + dot(mixed[1], down_z_ref[1])
-            back_ref[:, line * 2 * zpad : (line + 1) * 2 * zpad] = back.astype(BF16)
     parts = dot(down_x_ref[...], back_ref[...])
     lined = parts[:planes] + quarter(parts[planes:], zpad)
     for line in range(box.slab):
@@ -324,16 +283,16 @@
         low_ref[0, :, span] = both.astype(BF16)
 
 
-def call(kernel, out_shape, scratch, args, flops, limit, left=(), out_left=False):
+def call(kernel, out_shape, scratch, args, flops, limit, left=(), resident=(), scalars=()):
+    def space(n):
+        if n in left:
+            return pltpu.HBM
+        return pltpu.VMEM if n in resident else pltpu.SMEM if n in scalars else None
+
     return pl.pallas_call(
         kernel,
         out_shape=out_shape,
-        in_specs=[
-            pl.BlockSpec(memory_space=pltpu.HBM if n in left else None) for n in range(len(args))
-        ],
-        out_specs=jax.tree.map(
-            lambda _: pl.BlockSpec(memory_space=pltpu.HBM if out_left else None), out_shape
-        ),
+        in_specs=[pl.BlockSpec(memory_space=space(n)) for n in range(len(args))],
         scratch_shapes=scratch,
         compiler_params=pltpu.CompilerParams(vmem_limit_bytes=limit << 20),
         cost_estimate=pl.CostEstimate(flops=flops, bytes_accessed=4 << 20, transcendentals=0),
@@ -366,26 +325,6 @@
     band_me = lax.axis_index("band")
     first_row = offset[0]
 
-    shape = (blocks, box.rows, 2 * box.zpad)
-    tiles, height = 2 * box.zpad // 128, blocks * box.spad * box.slab
-    index_shape = jax.ShapeDtypeStruct((1, count), I32)
-    field, row_index, z_index, kinetic = call(
-        functools.partial(first_kernel, box),
-        (
-            jax.ShapeDtypeStruct(shape, BF16),
-            index_shape,
-            index_shape,
-            jax.ShapeDtypeStruct((1, count), F32),
-        ),
-        [pltpu.VMEM(shape, F32)],
-        (grid_map, response, up_y),
-        1 << 31,
-        56,
-    )
-    field, panel, contact = lax.optimization_barrier((field, panel, contact))
-    contact_low = jnp.transpose(contact, (1, 0, 2)).astype(BF16)
-    field = lax.all_to_all(field, "pw", split_axis=0, concat_axis=0, tiled=True)
-
     local = first_row - band_me * rows_here
     candidates = []
     for distance in range(bands):
@@ -393,61 +332,69 @@
         row = lax.dynamic_slice_in_dim(panel, row, 1, 0)
         candidates.append(xor_permute(row, "band", bands, distance) if distance else row)
     owner = (first_row + band_me) // rows_here
-    partner = candidates[0]
-    for distance in range(1, bands):
-        partner = jnp.where(owner == band_me ^ distance, candidates[distance], partner)
-    beside = with_layout_constraint(xor_permute(panel, "band", bands, 1), Layout((0, 1, 2)))
+    choice = (owner ^ band_me)[None]
+
+    index_shape = jax.ShapeDtypeStruct((1, count), I32)
+    row_index, z_index, kinetic, resp_here, up_y_here = call(
+        functools.partial(index_kernel, box),
+        (
+            index_shape,
+            index_shape,
+            jax.ShapeDtypeStruct((1, count), F32),
+            jax.ShapeDtypeStruct(response.shape, BF16),
+            jax.ShapeDtypeStruct(up_y.shape, BF16),
+        ),
+        [],
+        (grid_map, response, up_y),
+        1 << 20,
+        16,
+    )
+    shape = (blocks, box.rows, 2 * box.zpad)
+    both_shape = (blocks, box.rows, 4 * box.zpad)
+    field = call(
+        functools.partial(scatter_kernel, box),
+        jax.ShapeDtypeStruct(both_shape, BF16),
+        [pltpu.VMEM(both_shape, F32)],
+        (choice, row_index, z_index, resp_here, *candidates, up_y_here),
+        1 << 32,
+        SCATTER_LIMIT,
+        (),
+        range(1, 5 + bands),
+        (0,),
+    )
+    field, panel_sent, potential, contact = lax.optimization_barrier((field, panel, potential, contact))
+    potential_low, contact_low = (
+        jnp.pad(jnp.transpose(value, (1, 0, 2)).astype(BF16), ((0, 0), (0, 0), (0, -grid % 128)))
+        for value in (potential, contact)
+    )
+    beside = with_layout_constraint(xor_permute(panel_sent, "band", bands, 1), Layout((0, 1, 2)))
     shift = lax.dynamic_slice_in_dim(energies, first_row + band_me, 1, 0)
     factor = kinetic - shift[0]
-
-    other_field = call(
-        functools.partial(scattered, box),
-        jax.ShapeDtypeStruct(shape, BF16),
-        [pltpu.VMEM(shape, F32)],
-        (row_index, z_index, partner, up_y),
+    field = lax.all_to_all(field, "pw", split_axis=0, concat_axis=0, tiled=True)
+
+    tiles, height = 2 * box.zpad // 128, blocks * box.spad * box.slab
+    wide = call(
+        functools.partial(x_kernel, box),
+        jax.ShapeDtypeStruct((2, box.slab, grid, 2 * box.zpad), BF16),
+        [pltpu.VMEM((2 * tiles, height, 128), F32)],
+        (field, up_x),
         1 << 31,
-        16,
-    )
-    other_field = lax.all_to_all(other_field, "pw", split_axis=0, concat_axis=0, tiled=True)
-    groups = len(line_groups(box))
-    space = (box.slab, grid, grid)
-    columns = pltpu.VMEM((tiles, height, 128), F32)
-    wide = pltpu.VMEM((box.slab, grid, 2 * box.zpad), BF16)
-    real, imag = call(
-        functools.partial(response_kernel, box),
-        (jax.ShapeDtypeStruct(space, BF16), jax.ShapeDtypeStruct(space, BF16)),
-        [
-            columns,
-            wide,
-            pltpu.VMEM(space, F32),
-            pltpu.VMEM(space, BF16),
-            pltpu.VMEM(space, BF16),
-            pltpu.SemaphoreType.DMA((groups,)),
-            pltpu.SemaphoreType.DMA((groups, 2)),
-        ],
-        (field, jnp.transpose(potential, (1, 0, 2)), up_x, up_z),
-        1 << 32,
-        60,
-        (1,),
-        True,
+        MIX_LIMIT,
+        (),
+        range(2),
     )
     returned = call(
         functools.partial(mix_kernel, box),
         jax.ShapeDtypeStruct(shape, BF16),
         [
-            columns,
-            columns,
-            wide,
+            pltpu.VMEM((tiles, height, 128), F32),
             pltpu.VMEM((grid, box.slab * 2 * box.zpad), BF16),
-            pltpu.VMEM(space, BF16),
-            pltpu.VMEM(space, BF16),
-            pltpu.VMEM(space, BF16),
-            pltpu.SemaphoreType.DMA((groups, 3)),
         ],
-        (other_field, real, imag, contact_low, up_x, down_x, up_z, down_z),
+        (wide, potential_low, contact_low, down_x, up_z, down_z),
         1 << 32,
-        60,
-        (1, 2, 3),
+        MIX_LIMIT,
+        (),
+        range(6),
     )
     returned, panel_late, beside = lax.optimization_barrier((returned, panel, beside))
     rows_both = pl.pallas_call(

time: 83.9 us -> 78.7 us (0.938)
  Pallas kernels: 22.5 us -> 12.4 us
  starting transfers between devices: 26.7 us -> 20.5 us
  waiting for transfers between devices: 20.4 us -> 26.4 us
  local copies, waits for them, and re-layouts: 4.9 us -> 10 us
    pallas_call x5, Pallas kernels: 20.6 us -> 10.5 us  [call(): pl.pallas_call(kernel, out_shape=out_shape, in_specs=[pl.BlockSpec(memory...]
    all_to_all x1, waiting for transfers between devices: 5.39 us -> 10 us  [on_device(): field = lax.all_to_all(field, 'pw', split_axis=0, concat_axis=0, tiled=True)]
    all_to_all x1 -> x0, starting transfers between devices: 3.64 us -> none  [on_device(): lax.all_to_all(other_field, 'pw', split_axis=0, concat_axis=0, tiled=True)]
    pad x0 -> x2, local copies, waits for them, and re-layouts: none -> 2.99 us  [on_device(): jnp.pad(jnp.transpose(value, (1, 0, 2)).astype(BF16), ((0, 0), (0, 0), (0...]
    ppermute x10, waiting for transfers between devices: 9.36 us -> 11.8 us  [xor_permute(): lax.ppermute(value, axis, [(source, source ^ distance) for source in rang...]
    ppermute x10, starting transfers between devices: 12.9 us -> 11.1 us  [xor_permute(): lax.ppermute(value, axis, [(source, source ^ distance) for source in rang...]
    all_to_all x1 -> x0, waiting for transfers between devices: 1.68 us -> none  [on_device(): lax.all_to_all(other_field, 'pw', split_axis=0, concat_axis=0, tiled=True)]
    unnamed x29 -> x31, local copies, waits for them, and re-layouts: 4.18 us -> 5.4 us
  transfers between devices with their start and end apart: 13 -> 12, of which waited for: 8 -> 8; matrix products, arithmetic and copies ran while one was open for 6% -> 10% of each run, Pallas kernels for 19% -> 8%
where the time goes in v3:
time: 78.7 us; the launch traced here: 78.1 us
  waiting for transfers between devices  26.4 us (34%)
  starting transfers between devices  20.5 us (26%)
  Pallas kernels  12.4 us (16%)
  local copies, waits for them, and re-layouts  10 us (13%)
  other arithmetic  5.28 us (7%)
  matrix products  1.9 us (2%)
  between operations  1.49 us (2%)
    ppermute x10, waiting for transfers between devices, xor_permute(): lax.ppermute(value, axis, [(source, source ^ distance) for source in rang...  11.8 us
    ppermute x10, starting transfers between devices, xor_permute(): lax.ppermute(value, axis, [(source, source ^ distance) for source in rang...  11.1 us
    pallas_call x5, Pallas kernels, call(): pl.pallas_call(kernel, out_shape=out_shape, in_specs=[pl.BlockSpec(memory...  10.5 us
    all_to_all x1, waiting for transfers between devices, on_device(): field = lax.all_to_all(field, 'pw', split_axis=0, concat_axis=0, tiled=True)  10 us
    all_to_all x1, starting transfers between devices, on_device(): field = lax.all_to_all(field, 'pw', split_axis=0, concat_axis=0, tiled=True)  5.81 us
    unnamed x31, local copies, waits for them, and re-layouts  5.4 us
    all_to_all x1, waiting for transfers between devices, on_device(): lax.all_to_all(returned, 'pw', split_axis=0, concat_axis=0, tiled=True)  4.6 us
    all_to_all x1, starting transfers between devices, on_device(): lax.all_to_all(returned, 'pw', split_axis=0, concat_axis=0, tiled=True)  3.64 us
  transfers between devices with their start and end apart: 12, of which 8 were waited for; matrix products, arithmetic and copies ran while one was open for 10% of the time, Pallas kernels for 8%

profile of v3, /device:TPU:0, one launch (start us, length us, event | category | flops | bytes accessed | tf_op | source)
XLA Modules:
  0.0 78.1 jit_solution(13688416399712376249)
XLA Ops:
  1.3 1.0 %constant_dynamic-slice_fusion = (bf16[1,2,7808]{2,1,0:T(2,128)(2,1)S(1)}, bf16[1,2,7808]{2,1,0:T(2,128)(2,1)S(1)}, bf16[1,2,7808]{2,1,0:T(2,128)(2,1)S(1)}, bf16[1,2,7808]{2,1,0:T(2,128)(2,1)S(1)}) fusion(bf16[64,2,7808]{2,1,0:T(2,128)(2,1)} %mine_ref, s32[]{:T(128)S(6)} %min.16, s32[]{:T(128)S(6)} %min.15, s32[]{:T(128)S(6)} %min.14, s32[]{:T(128)S(6)} %min.13), kind=kLoop, calls=%fused_computation.27 | loop fusion | bytes 249872 | tf_op jit(solution)/shard_map/dynamic_slice | solution.py:332
  2.8 2.6 %collective-permute-start.1 = (bf16[1,2,7808]{2,1,0:T(2,128)(2,1)S(1)}, bf16[1,2,7808]{2,1,0:T(2,128)(2,1)S(1)}, u32[]{:S(2)}, u32[]{:S(2)}) collective-permute-start(bf16[1,2,7808]{2,1,0:T(2,128)(2,1)S(1)} %get-tuple-element.35), channel_id=1, source_target_pairs={{0,16},{8,24},{16,0},{24,8},{1,17},{9,25},{17,1},{25,9},{2,18},{10... | collective-permute-start | bytes 93704 | tf_op jit(solution)/shard_map/ppermute | solution.py:303
  5.5 0.8 copy-done.5
  6.2 0.8 copy-done.7
  7.0 0.8 copy-done.8
  7.9 0.9 %collective-permute-done.2.refs_3_ = bf16[1,2,7808]{2,1,0:T(2,128)(2,1)S(1)} collective-permute-done((bf16[1,2,7808]{2,1,0:T(2,128)(2,1)S(1)}, bf16[1,2,7808]{2,1,0:T(2,128)(2,1)S(1)}, u32[]{:S(2)}, u32[]{:S(2)}) %collective-permute-start.2) | collective-permute-done | bytes 31264 | tf_op jit(solution)/shard_map/ppermute | solution.py:303
  8.7 3.3 %shard_map.141 = bf16[8,144,256]{2,1,0:T(8,128)(2,1)} custom-call(s32[1]{0:T(128)} %bitcast.1.choice_ref, s32[1,7808]{1,0:T(1,128)S(1)} %get-tuple-element.18.row_ref, s32[1,7808]{1,0:T(1,128)S(1)} %get-tuple-element.19.z_ref, bf16[1,2,7808]{2,1,0:T(2,128)(2,1)S(1)} %get-tuple-element.20.resp_ref, bf16[1,2,7808]{2,1,0:T(2,128)(2,1)S(1)} %get-tuple-element.37.refs_0_, ...), custom_call_target="tpu_custom_call" | custom-call | flops 4294967296 | bytes 4194304 | tf_op jit(solution)/shard_map/pallas_call | solution.py:292
  12.2 5.8 %all-to-all-start = ((bf16[8,144,256]{2,1,0:T(8,128)(2,1)}), bf16[8,144,256]{2,1,0:T(8,128)(2,1)S(1)}, u32[]{:S(2)}, u32[]{:S(2)}) async-start(bf16[8,144,256]{2,1,0:T(8,128)(2,1)} %shard_map.141), calls=%async_computation | async-start | bytes 1179648 | tf_op jit(solution)/shard_map/all_to_all | solution.py:373
  18.0 3.4 %convert_bitcast_fusion = (bf16[20,160,160]{2,1,0:T(8,128)(2,1)S(1)}, bf16[20,160,160]{2,1,0:T(8,128)(2,1)S(1)}) fusion(f32[160,20,160]{2,0,1:T(8,128)} %param.19, f32[160,20,160]{2,0,1:T(8,128)} %param.18), kind=kLoop, calls=%fused_computation.6 | loop fusion | flops 1024000 | bytes 6144000 | tf_op jit(solution)/shard_map/convert_element_type | solution.py:367
  21.4 1.5 %pad.7.pot_ref = bf16[20,160,256]{2,1,0:T(8,128)(2,1)} pad(bf16[20,160,160]{2,1,0:T(8,128)(2,1)S(1)} %get-tuple-element.50, bf16[]{:T(256)} %constant.48.clone.1), padding=0_0x0_0x0_96 | pad | bytes 2662402 | tf_op jit(solution)/shard_map/jit(_pad)/pad | solution.py:367
  22.8 1.5 %pad.8.con_ref = bf16[20,160,256]{2,1,0:T(8,128)(2,1)} pad(bf16[20,160,160]{2,1,0:T(8,128)(2,1)S(1)} %get-tuple-element.49, bf16[]{:T(256)} %constant.48.clone.1), padding=0_0x0_0x0_96 | pad | bytes 2662402 | tf_op jit(solution)/shard_map/jit(_pad)/pad | solution.py:367
  24.4 10.0 %all-to-all-done.in_ref = bf16[8,144,256]{2,1,0:T(8,128)(2,1)S(1)} async-done(((bf16[8,144,256]{2,1,0:T(8,128)(2,1)}), bf16[8,144,256]{2,1,0:T(8,128)(2,1)S(1)}, u32[]{:S(2)}, u32[]{:S(2)}) %all-to-all-start) | async-done | bytes 589856 | tf_op jit(solution)/shard_map/all_to_all | solution.py:373
  34.4 0.7 shard_map.142.wide_ref
  36.3 3.8 %shard_map.143 = bf16[8,144,128]{2,1,0:T(8,128)(2,1)} custom-call(bf16[2,20,160,128]{3,2,1,0:T(8,128)(2,1)S(1)} %shard_map.142.wide_ref, bf16[20,160,256]{2,1,0:T(8,128)(2,1)S(1)} %copy-done.3, bf16[20,160,256]{2,1,0:T(8,128)(2,1)S(1)} %copy-done.4, bf16[128,160]{1,0:T(8,128)(2,1)S(1)} %copy-done.11, bf16[2,128,256]{2,1,0:T(8,128)(2,1)S(1)} %copy-done.9, ...), custom_call_target="tpu_custom_call" | custom-call | flops 4294967296 | bytes 4194304 | tf_op jit(solution)/shard_map/pallas_call | solution.py:292
  40.1 3.6 %all-to-all-start.1 = ((bf16[8,144,128]{2,1,0:T(8,128)(2,1)}), bf16[8,144,128]{2,1,0:T(8,128)(2,1)S(1)}, u32[]{:S(2)}, u32[]{:S(2)}) async-start(bf16[8,144,128]{2,1,0:T(8,128)(2,1)} %shard_map.143), calls=%async_computation.1 | async-start | bytes 589824 | tf_op jit(solution)/shard_map/all_to_all | solution.py:409
  44.3 0.7 add_reduce_fusion
  45.1 1.9 %shard_map.144 = bf16[128,2,7808]{2,1,0:T(2,128)(2,1)S(1)} custom-call(bf16[64,2,7808]{2,1,0:T(2,128)(2,1)S(1)} %copy-done.2, bf16[64,2,7808]{2,1,0:T(2,128)(2,1)} %collective-permute-done.3.other_ref), custom_call_target="tpu_custom_call" | custom-call | bytes 8388608 | tf_op jit(solution)/shard_map/pallas_call | solution.py:400
  47.0 1.9 %copy-done = bf16[128,2,7808]{2,1,0:T(2,128)(2,1)} copy-done((bf16[128,2,7808]{2,1,0:T(2,128)(2,1)}, bf16[128,2,7808]{2,1,0:T(2,128)(2,1)S(1)}, u32[]{:S(2)}) %copy-start) | copy-done | bytes 3997720
  48.9 4.6 %all-to-all-done.1.in_ref = bf16[8,144,128]{2,1,0:T(8,128)(2,1)S(1)} async-done(((bf16[8,144,128]{2,1,0:T(8,128)(2,1)}), bf16[8,144,128]{2,1,0:T(8,128)(2,1)S(1)}, u32[]{:S(2)}, u32[]{:S(2)}) %all-to-all-start.1) | async-done | bytes 294944 | tf_op jit(solution)/shard_map/all_to_all | solution.py:409
  53.5 2.7 %shard_map.145 = (bf16[1,2,7808]{2,1,0:T(2,128)(2,1)S(1)}, f32[1,2,7808]{2,1,0:T(2,128)S(1)}) custom-call(bf16[8,144,128]{2,1,0:T(8,128)(2,1)S(1)} %all-to-all-done.1.in_ref, s32[1,7808]{1,0:T(1,128)S(1)} %get-tuple-element.18.row_ref, s32[1,7808]{1,0:T(1,128)S(1)} %get-tuple-element.19.z_ref, bf16[1,2,7808]{2,1,0:T(2,128)(2,1)S(1)} %copy-done.6, ...), custom_call_target="tpu_custom_call" | custom-call | flops 4294967296 | bytes 4194304 | tf_op jit(solution)/shard_map/pallas_call | solution.py:292
  56.2 0.9 %collective-permute-start.4 = (bf16[1,2,7808]{2,1,0:T(2,128)(2,1)S(1)}, bf16[1,2,7808]{2,1,0:T(2,128)(2,1)S(1)}, u32[]{:S(2)}, u32[]{:S(2)}) collective-permute-start(bf16[1,2,7808]{2,1,0:T(2,128)(2,1)S(1)} %get-tuple-element.32), channel_id=1, source_target_pairs={{0,16},{8,24},{16,0},{24,8},{1,17},{9,25},{17,1},{25,9},{2,18},{10... | collective-permute-start | bytes 93704 | tf_op jit(solution)/shard_map/ppermute | solution.py:303
  57.2 3.0 %collective-permute-done.4 = bf16[1,2,7808]{2,1,0:T(2,128)(2,1)S(1)} collective-permute-done((bf16[1,2,7808]{2,1,0:T(2,128)(2,1)S(1)}, bf16[1,2,7808]{2,1,0:T(2,128)(2,1)S(1)}, u32[]{:S(2)}, u32[]{:S(2)}) %collective-permute-start.4) | collective-permute-done | bytes 31264 | tf_op jit(solution)/shard_map/ppermute | solution.py:303
  60.7 1.2 %fusion.5 = f32[2,128,2]{1,2,0:T(2,128)S(1)} fusion(bf16[128,2,7808]{2,1,0:T(2,128)(2,1)S(1)} %copy-done.1, bf16[2,2,2,7808]{3,2,1,0:T(2,128)(2,1)S(1)} %pad_maximum_fusion), kind=kOutput, calls=%fused_computation.8 | convolution fusion | flops 15990784 | bytes 4124672 | tf_op jit(solution)/shard_map/mcj,dncj->dmn/dot_general | solution.py:429
  61.9 1.5 %collective-permute-start.5 = (f32[2,128,2]{1,2,0:T(2,128)S(1)}, f32[2,128,2]{1,2,0:T(2,128)S(1)}, u32[]{:S(2)}, u32[]{:S(2)}) collective-permute-start(f32[2,128,2]{1,2,0:T(2,128)S(1)} %fusion.5), channel_id=1, source_target_pairs={{0,1},{1,0},{2,3},{3,2},{4,5},{5,4},{6,7},{7,6},{8,9},{9,8},{10,11... | collective-permute-start | bytes 6152 | tf_op jit(solution)/shard_map/ppermute | solution.py:303
  63.4 2.1 %collective-permute-done.5 = f32[2,128,2]{1,2,0:T(2,128)S(1)} collective-permute-done((f32[2,128,2]{1,2,0:T(2,128)S(1)}, f32[2,128,2]{1,2,0:T(2,128)S(1)}, u32[]{:S(2)}, u32[]{:S(2)}) %collective-permute-start.5) | collective-permute-done | bytes 2080 | tf_op jit(solution)/shard_map/ppermute | solution.py:303
  65.5 1.1 %collective-permute-start.6 = (f32[2,128,2]{1,2,0:T(2,128)S(1)}, f32[2,128,2]{1,2,0:T(2,128)S(1)}, u32[]{:S(2)}, u32[]{:S(2)}) collective-permute-start(f32[2,128,2]{1,2,0:T(2,128)S(1)} %add.55), channel_id=1, source_target_pairs={{0,2},{1,3},{2,0},{3,1},{4,6},{5,7},{6,4},{7,5},{8,10},{9,11},{10,... | collective-permute-start | bytes 6152 | tf_op jit(solution)/shard_map/ppermute | solution.py:303
  67.3 2.6 %collective-permute-start.8 = (f32[2,128,2]{1,2,0:T(2,128)S(1)}, f32[2,128,2]{1,2,0:T(2,128)S(1)}, u32[]{:S(2)}, u32[]{:S(2)}) collective-permute-start(f32[2,128,2]{1,2,0:T(2,128)S(1)} %add.55), channel_id=1, source_target_pairs={{0,6},{1,7},{2,4},{3,5},{4,2},{5,3},{6,0},{7,1},{8,14},{9,15},{10,... | collective-permute-start | bytes 6152 | tf_op jit(solution)/shard_map/ppermute | solution.py:303
  69.9 1.2 %collective-permute-done.7 = f32[2,128,2]{1,2,0:T(2,128)S(1)} collective-permute-done((f32[2,128,2]{1,2,0:T(2,128)S(1)}, f32[2,128,2]{1,2,0:T(2,128)S(1)}, u32[]{:S(2)}, u32[]{:S(2)}) %collective-permute-start.7) | collective-permute-done | bytes 2080 | tf_op jit(solution)/shard_map/ppermute | solution.py:303
  71.1 1.6 %collective-permute-done.8 = f32[2,128,2]{1,2,0:T(2,128)S(1)} collective-permute-done((f32[2,128,2]{1,2,0:T(2,128)S(1)}, f32[2,128,2]{1,2,0:T(2,128)S(1)}, u32[]{:S(2)}, u32[]{:S(2)}) %collective-permute-start.8) | collective-permute-done | bytes 2080 | tf_op jit(solution)/shard_map/ppermute | solution.py:303
  73.4 0.9 %collective-permute-start.9 = (bf16[1,2,7808]{2,1,0:T(2,128)(2,1)S(1)}, bf16[1,2,7808]{2,1,0:T(2,128)(2,1)S(1)}, u32[]{:S(2)}, u32[]{:S(2)}) collective-permute-start(bf16[1,2,7808]{2,1,0:T(2,128)(2,1)S(1)} %slice.43), channel_id=1, source_target_pairs={{0,16},{8,24},{16,0},{24,8},{1,17},{9,25},{17,1},{25,9},{2,18},{10... | collective-permute-start | bytes 93704 | tf_op jit(solution)/shard_map/ppermute | solution.py:303
  74.3 3.0 %collective-permute-done.9 = bf16[1,2,7808]{2,1,0:T(2,128)(2,1)S(1)} collective-permute-done((bf16[1,2,7808]{2,1,0:T(2,128)(2,1)S(1)}, bf16[1,2,7808]{2,1,0:T(2,128)(2,1)S(1)}, u32[]{:S(2)}, u32[]{:S(2)}) %collective-permute-start.9) | collective-permute-done | bytes 31264 | tf_op jit(solution)/shard_map/ppermute | solution.py:303
  77.4 0.7 fusion.10
  (48 shorter events, 4.5 us)
Async XLA Ops:
  2.3 5.5 %collective-permute-start = (bf16[1,2,7808]{2,1,0:T(2,128)(2,1)S(1)}, bf16[1,2,7808]{2,1,0:T(2,128)(2,1)S(1)}, u32[]{:S(2)}, u32[]{:S(2)}) collective-permute-start(bf16[1,2,7808]{2,1,0:T(2,128)(2,1)S(1)} %get-tuple-element.36), channel_id=1, source_target_pairs={{0,8},{8,0},{16,24},{24,16},{1,9},{9,1},{17,25},{25,17},{2,10},{10... | collective-permute-start | bytes 93704 | tf_op jit(solution)/shard_map/ppermute | solution.py:303
  2.8 5.0 %collective-permute-start.1 = (bf16[1,2,7808]{2,1,0:T(2,128)(2,1)S(1)}, bf16[1,2,7808]{2,1,0:T(2,128)(2,1)S(1)}, u32[]{:S(2)}, u32[]{:S(2)}) collective-permute-start(bf16[1,2,7808]{2,1,0:T(2,128)(2,1)S(1)} %get-tuple-element.35), channel_id=1, source_target_pairs={{0,16},{8,24},{16,0},{24,8},{1,17},{9,25},{17,1},{25,9},{2,18},{10... | collective-permute-start | bytes 93704 | tf_op jit(solution)/shard_map/ppermute | solution.py:303
  5.4 3.3 %collective-permute-start.2 = (bf16[1,2,7808]{2,1,0:T(2,128)(2,1)S(1)}, bf16[1,2,7808]{2,1,0:T(2,128)(2,1)S(1)}, u32[]{:S(2)}, u32[]{:S(2)}) collective-permute-start(bf16[1,2,7808]{2,1,0:T(2,128)(2,1)S(1)} %get-tuple-element.34), channel_id=1, source_target_pairs={{0,24},{8,16},{16,8},{24,0},{1,25},{9,17},{17,9},{25,1},{2,26},{10... | collective-permute-start | bytes 93704 | tf_op jit(solution)/shard_map/ppermute | solution.py:303
  5.5 0.8 copy-start.5
  6.2 0.8 copy-start.7
  7.0 0.8 copy-start.8
  8.7 3.3 %copy-start.2 = (bf16[64,2,7808]{2,1,0:T(2,128)(2,1)S(1)}, bf16[64,2,7808]{2,1,0:T(2,128)(2,1)}, u32[]{:S(2)}) copy-start(bf16[64,2,7808]{2,1,0:T(2,128)(2,1)} %mine_ref) | copy-start | bytes 5996548
  12.0 28.1 %collective-permute-start.3 = (bf16[64,2,7808]{2,1,0:T(2,128)(2,1)S(1)}, bf16[64,2,7808]{2,1,0:T(2,128)(2,1)}, u32[]{:S(2)}, u32[]{:S(2)}) collective-permute-start(bf16[64,2,7808]{2,1,0:T(2,128)(2,1)S(1)} %copy-done.2), channel_id=1, source_target_pairs={{0,8},{8,0},{16,24},{24,16},{1,9},{9,1},{17,25},{25,17},{2,10},{10... | collective-permute-start | bytes 5996552 | tf_op jit(solution)/shard_map/ppermute | solution.py:303
  12.2 22.2 %all-to-all-start = ((bf16[8,144,256]{2,1,0:T(8,128)(2,1)}), bf16[8,144,256]{2,1,0:T(8,128)(2,1)S(1)}, u32[]{:S(2)}, u32[]{:S(2)}) async-start(bf16[8,144,256]{2,1,0:T(8,128)(2,1)} %shard_map.141), calls=%async_computation | async-start | bytes 1179648 | tf_op jit(solution)/shard_map/all_to_all | solution.py:373
  21.3 13.0 %copy-start.13 = (bf16[160,128]{1,0:T(8,128)(2,1)S(1)}, bf16[160,128]{1,0:T(8,128)(2,1)}, u32[]{:S(2)}) copy-start(bf16[160,128]{1,0:T(8,128)(2,1)} %constant.53.clone.up_x_ref) | copy-start | bytes 122884
  24.3 10.8 %copy-start.9 = (bf16[2,128,256]{2,1,0:T(8,128)(2,1)S(1)}, bf16[2,128,256]{2,1,0:T(8,128)(2,1)}, u32[]{:S(2)}) copy-start(bf16[2,128,256]{2,1,0:T(8,128)(2,1)} %constant.55.clone.up_z_ref) | copy-start | bytes 393220
  24.4 10.8 %copy-start.10 = (bf16[512,128]{1,0:T(8,128)(2,1)S(1)}, bf16[512,128]{1,0:T(8,128)(2,1)}, u32[]{:S(2)}) copy-start(bf16[512,128]{1,0:T(8,128)(2,1)} %constant.56.clone.down_z_ref) | copy-start | bytes 393220
  24.4 10.8 %copy-start.11 = (bf16[128,160]{1,0:T(8,128)(2,1)S(1)}, bf16[128,160]{1,0:T(8,128)(2,1)}, u32[]{:S(2)}) copy-start(bf16[128,160]{1,0:T(8,128)(2,1)} %constant.54.clone.down_x_ref) | copy-start | bytes 122884
  34.4 1.4 %copy-start.3 = (bf16[20,160,256]{2,1,0:T(8,128)(2,1)S(1)}, bf16[20,160,256]{2,1,0:T(8,128)(2,1)}, u32[]{:S(2)}) copy-start(bf16[20,160,256]{2,1,0:T(8,128)(2,1)} %pad.7.pot_ref) | copy-start | bytes 4915204
  34.4 1.9 %copy-start.4 = (bf16[20,160,256]{2,1,0:T(8,128)(2,1)S(1)}, bf16[20,160,256]{2,1,0:T(8,128)(2,1)}, u32[]{:S(2)}) copy-start(bf16[20,160,256]{2,1,0:T(8,128)(2,1)} %pad.8.con_ref) | copy-start | bytes 4915204
  36.3 7.4 %copy-start.14 = (f32[256]{0:T(256)S(1)}, f32[256]{0:T(256)}, u32[]{:S(2)}) copy-start(f32[256]{0:T(256)} %param.15) | copy-start | bytes 3076
  40.1 13.4 %all-to-all-start.1 = ((bf16[8,144,128]{2,1,0:T(8,128)(2,1)}), bf16[8,144,128]{2,1,0:T(8,128)(2,1)S(1)}, u32[]{:S(2)}, u32[]{:S(2)}) async-start(bf16[8,144,128]{2,1,0:T(8,128)(2,1)} %shard_map.143), calls=%async_computation.1 | async-start | bytes 589824 | tf_op jit(solution)/shard_map/all_to_all | solution.py:409
  45.1 8.4 %copy-start.6 = (bf16[1,2,7808]{2,1,0:T(2,128)(2,1)S(1)}, bf16[1,2,7808]{2,1,0:T(2,128)(2,1)}, u32[]{:S(2)}) copy-start(bf16[1,2,7808]{2,1,0:T(2,128)(2,1)} %resp_ref.3) | copy-start | bytes 93700
  45.1 8.4 %copy-start.12 = (bf16[112,160]{1,0:T(8,128)(2,1)S(1)}, bf16[112,160]{1,0:T(8,128)(2,1)}, u32[]{:S(2)}) copy-start(bf16[112,160]{1,0:T(8,128)(2,1)} %constant.52.clone.down_y_ref) | copy-start | bytes 107524
  47.0 1.9 %copy-start = (bf16[128,2,7808]{2,1,0:T(2,128)(2,1)}, bf16[128,2,7808]{2,1,0:T(2,128)(2,1)S(1)}, u32[]{:S(2)}) copy-start(bf16[128,2,7808]{2,1,0:T(2,128)(2,1)S(1)} %shard_map.144) | copy-start | bytes 11993092
  53.5 7.2 %copy-start.1 = (bf16[128,2,7808]{2,1,0:T(2,128)(2,1)S(1)}, bf16[128,2,7808]{2,1,0:T(2,128)(2,1)}, u32[]{:S(2)}) copy-start(bf16[128,2,7808]{2,1,0:T(2,128)(2,1)} %copy-done) | copy-start | bytes 11993092
  56.2 4.0 %collective-permute-start.4 = (bf16[1,2,7808]{2,1,0:T(2,128)(2,1)S(1)}, bf16[1,2,7808]{2,1,0:T(2,128)(2,1)S(1)}, u32[]{:S(2)}, u32[]{:S(2)}) collective-permute-start(bf16[1,2,7808]{2,1,0:T(2,128)(2,1)S(1)} %get-tuple-element.32), channel_id=1, source_target_pairs={{0,16},{8,24},{16,0},{24,8},{1,17},{9,25},{17,1},{25,9},{2,18},{10... | collective-permute-start | bytes 93704 | tf_op jit(solution)/shard_map/ppermute | solution.py:303
  61.9 3.6 %collective-permute-start.5 = (f32[2,128,2]{1,2,0:T(2,128)S(1)}, f32[2,128,2]{1,2,0:T(2,128)S(1)}, u32[]{:S(2)}, u32[]{:S(2)}) collective-permute-start(f32[2,128,2]{1,2,0:T(2,128)S(1)} %fusion.5), channel_id=1, source_target_pairs={{0,1},{1,0},{2,3},{3,2},{4,5},{5,4},{6,7},{7,6},{8,9},{9,8},{10,11... | collective-permute-start | bytes 6152 | tf_op jit(solution)/shard_map/ppermute | solution.py:303
  65.5 4.4 %collective-permute-start.6 = (f32[2,128,2]{1,2,0:T(2,128)S(1)}, f32[2,128,2]{1,2,0:T(2,128)S(1)}, u32[]{:S(2)}, u32[]{:S(2)}) collective-permute-start(f32[2,128,2]{1,2,0:T(2,128)S(1)} %add.55), channel_id=1, source_target_pairs={{0,2},{1,3},{2,0},{3,1},{4,6},{5,7},{6,4},{7,5},{8,10},{9,11},{10,... | collective-permute-start | bytes 6152 | tf_op jit(solution)/shard_map/ppermute | solution.py:303
  66.6 4.5 %collective-permute-start.7 = (f32[2,128,2]{1,2,0:T(2,128)S(1)}, f32[2,128,2]{1,2,0:T(2,128)S(1)}, u32[]{:S(2)}, u32[]{:S(2)}) collective-permute-start(f32[2,128,2]{1,2,0:T(2,128)S(1)} %add.55), channel_id=1, source_target_pairs={{0,4},{1,5},{2,6},{3,7},{4,0},{5,1},{6,2},{7,3},{8,12},{9,13},{10,... | collective-permute-start | bytes 6152 | tf_op jit(solution)/shard_map/ppermute | solution.py:303
  67.3 5.4 %collective-permute-start.8 = (f32[2,128,2]{1,2,0:T(2,128)S(1)}, f32[2,128,2]{1,2,0:T(2,128)S(1)}, u32[]{:S(2)}, u32[]{:S(2)}) collective-permute-start(f32[2,128,2]{1,2,0:T(2,128)S(1)} %add.55), channel_id=1, source_target_pairs={{0,6},{1,7},{2,4},{3,5},{4,2},{5,3},{6,0},{7,1},{8,14},{9,15},{10,... | collective-permute-start | bytes 6152 | tf_op jit(solution)/shard_map/ppermute | solution.py:303
  73.4 4.0 %collective-permute-start.9 = (bf16[1,2,7808]{2,1,0:T(2,128)(2,1)S(1)}, bf16[1,2,7808]{2,1,0:T(2,128)(2,1)S(1)}, u32[]{:S(2)}, u32[]{:S(2)}) collective-permute-start(bf16[1,2,7808]{2,1,0:T(2,128)(2,1)S(1)} %slice.43), channel_id=1, source_target_pairs={{0,16},{8,24},{16,0},{24,8},{1,17},{9,25},{17,1},{25,9},{2,18},{10... | collective-permute-start | bytes 93704 | tf_op jit(solution)/shard_map/ppermute | solution.py:303

commit v4 on v3

--- a/solution.py
+++ b/solution.py
@@ -27,11 +27,12 @@
         folded = np.arange(grid)
         folded = np.where(folded >= grid // 2, folded - grid, folded)
         flat = np.sort((folded[:, None] ** 2 + folded[None, :] ** 2).ravel())
-        used, half = set(), 0
+        used, half, limits = set(), 0, []
         for block in range(blocks):
             planes = folded[block + blocks * np.arange(self.slab)] ** 2
             radii = np.sort((planes[:, None] + flat[None, :]).ravel())
             limit = int(radii[count - 1])
+            limits.append(limit)
             used |= set(np.nonzero(planes <= limit)[0].tolist())
             half = max(half, math.isqrt(limit - int(planes.min())))
         self.low = 0
@@ -45,7 +46,21 @@
         self.width = min(2 * self.half + 1, grid)
         self.ypad = up(self.width, 8)
         self.zpad = 64 if self.width <= 64 else up(self.width, 128)
-        self.rows = up(self.slots * self.slab, 16)
+        reach = []
+        for x in self.planes:
+            held = [
+                math.isqrt(limit - int(folded[block + blocks * x]) ** 2)
+                for block, limit in enumerate(limits)
+                if int(folded[block + blocks * x]) ** 2 <= limit
+            ]
+            reach.append(max(held, default=0))
+        narrow = int(np.argmin(reach))
+        fits = self.slots > 1 and 2 * reach[narrow] + 1 <= self.zpad - self.width
+        self.order = [s for s in range(self.slots) if s != narrow] + [narrow]
+        self.narrow, self.reach = (narrow if fits else None), reach[narrow]
+        self.turn = self.width - self.half + self.reach
+        self.sent = self.slots - 1 if fits else self.slots
+        self.rows = up(self.sent * self.slab, 16)
         self.spad = self.slots
         while self.spad * self.slab % 8 or self.spad * self.slab < self.rows:
             self.spad += 1
@@ -65,7 +80,6 @@
             return np.pad(part, ((0, rows - part.shape[0]), (0, columns - part.shape[1])))
 
         cos_y, sin_y = self.waves(every, boxed)
-        up_y = np.concatenate([padded(cos_y, grid, ypad), padded(sin_y, grid, ypad)], 1)
         down_y = np.concatenate([padded(cos_y.T, ypad, grid), padded(-sin_y.T, ypad, grid)], 0)
         cos_z, sin_z = padded(cos_y, grid, zpad), padded(sin_y, grid, zpad)
         cos_z, sin_z = (padded(part, up(grid, 128), zpad) for part in (cos_z, sin_z))
@@ -73,7 +87,7 @@
         down_z = np.concatenate(
             [np.concatenate([cos_z, -sin_z], 1), np.concatenate([sin_z, cos_z], 1)], 0
         )
-        planes = np.array([p + self.blocks * x for p in range(self.blocks) for x in self.planes])
+        planes = np.array([p + self.blocks * x for p in range(self.blocks) for x in (self.planes[s] for s in self.order)])
         cos_x, sin_x = self.waves(every, planes)
 
         def slotted(part):
@@ -84,7 +98,7 @@
         cos_x, sin_x = slotted(cos_x), slotted(sin_x)
         up_x = np.concatenate([cos_x, sin_x], 1)
         down_x = np.concatenate([cos_x.T, -sin_x.T], 0)
-        return [jnp.asarray(t, BF16) for t in (up_y, down_y, up_x, down_x, up_z, down_z)]
+        return [jnp.asarray(t, BF16) for t in (down_y, up_x, down_x, up_z, down_z)]
 
 
 def quarter(field, zpad):
@@ -97,6 +111,19 @@
             pieces.append(jnp.where(lane < zpad, -turned, turned))
         else:
             pieces += [-piece[:, zpad:], piece[:, :zpad]]
+    return pieces[0] if len(pieces) == 1 else jnp.concatenate(pieces, 1)
+
+
+def moved(box, field, back):
+    pieces, span = [], 2 * box.zpad
+    least = box.half - box.reach if back else box.width
+    for start in range(0, field.shape[1], span):
+        piece = field[:, start : start + span]
+        turned = pltpu.roll(piece, span - box.turn if back else box.turn, 1)
+        lane = lax.broadcasted_iota(I32, piece.shape, 1)
+        lane = jnp.where(lane >= box.zpad, lane - box.zpad, lane)
+        inside = (lane >= least) & (lane <= least + 2 * box.reach)
+        pieces.append(jnp.where(inside, turned, 0.0))
     return pieces[0] if len(pieces) == 1 else jnp.concatenate(pieces, 1)
 
 
@@ -130,13 +157,19 @@
         ]
         piece = dot(chosen, jnp.concatenate(values, 0), ((1,), (1,)))
         total = piece if total is None else total + piece
-    for s in range(box.slots):
+    added = None
+    for n, s in reversed(list(enumerate(box.order))):
         plane = total[s * ypad : (s + 1) * ypad]
         both = jnp.concatenate([plane, quarter(plane, zpad)], 0).astype(BF16)
         lines = dot(up_y_ref[...], both)
+        if n == box.sent:
+            added = moved(box, lines, False)
+            continue
+        if n == 0 and added is not None:
+            lines = lines + added
         for q in range(box.blocks):
-            space_ref[q, s * slab : (s + 1) * slab, :] = lines[q * slab : (q + 1) * slab]
-    used = box.slots * slab
+            space_ref[q, n * slab : (n + 1) * slab, :] = lines[q * slab : (q + 1) * slab]
+    used = box.sent * slab
     for q in range(box.blocks):
         if used < box.rows:
             space_ref[q, used:, :] = jnp.zeros((box.rows - used, space_ref.shape[2]), F32)
@@ -148,7 +181,7 @@
     return folded * folded
 
 
-def index_kernel(box, map_ref, resp_ref, table_ref, row_ref, z_ref, kinetic_ref, resp_out, table_out):
+def index_kernel(box, map_ref, resp_ref, row_ref, z_ref, kinetic_ref, resp_out, table_ref):
     grid, cell = box.grid, map_ref[...][None, :].astype(F32)
     local_x = jnp.floor((cell + 0.5) * (1.0 / (grid * grid)))
     cell = cell - local_x * (grid * grid)
@@ -166,7 +199,15 @@
     row_ref[...] = (slot * box.ypad + boxed(grid_y)).astype(I32)
     z_ref[...] = boxed(grid_z).astype(I32)
     resp_out[...] = resp_ref[...]
-    table_out[...] = table_ref[...]
+    line = lax.broadcasted_iota(I32, table_ref.shape, 0).astype(F32)
+    column = lax.broadcasted_iota(I32, table_ref.shape, 1)
+    sine = column >= box.ypad
+    column = jnp.where(sine, column - box.ypad, column)
+    products = line * (column - box.half).astype(F32)
+    products = products - jnp.floor((products + 0.5) * (1.0 / grid)) * grid
+    products = jnp.where(sine, products - grid / 4, products)
+    waves = jnp.cos(products * (2.0 * math.pi / grid)) * (1.0 / math.sqrt(grid))
+    table_ref[...] = jnp.where(column < box.width, waves, 0.0).astype(BF16)
 
 
 def spread_rows(box, in_ref, from_ref):
@@ -180,6 +221,12 @@
                 from_ref[t, p * stride + box.rows : (p + 1) * stride, :] = jnp.zeros(
                     (stride - box.rows, 128), F32
                 )
+        if box.narrow is None:
+            continue
+        first = p * stride + box.sent * box.slab
+        neighbour = moved(box, in_ref[p].astype(F32)[: box.slab], True)
+        for t in range(from_ref.shape[0]):
+            from_ref[t, first : first + box.slab, :] = neighbour[:, t * 128 : (t + 1) * 128]
 
 
 def along_x(box, from_ref, field, up_x_ref, wide_ref):
@@ -235,6 +282,12 @@
             column = (line * tiles + t) * 128
             to_ref[t, pl.ds(line, planes, stride=box.slab), :] = lined[:, column : column + 128]
     for p in range(box.blocks):
+        if box.narrow is not None:
+            first, last = p * stride, p * stride + box.sent * box.slab
+            added = [to_ref[t, last : last + box.slab, :] for t in range(tiles)]
+            added = moved(box, jnp.concatenate(added, 1), False)
+            for t in range(tiles):
+                to_ref[t, first : first + box.slab, :] += added[:, t * 128 : (t + 1) * 128]
         for t in range(tiles):
             out_ref[p, :, t * 128 : (t + 1) * 128] = to_ref[
                 t, p * stride : p * stride + box.rows, :
@@ -261,10 +314,13 @@
         space_ref[q] = in_ref[q].astype(F32)
     fields = []
     for s in range(box.slots):
+        n = 0 if s == box.narrow else box.order.index(s)
         plane = jnp.concatenate(
-            [space_ref[q, s * slab : (s + 1) * slab, :] for q in range(box.blocks)], 0
-        ).astype(BF16)
-        parts = dot(down_y_ref[...], plane)
+            [space_ref[q, n * slab : (n + 1) * slab, :] for q in range(box.blocks)], 0
+        )
+        if s == box.narrow:
+            plane = moved(box, plane, True)
+        parts = dot(down_y_ref[...], plane.astype(BF16))
         fields.append(parts[:ypad] + quarter(parts[ypad:], zpad))
     field = jnp.concatenate(fields, 0).T.astype(BF16)
     for start, size in chunks(box.count, 1024):
@@ -321,7 +377,7 @@
     grid = potential.shape[0]
     bands, blocks = sizes
     box = Box(grid, blocks, count)
-    up_y, down_y, up_x, down_x, up_z, down_z = box.tables()
+    down_y, up_x, down_x, up_z, down_z = box.tables()
     band_me = lax.axis_index("band")
     first_row = offset[0]
 
@@ -342,10 +398,10 @@
             index_shape,
             jax.ShapeDtypeStruct((1, count), F32),
             jax.ShapeDtypeStruct(response.shape, BF16),
-            jax.ShapeDtypeStruct(up_y.shape, BF16),
+            jax.ShapeDtypeStruct((grid, 2 * box.ypad), BF16),
         ),
         [],
-        (grid_map, response, up_y),
+        (grid_map, response),
         1 << 20,
         16,
     )

time: 78.7 us -> 76.6 us (0.973)
  waiting for transfers between devices: 26.4 us -> 24.9 us
  local copies, waits for them, and re-layouts: 10 us -> 9.04 us
    all_to_all x1, waiting for transfers between devices: 10 us -> 8.61 us  [on_device(): field = lax.all_to_all(field, 'pw', split_axis=0, concat_axis=0, tiled=True)]
    unnamed x31 -> x29, local copies, waits for them, and re-layouts: 5.4 us -> 4.39 us
  transfers between devices with their start and end apart: 12 -> 12, of which waited for: 8 -> 8; matrix products, arithmetic and copies ran while one was open for 10% -> 10% of each run, Pallas kernels for 8% -> 9%
where the time goes in v4:
time: 76.6 us; the launch traced here: 76.1 us
  waiting for transfers between devices  24.9 us (33%)
  starting transfers between devices  20.4 us (27%)
  Pallas kernels  13.1 us (17%)
  local copies, waits for them, and re-layouts  9.04 us (12%)
  other arithmetic  5.28 us (7%)
  matrix products  1.9 us (2%)
  between operations  1.48 us (2%)
    ppermute x10, waiting for transfers between devices, xor_permute(): lax.ppermute(value, axis, [(source, source ^ distance) for source in rang...  12.3 us
    pallas_call x5, Pallas kernels, call(): pl.pallas_call(kernel, out_shape=out_shape, in_specs=[pl.BlockSpec(memory...  11.2 us
    ppermute x10, starting transfers between devices, xor_permute(): lax.ppermute(value, axis, [(source, source ^ distance) for source in rang...  11 us
    all_to_all x1, waiting for transfers between devices, on_device(): field = lax.all_to_all(field, 'pw', split_axis=0, concat_axis=0, tiled=True)  8.61 us
    all_to_all x1, starting transfers between devices, on_device(): field = lax.all_to_all(field, 'pw', split_axis=0, concat_axis=0, tiled=True)  5.81 us
    unnamed x29, local copies, waits for them, and re-layouts  4.39 us
    all_to_all x1, waiting for transfers between devices, on_device(): lax.all_to_all(returned, 'pw', split_axis=0, concat_axis=0, tiled=True)  3.95 us
    all_to_all x1, starting transfers between devices, on_device(): lax.all_to_all(returned, 'pw', split_axis=0, concat_axis=0, tiled=True)  3.64 us
  transfers between devices with their start and end apart: 12, of which 8 were waited for; matrix products, arithmetic and copies ran while one was open for 10% of the time, Pallas kernels for 9%

profile of v4, /device:TPU:0, one launch (start us, length us, event | category | flops | bytes accessed | tf_op | source)
XLA Modules:
  0.0 76.1 jit_solution(6492330340647253415)
XLA Ops:
  1.3 1.0 %constant_dynamic-slice_fusion = (bf16[1,2,7808]{2,1,0:T(2,128)(2,1)S(1)}, bf16[1,2,7808]{2,1,0:T(2,128)(2,1)S(1)}, bf16[1,2,7808]{2,1,0:T(2,128)(2,1)S(1)}, bf16[1,2,7808]{2,1,0:T(2,128)(2,1)S(1)}) fusion(bf16[64,2,7808]{2,1,0:T(2,128)(2,1)} %mine_ref, s32[]{:T(128)S(6)} %min.16, s32[]{:T(128)S(6)} %min.15, s32[]{:T(128)S(6)} %min.14, s32[]{:T(128)S(6)} %min.13), kind=kLoop, calls=%fused_computation.27 | loop fusion | bytes 249872 | tf_op jit(solution)/shard_map/dynamic_slice | solution.py:388
  2.7 2.7 %collective-permute-start.1 = (bf16[1,2,7808]{2,1,0:T(2,128)(2,1)S(1)}, bf16[1,2,7808]{2,1,0:T(2,128)(2,1)S(1)}, u32[]{:S(2)}, u32[]{:S(2)}) collective-permute-start(bf16[1,2,7808]{2,1,0:T(2,128)(2,1)S(1)} %get-tuple-element.35), channel_id=1, source_target_pairs={{0,16},{8,24},{16,0},{24,8},{1,17},{9,25},{17,1},{25,9},{2,18},{10... | collective-permute-start | bytes 93704 | tf_op jit(solution)/shard_map/ppermute | solution.py:359
  5.5 0.8 copy-done.5
  6.2 0.8 copy-done.7
  7.4 1.4 %collective-permute-done.2.refs_3_ = bf16[1,2,7808]{2,1,0:T(2,128)(2,1)S(1)} collective-permute-done((bf16[1,2,7808]{2,1,0:T(2,128)(2,1)S(1)}, bf16[1,2,7808]{2,1,0:T(2,128)(2,1)S(1)}, u32[]{:S(2)}, u32[]{:S(2)}) %collective-permute-start.2) | collective-permute-done | bytes 31264 | tf_op jit(solution)/shard_map/ppermute | solution.py:359
  8.7 3.3 %shard_map.132 = bf16[8,128,256]{2,1,0:T(8,128)(2,1)} custom-call(s32[1]{0:T(128)} %bitcast.1.choice_ref, s32[1,7808]{1,0:T(1,128)S(1)} %get-tuple-element.18.row_ref, s32[1,7808]{1,0:T(1,128)S(1)} %get-tuple-element.19.z_ref, bf16[1,2,7808]{2,1,0:T(2,128)(2,1)S(1)} %get-tuple-element.20.resp_ref, bf16[1,2,7808]{2,1,0:T(2,128)(2,1)S(1)} %get-tuple-element.37.refs_0_, ...), custom_call_target="tpu_custom_call" | custom-call | flops 4294967296 | bytes 4194304 | tf_op jit(solution)/shard_map/pallas_call | solution.py:348
  12.2 5.8 %all-to-all-start = ((bf16[8,128,256]{2,1,0:T(8,128)(2,1)}), bf16[8,128,256]{2,1,0:T(8,128)(2,1)S(1)}, u32[]{:S(2)}, u32[]{:S(2)}) async-start(bf16[8,128,256]{2,1,0:T(8,128)(2,1)} %shard_map.132), calls=%async_computation | async-start | bytes 1048576 | tf_op jit(solution)/shard_map/all_to_all | solution.py:429
  18.0 3.4 %convert_bitcast_fusion = (bf16[20,160,160]{2,1,0:T(8,128)(2,1)S(1)}, bf16[20,160,160]{2,1,0:T(8,128)(2,1)S(1)}) fusion(f32[160,20,160]{2,0,1:T(8,128)} %param.18, f32[160,20,160]{2,0,1:T(8,128)} %param.17), kind=kLoop, calls=%fused_computation.6 | loop fusion | flops 1024000 | bytes 6144000 | tf_op jit(solution)/shard_map/convert_element_type | solution.py:423
  21.4 1.5 %pad.7.pot_ref = bf16[20,160,256]{2,1,0:T(8,128)(2,1)} pad(bf16[20,160,160]{2,1,0:T(8,128)(2,1)S(1)} %get-tuple-element.50, bf16[]{:T(256)} %constant.46.clone.1), padding=0_0x0_0x0_96 | pad | bytes 2662402 | tf_op jit(solution)/shard_map/jit(_pad)/pad | solution.py:423
  22.9 1.5 %pad.8.con_ref = bf16[20,160,256]{2,1,0:T(8,128)(2,1)} pad(bf16[20,160,160]{2,1,0:T(8,128)(2,1)S(1)} %get-tuple-element.49, bf16[]{:T(256)} %constant.46.clone.1), padding=0_0x0_0x0_96 | pad | bytes 2662402 | tf_op jit(solution)/shard_map/jit(_pad)/pad | solution.py:423
  24.4 8.6 %all-to-all-done.in_ref = bf16[8,128,256]{2,1,0:T(8,128)(2,1)S(1)} async-done(((bf16[8,128,256]{2,1,0:T(8,128)(2,1)}), bf16[8,128,256]{2,1,0:T(8,128)(2,1)S(1)}, u32[]{:S(2)}, u32[]{:S(2)}) %all-to-all-start) | async-done | bytes 524320 | tf_op jit(solution)/shard_map/all_to_all | solution.py:429
  33.0 0.9 %shard_map.133.wide_ref = bf16[2,20,160,128]{3,2,1,0:T(8,128)(2,1)S(1)} custom-call(bf16[8,128,256]{2,1,0:T(8,128)(2,1)S(1)} %all-to-all-done.in_ref, bf16[160,128]{1,0:T(8,128)(2,1)S(1)} %copy-done.12), custom_call_target="tpu_custom_call" | custom-call | flops 2147483648 | bytes 4194304 | tf_op jit(solution)/shard_map/pallas_call | solution.py:348
  34.9 3.9 %shard_map.134 = bf16[8,128,128]{2,1,0:T(8,128)(2,1)} custom-call(bf16[2,20,160,128]{3,2,1,0:T(8,128)(2,1)S(1)} %shard_map.133.wide_ref, bf16[20,160,256]{2,1,0:T(8,128)(2,1)S(1)} %copy-done.3, bf16[20,160,256]{2,1,0:T(8,128)(2,1)S(1)} %copy-done.4, bf16[128,160]{1,0:T(8,128)(2,1)S(1)} %copy-done.10, bf16[2,128,256]{2,1,0:T(8,128)(2,1)S(1)} %copy-done.8, ...), custom_call_target="tpu_custom_call" | custom-call | flops 4294967296 | bytes 4194304 | tf_op jit(solution)/shard_map/pallas_call | solution.py:348
  38.8 3.6 %all-to-all-start.1 = ((bf16[8,128,128]{2,1,0:T(8,128)(2,1)}), bf16[8,128,128]{2,1,0:T(8,128)(2,1)S(1)}, u32[]{:S(2)}, u32[]{:S(2)}) async-start(bf16[8,128,128]{2,1,0:T(8,128)(2,1)} %shard_map.134), calls=%async_computation.1 | async-start | bytes 524288 | tf_op jit(solution)/shard_map/all_to_all | solution.py:465
  43.0 0.7 add_reduce_fusion
  43.8 1.9 %shard_map.135 = bf16[128,2,7808]{2,1,0:T(2,128)(2,1)S(1)} custom-call(bf16[64,2,7808]{2,1,0:T(2,128)(2,1)S(1)} %copy-done.2, bf16[64,2,7808]{2,1,0:T(2,128)(2,1)} %collective-permute-done.3.other_ref), custom_call_target="tpu_custom_call" | custom-call | bytes 8388608 | tf_op jit(solution)/shard_map/pallas_call | solution.py:456
  45.7 1.9 %copy-done = bf16[128,2,7808]{2,1,0:T(2,128)(2,1)} copy-done((bf16[128,2,7808]{2,1,0:T(2,128)(2,1)}, bf16[128,2,7808]{2,1,0:T(2,128)(2,1)S(1)}, u32[]{:S(2)}) %copy-start) | copy-done | bytes 3997720
  47.6 3.9 %all-to-all-done.1.in_ref = bf16[8,128,128]{2,1,0:T(8,128)(2,1)S(1)} async-done(((bf16[8,128,128]{2,1,0:T(8,128)(2,1)}), bf16[8,128,128]{2,1,0:T(8,128)(2,1)S(1)}, u32[]{:S(2)}, u32[]{:S(2)}) %all-to-all-start.1) | async-done | bytes 262176 | tf_op jit(solution)/shard_map/all_to_all | solution.py:465
  51.5 2.7 %shard_map.136 = (bf16[1,2,7808]{2,1,0:T(2,128)(2,1)S(1)}, f32[1,2,7808]{2,1,0:T(2,128)S(1)}) custom-call(bf16[8,128,128]{2,1,0:T(8,128)(2,1)S(1)} %all-to-all-done.1.in_ref, s32[1,7808]{1,0:T(1,128)S(1)} %get-tuple-element.18.row_ref, s32[1,7808]{1,0:T(1,128)S(1)} %get-tuple-element.19.z_ref, bf16[1,2,7808]{2,1,0:T(2,128)(2,1)S(1)} %copy-done.6, ...), custom_call_target="tpu_custom_call" | custom-call | flops 4294967296 | bytes 4194304 | tf_op jit(solution)/shard_map/pallas_call | solution.py:348
  54.3 0.9 %collective-permute-start.4 = (bf16[1,2,7808]{2,1,0:T(2,128)(2,1)S(1)}, bf16[1,2,7808]{2,1,0:T(2,128)(2,1)S(1)}, u32[]{:S(2)}, u32[]{:S(2)}) collective-permute-start(bf16[1,2,7808]{2,1,0:T(2,128)(2,1)S(1)} %get-tuple-element.32), channel_id=1, source_target_pairs={{0,16},{8,24},{16,0},{24,8},{1,17},{9,25},{17,1},{25,9},{2,18},{10... | collective-permute-start | bytes 93704 | tf_op jit(solution)/shard_map/ppermute | solution.py:359
  55.2 3.0 %collective-permute-done.4 = bf16[1,2,7808]{2,1,0:T(2,128)(2,1)S(1)} collective-permute-done((bf16[1,2,7808]{2,1,0:T(2,128)(2,1)S(1)}, bf16[1,2,7808]{2,1,0:T(2,128)(2,1)S(1)}, u32[]{:S(2)}, u32[]{:S(2)}) %collective-permute-start.4) | collective-permute-done | bytes 31264 | tf_op jit(solution)/shard_map/ppermute | solution.py:359
  58.7 1.2 %fusion.5 = f32[2,128,2]{1,2,0:T(2,128)S(1)} fusion(bf16[128,2,7808]{2,1,0:T(2,128)(2,1)S(1)} %copy-done.1, bf16[2,2,2,7808]{3,2,1,0:T(2,128)(2,1)S(1)} %pad_maximum_fusion), kind=kOutput, calls=%fused_computation.8 | convolution fusion | flops 15990784 | bytes 4124672 | tf_op jit(solution)/shard_map/mcj,dncj->dmn/dot_general | solution.py:485
  60.0 1.4 %collective-permute-start.5 = (f32[2,128,2]{1,2,0:T(2,128)S(1)}, f32[2,128,2]{1,2,0:T(2,128)S(1)}, u32[]{:S(2)}, u32[]{:S(2)}) collective-permute-start(f32[2,128,2]{1,2,0:T(2,128)S(1)} %fusion.5), channel_id=1, source_target_pairs={{0,1},{1,0},{2,3},{3,2},{4,5},{5,4},{6,7},{7,6},{8,9},{9,8},{10,11... | collective-permute-start | bytes 6152 | tf_op jit(solution)/shard_map/ppermute | solution.py:359
  61.4 2.2 %collective-permute-done.5 = f32[2,128,2]{1,2,0:T(2,128)S(1)} collective-permute-done((f32[2,128,2]{1,2,0:T(2,128)S(1)}, f32[2,128,2]{1,2,0:T(2,128)S(1)}, u32[]{:S(2)}, u32[]{:S(2)}) %collective-permute-start.5) | collective-permute-done | bytes 2080 | tf_op jit(solution)/shard_map/ppermute | solution.py:359
  63.6 1.1 %collective-permute-start.6 = (f32[2,128,2]{1,2,0:T(2,128)S(1)}, f32[2,128,2]{1,2,0:T(2,128)S(1)}, u32[]{:S(2)}, u32[]{:S(2)}) collective-permute-start(f32[2,128,2]{1,2,0:T(2,128)S(1)} %add.55), channel_id=1, source_target_pairs={{0,2},{1,3},{2,0},{3,1},{4,6},{5,7},{6,4},{7,5},{8,10},{9,11},{10,... | collective-permute-start | bytes 6152 | tf_op jit(solution)/shard_map/ppermute | solution.py:359
  65.3 2.7 %collective-permute-start.8 = (f32[2,128,2]{1,2,0:T(2,128)S(1)}, f32[2,128,2]{1,2,0:T(2,128)S(1)}, u32[]{:S(2)}, u32[]{:S(2)}) collective-permute-start(f32[2,128,2]{1,2,0:T(2,128)S(1)} %add.55), channel_id=1, source_target_pairs={{0,6},{1,7},{2,4},{3,5},{4,2},{5,3},{6,0},{7,1},{8,14},{9,15},{10,... | collective-permute-start | bytes 6152 | tf_op jit(solution)/shard_map/ppermute | solution.py:359
  68.0 1.2 %collective-permute-done.7 = f32[2,128,2]{1,2,0:T(2,128)S(1)} collective-permute-done((f32[2,128,2]{1,2,0:T(2,128)S(1)}, f32[2,128,2]{1,2,0:T(2,128)S(1)}, u32[]{:S(2)}, u32[]{:S(2)}) %collective-permute-start.7) | collective-permute-done | bytes 2080 | tf_op jit(solution)/shard_map/ppermute | solution.py:359
  69.1 1.5 %collective-permute-done.8 = f32[2,128,2]{1,2,0:T(2,128)S(1)} collective-permute-done((f32[2,128,2]{1,2,0:T(2,128)S(1)}, f32[2,128,2]{1,2,0:T(2,128)S(1)}, u32[]{:S(2)}, u32[]{:S(2)}) %collective-permute-start.8) | collective-permute-done | bytes 2080 | tf_op jit(solution)/shard_map/ppermute | solution.py:359
  70.7 0.6 convolution_bitcast_fusion
  71.4 0.9 %collective-permute-start.9 = (bf16[1,2,7808]{2,1,0:T(2,128)(2,1)S(1)}, bf16[1,2,7808]{2,1,0:T(2,128)(2,1)S(1)}, u32[]{:S(2)}, u32[]{:S(2)}) collective-permute-start(bf16[1,2,7808]{2,1,0:T(2,128)(2,1)S(1)} %slice.43), channel_id=1, source_target_pairs={{0,16},{8,24},{16,0},{24,8},{1,17},{9,25},{17,1},{25,9},{2,18},{10... | collective-permute-start | bytes 93704 | tf_op jit(solution)/shard_map/ppermute | solution.py:359
  72.3 3.1 %collective-permute-done.9 = bf16[1,2,7808]{2,1,0:T(2,128)(2,1)S(1)} collective-permute-done((bf16[1,2,7808]{2,1,0:T(2,128)(2,1)S(1)}, bf16[1,2,7808]{2,1,0:T(2,128)(2,1)S(1)}, u32[]{:S(2)}, u32[]{:S(2)}) %collective-permute-start.9) | collective-permute-done | bytes 31264 | tf_op jit(solution)/shard_map/ppermute | solution.py:359
  75.4 0.7 fusion.10
  (46 shorter events, 3.8 us)
Async XLA Ops:
  2.3 5.1 %collective-permute-start = (bf16[1,2,7808]{2,1,0:T(2,128)(2,1)S(1)}, bf16[1,2,7808]{2,1,0:T(2,128)(2,1)S(1)}, u32[]{:S(2)}, u32[]{:S(2)}) collective-permute-start(bf16[1,2,7808]{2,1,0:T(2,128)(2,1)S(1)} %get-tuple-element.36), channel_id=1, source_target_pairs={{0,8},{8,0},{16,24},{24,16},{1,9},{9,1},{17,25},{25,17},{2,10},{10... | collective-permute-start | bytes 93704 | tf_op jit(solution)/shard_map/ppermute | solution.py:359
  2.7 4.7 %collective-permute-start.1 = (bf16[1,2,7808]{2,1,0:T(2,128)(2,1)S(1)}, bf16[1,2,7808]{2,1,0:T(2,128)(2,1)S(1)}, u32[]{:S(2)}, u32[]{:S(2)}) collective-permute-start(bf16[1,2,7808]{2,1,0:T(2,128)(2,1)S(1)} %get-tuple-element.35), channel_id=1, source_target_pairs={{0,16},{8,24},{16,0},{24,8},{1,17},{9,25},{17,1},{25,9},{2,18},{10... | collective-permute-start | bytes 93704 | tf_op jit(solution)/shard_map/ppermute | solution.py:359
  5.4 3.3 %collective-permute-start.2 = (bf16[1,2,7808]{2,1,0:T(2,128)(2,1)S(1)}, bf16[1,2,7808]{2,1,0:T(2,128)(2,1)S(1)}, u32[]{:S(2)}, u32[]{:S(2)}) collective-permute-start(bf16[1,2,7808]{2,1,0:T(2,128)(2,1)S(1)} %get-tuple-element.34), channel_id=1, source_target_pairs={{0,24},{8,16},{16,8},{24,0},{1,25},{9,17},{17,9},{25,1},{2,26},{10... | collective-permute-start | bytes 93704 | tf_op jit(solution)/shard_map/ppermute | solution.py:359
  5.5 0.8 copy-start.5
  6.2 0.8 copy-start.7
  8.7 3.3 %copy-start.2 = (bf16[64,2,7808]{2,1,0:T(2,128)(2,1)S(1)}, bf16[64,2,7808]{2,1,0:T(2,128)(2,1)}, u32[]{:S(2)}) copy-start(bf16[64,2,7808]{2,1,0:T(2,128)(2,1)} %mine_ref) | copy-start | bytes 5996548
  12.0 26.8 %collective-permute-start.3 = (bf16[64,2,7808]{2,1,0:T(2,128)(2,1)S(1)}, bf16[64,2,7808]{2,1,0:T(2,128)(2,1)}, u32[]{:S(2)}, u32[]{:S(2)}) collective-permute-start(bf16[64,2,7808]{2,1,0:T(2,128)(2,1)S(1)} %copy-done.2), channel_id=1, source_target_pairs={{0,8},{8,0},{16,24},{24,16},{1,9},{9,1},{17,25},{25,17},{2,10},{10... | collective-permute-start | bytes 5996552 | tf_op jit(solution)/shard_map/ppermute | solution.py:359
  12.2 20.8 %all-to-all-start = ((bf16[8,128,256]{2,1,0:T(8,128)(2,1)}), bf16[8,128,256]{2,1,0:T(8,128)(2,1)S(1)}, u32[]{:S(2)}, u32[]{:S(2)}) async-start(bf16[8,128,256]{2,1,0:T(8,128)(2,1)} %shard_map.132), calls=%async_computation | async-start | bytes 1048576 | tf_op jit(solution)/shard_map/all_to_all | solution.py:429
  21.4 11.6 %copy-start.12 = (bf16[160,128]{1,0:T(8,128)(2,1)S(1)}, bf16[160,128]{1,0:T(8,128)(2,1)}, u32[]{:S(2)}) copy-start(bf16[160,128]{1,0:T(8,128)(2,1)} %constant.50.clone.up_x_ref) | copy-start | bytes 122884
  24.4 9.6 %copy-start.8 = (bf16[2,128,256]{2,1,0:T(8,128)(2,1)S(1)}, bf16[2,128,256]{2,1,0:T(8,128)(2,1)}, u32[]{:S(2)}) copy-start(bf16[2,128,256]{2,1,0:T(8,128)(2,1)} %constant.52.clone.up_z_ref) | copy-start | bytes 393220
  24.4 9.6 %copy-start.9 = (bf16[512,128]{1,0:T(8,128)(2,1)S(1)}, bf16[512,128]{1,0:T(8,128)(2,1)}, u32[]{:S(2)}) copy-start(bf16[512,128]{1,0:T(8,128)(2,1)} %constant.53.clone.down_z_ref) | copy-start | bytes 393220
  24.4 9.6 %copy-start.10 = (bf16[128,160]{1,0:T(8,128)(2,1)S(1)}, bf16[128,160]{1,0:T(8,128)(2,1)}, u32[]{:S(2)}) copy-start(bf16[128,160]{1,0:T(8,128)(2,1)} %constant.51.clone.down_x_ref) | copy-start | bytes 122884
  33.0 1.4 %copy-start.3 = (bf16[20,160,256]{2,1,0:T(8,128)(2,1)S(1)}, bf16[20,160,256]{2,1,0:T(8,128)(2,1)}, u32[]{:S(2)}) copy-start(bf16[20,160,256]{2,1,0:T(8,128)(2,1)} %pad.7.pot_ref) | copy-start | bytes 4915204
  33.0 1.9 %copy-start.4 = (bf16[20,160,256]{2,1,0:T(8,128)(2,1)S(1)}, bf16[20,160,256]{2,1,0:T(8,128)(2,1)}, u32[]{:S(2)}) copy-start(bf16[20,160,256]{2,1,0:T(8,128)(2,1)} %pad.8.con_ref) | copy-start | bytes 4915204
  34.9 7.5 %copy-start.13 = (f32[256]{0:T(256)S(1)}, f32[256]{0:T(256)}, u32[]{:S(2)}) copy-start(f32[256]{0:T(256)} %param.14) | copy-start | bytes 3076
  38.8 12.7 %all-to-all-start.1 = ((bf16[8,128,128]{2,1,0:T(8,128)(2,1)}), bf16[8,128,128]{2,1,0:T(8,128)(2,1)S(1)}, u32[]{:S(2)}, u32[]{:S(2)}) async-start(bf16[8,128,128]{2,1,0:T(8,128)(2,1)} %shard_map.134), calls=%async_computation.1 | async-start | bytes 524288 | tf_op jit(solution)/shard_map/all_to_all | solution.py:465
  43.8 7.8 %copy-start.6 = (bf16[1,2,7808]{2,1,0:T(2,128)(2,1)S(1)}, bf16[1,2,7808]{2,1,0:T(2,128)(2,1)}, u32[]{:S(2)}) copy-start(bf16[1,2,7808]{2,1,0:T(2,128)(2,1)} %resp_ref.3) | copy-start | bytes 93700
  43.8 7.8 %copy-start.11 = (bf16[112,160]{1,0:T(8,128)(2,1)S(1)}, bf16[112,160]{1,0:T(8,128)(2,1)}, u32[]{:S(2)}) copy-start(bf16[112,160]{1,0:T(8,128)(2,1)} %constant.49.clone.down_y_ref) | copy-start | bytes 107524
  45.7 1.9 %copy-start = (bf16[128,2,7808]{2,1,0:T(2,128)(2,1)}, bf16[128,2,7808]{2,1,0:T(2,128)(2,1)S(1)}, u32[]{:S(2)}) copy-start(bf16[128,2,7808]{2,1,0:T(2,128)(2,1)S(1)} %shard_map.135) | copy-start | bytes 11993092
  51.5 7.2 %copy-start.1 = (bf16[128,2,7808]{2,1,0:T(2,128)(2,1)S(1)}, bf16[128,2,7808]{2,1,0:T(2,128)(2,1)}, u32[]{:S(2)}) copy-start(bf16[128,2,7808]{2,1,0:T(2,128)(2,1)} %copy-done) | copy-start | bytes 11993092
  54.3 4.0 %collective-permute-start.4 = (bf16[1,2,7808]{2,1,0:T(2,128)(2,1)S(1)}, bf16[1,2,7808]{2,1,0:T(2,128)(2,1)S(1)}, u32[]{:S(2)}, u32[]{:S(2)}) collective-permute-start(bf16[1,2,7808]{2,1,0:T(2,128)(2,1)S(1)} %get-tuple-element.32), channel_id=1, source_target_pairs={{0,16},{8,24},{16,0},{24,8},{1,17},{9,25},{17,1},{25,9},{2,18},{10... | collective-permute-start | bytes 93704 | tf_op jit(solution)/shard_map/ppermute | solution.py:359
  60.0 3.6 %collective-permute-start.5 = (f32[2,128,2]{1,2,0:T(2,128)S(1)}, f32[2,128,2]{1,2,0:T(2,128)S(1)}, u32[]{:S(2)}, u32[]{:S(2)}) collective-permute-start(f32[2,128,2]{1,2,0:T(2,128)S(1)} %fusion.5), channel_id=1, source_target_pairs={{0,1},{1,0},{2,3},{3,2},{4,5},{5,4},{6,7},{7,6},{8,9},{9,8},{10,11... | collective-permute-start | bytes 6152 | tf_op jit(solution)/shard_map/ppermute | solution.py:359
  63.6 4.4 %collective-permute-start.6 = (f32[2,128,2]{1,2,0:T(2,128)S(1)}, f32[2,128,2]{1,2,0:T(2,128)S(1)}, u32[]{:S(2)}, u32[]{:S(2)}) collective-permute-start(f32[2,128,2]{1,2,0:T(2,128)S(1)} %add.55), channel_id=1, source_target_pairs={{0,2},{1,3},{2,0},{3,1},{4,6},{5,7},{6,4},{7,5},{8,10},{9,11},{10,... | collective-permute-start | bytes 6152 | tf_op jit(solution)/shard_map/ppermute | solution.py:359
  64.6 4.5 %collective-permute-start.7 = (f32[2,128,2]{1,2,0:T(2,128)S(1)}, f32[2,128,2]{1,2,0:T(2,128)S(1)}, u32[]{:S(2)}, u32[]{:S(2)}) collective-permute-start(f32[2,128,2]{1,2,0:T(2,128)S(1)} %add.55), channel_id=1, source_target_pairs={{0,4},{1,5},{2,6},{3,7},{4,0},{5,1},{6,2},{7,3},{8,12},{9,13},{10,... | collective-permute-start | bytes 6152 | tf_op jit(solution)/shard_map/ppermute | solution.py:359
  65.3 5.4 %collective-permute-start.8 = (f32[2,128,2]{1,2,0:T(2,128)S(1)}, f32[2,128,2]{1,2,0:T(2,128)S(1)}, u32[]{:S(2)}, u32[]{:S(2)}) collective-permute-start(f32[2,128,2]{1,2,0:T(2,128)S(1)} %add.55), channel_id=1, source_target_pairs={{0,6},{1,7},{2,4},{3,5},{4,2},{5,3},{6,0},{7,1},{8,14},{9,15},{10,... | collective-permute-start | bytes 6152 | tf_op jit(solution)/shard_map/ppermute | solution.py:359
  71.4 4.0 %collective-permute-start.9 = (bf16[1,2,7808]{2,1,0:T(2,128)(2,1)S(1)}, bf16[1,2,7808]{2,1,0:T(2,128)(2,1)S(1)}, u32[]{:S(2)}, u32[]{:S(2)}) collective-permute-start(bf16[1,2,7808]{2,1,0:T(2,128)(2,1)S(1)} %slice.43), channel_id=1, source_target_pairs={{0,16},{8,24},{16,0},{24,8},{1,17},{9,25},{17,1},{25,9},{2,18},{10... | collective-permute-start | bytes 93704 | tf_op jit(solution)/shard_map/ppermute | solution.py:359

commit v5 on v4

--- a/solution.py
+++ b/solution.py
@@ -362,7 +362,7 @@
 def sum_over(value, axis, size):
     near = 1
     while near < size:
-        radix = 2 if (size // near).bit_length() % 2 == 0 else 4
+        radix = 4 if size // near >= 4 else 2
         if radix == 2:
             value = value + xor_permute(value, axis, size, near)
         else:

time: 76.6 us -> 76.4 us (level)
  transfers between devices with their start and end apart: 12 -> 12, of which waited for: 8 -> 9; matrix products, arithmetic and copies ran while one was open for 10% -> 10% of each run, Pallas kernels for 9% -> 9%
where the time goes in v5:
time: 76.4 us; the launch traced here: 75.8 us
  waiting for transfers between devices  25 us (33%)
  starting transfers between devices  20.1 us (26%)
  Pallas kernels  13.1 us (17%)
  local copies, waits for them, and re-layouts  9.04 us (12%)
  other arithmetic  5.28 us (7%)
  matrix products  1.9 us (2%)
  between operations  1.48 us (2%)
    ppermute x10, waiting for transfers between devices, xor_permute(): lax.ppermute(value, axis, [(source, source ^ distance) for source in rang...  12.4 us
    pallas_call x5, Pallas kernels, call(): pl.pallas_call(kernel, out_shape=out_shape, in_specs=[pl.BlockSpec(memory...  11.2 us
    ppermute x10, starting transfers between devices, xor_permute(): lax.ppermute(value, axis, [(source, source ^ distance) for source in rang...  10.6 us
    all_to_all x1, waiting for transfers between devices, on_device(): field = lax.all_to_all(field, 'pw', split_axis=0, concat_axis=0, tiled=True)  8.61 us
    all_to_all x1, starting transfers between devices, on_device(): field = lax.all_to_all(field, 'pw', split_axis=0, concat_axis=0, tiled=True)  5.81 us
    unnamed x29, local copies, waits for them, and re-layouts  4.39 us
    all_to_all x1, waiting for transfers between devices, on_device(): lax.all_to_all(returned, 'pw', split_axis=0, concat_axis=0, tiled=True)  3.95 us
    all_to_all x1, starting transfers between devices, on_device(): lax.all_to_all(returned, 'pw', split_axis=0, concat_axis=0, tiled=True)  3.64 us
  transfers between devices with their start and end apart: 12, of which 9 were waited for; matrix products, arithmetic and copies ran while one was open for 10% of the time, Pallas kernels for 9%

profile of v5, /device:TPU:0, one launch (start us, length us, event | category | flops | bytes accessed | tf_op | source)
XLA Modules:
  0.0 75.8 jit_solution(4512757073237437533)
XLA Ops:
  1.3 1.0 %constant_dynamic-slice_fusion = (bf16[1,2,7808]{2,1,0:T(2,128)(2,1)S(1)}, bf16[1,2,7808]{2,1,0:T(2,128)(2,1)S(1)}, bf16[1,2,7808]{2,1,0:T(2,128)(2,1)S(1)}, bf16[1,2,7808]{2,1,0:T(2,128)(2,1)S(1)}) fusion(bf16[64,2,7808]{2,1,0:T(2,128)(2,1)} %mine_ref, s32[]{:T(128)S(6)} %min.16, s32[]{:T(128)S(6)} %min.15, s32[]{:T(128)S(6)} %min.14, s32[]{:T(128)S(6)} %min.13), kind=kLoop, calls=%fused_computation.28 | loop fusion | bytes 249872 | tf_op jit(solution)/shard_map/dynamic_slice | solution.py:388
  2.8 2.6 %collective-permute-start.1 = (bf16[1,2,7808]{2,1,0:T(2,128)(2,1)S(1)}, bf16[1,2,7808]{2,1,0:T(2,128)(2,1)S(1)}, u32[]{:S(2)}, u32[]{:S(2)}) collective-permute-start(bf16[1,2,7808]{2,1,0:T(2,128)(2,1)S(1)} %get-tuple-element.35), channel_id=1, source_target_pairs={{0,16},{8,24},{16,0},{24,8},{1,17},{9,25},{17,1},{25,9},{2,18},{10... | collective-permute-start | bytes 93704 | tf_op jit(solution)/shard_map/ppermute | solution.py:359
  5.5 0.8 copy-done.5
  6.2 0.8 copy-done.7
  7.4 1.4 %collective-permute-done.2.refs_3_ = bf16[1,2,7808]{2,1,0:T(2,128)(2,1)S(1)} collective-permute-done((bf16[1,2,7808]{2,1,0:T(2,128)(2,1)S(1)}, bf16[1,2,7808]{2,1,0:T(2,128)(2,1)S(1)}, u32[]{:S(2)}, u32[]{:S(2)}) %collective-permute-start.2) | collective-permute-done | bytes 31264 | tf_op jit(solution)/shard_map/ppermute | solution.py:359
  8.7 3.3 %shard_map.132 = bf16[8,128,256]{2,1,0:T(8,128)(2,1)} custom-call(s32[1]{0:T(128)} %bitcast.1.choice_ref, s32[1,7808]{1,0:T(1,128)S(1)} %get-tuple-element.18.row_ref, s32[1,7808]{1,0:T(1,128)S(1)} %get-tuple-element.19.z_ref, bf16[1,2,7808]{2,1,0:T(2,128)(2,1)S(1)} %get-tuple-element.20.resp_ref, bf16[1,2,7808]{2,1,0:T(2,128)(2,1)S(1)} %get-tuple-element.37.refs_0_, ...), custom_call_target="tpu_custom_call" | custom-call | flops 4294967296 | bytes 4194304 | tf_op jit(solution)/shard_map/pallas_call | solution.py:348
  12.2 5.8 %all-to-all-start = ((bf16[8,128,256]{2,1,0:T(8,128)(2,1)}), bf16[8,128,256]{2,1,0:T(8,128)(2,1)S(1)}, u32[]{:S(2)}, u32[]{:S(2)}) async-start(bf16[8,128,256]{2,1,0:T(8,128)(2,1)} %shard_map.132), calls=%async_computation | async-start | bytes 1048576 | tf_op jit(solution)/shard_map/all_to_all | solution.py:429
  18.0 3.4 %convert_bitcast_fusion = (bf16[20,160,160]{2,1,0:T(8,128)(2,1)S(1)}, bf16[20,160,160]{2,1,0:T(8,128)(2,1)S(1)}) fusion(f32[160,20,160]{2,0,1:T(8,128)} %param.18, f32[160,20,160]{2,0,1:T(8,128)} %param.17), kind=kLoop, calls=%fused_computation.6 | loop fusion | flops 1024000 | bytes 6144000 | tf_op jit(solution)/shard_map/convert_element_type | solution.py:423
  21.4 1.5 %pad.7.pot_ref = bf16[20,160,256]{2,1,0:T(8,128)(2,1)} pad(bf16[20,160,160]{2,1,0:T(8,128)(2,1)S(1)} %get-tuple-element.50, bf16[]{:T(256)} %constant.46.clone.1), padding=0_0x0_0x0_96 | pad | bytes 2662402 | tf_op jit(solution)/shard_map/jit(_pad)/pad | solution.py:423
  22.9 1.5 %pad.8.con_ref = bf16[20,160,256]{2,1,0:T(8,128)(2,1)} pad(bf16[20,160,160]{2,1,0:T(8,128)(2,1)S(1)} %get-tuple-element.49, bf16[]{:T(256)} %constant.46.clone.1), padding=0_0x0_0x0_96 | pad | bytes 2662402 | tf_op jit(solution)/shard_map/jit(_pad)/pad | solution.py:423
  24.4 8.6 %all-to-all-done.in_ref = bf16[8,128,256]{2,1,0:T(8,128)(2,1)S(1)} async-done(((bf16[8,128,256]{2,1,0:T(8,128)(2,1)}), bf16[8,128,256]{2,1,0:T(8,128)(2,1)S(1)}, u32[]{:S(2)}, u32[]{:S(2)}) %all-to-all-start) | async-done | bytes 524320 | tf_op jit(solution)/shard_map/all_to_all | solution.py:429
  33.0 0.9 %shard_map.133.wide_ref = bf16[2,20,160,128]{3,2,1,0:T(8,128)(2,1)S(1)} custom-call(bf16[8,128,256]{2,1,0:T(8,128)(2,1)S(1)} %all-to-all-done.in_ref, bf16[160,128]{1,0:T(8,128)(2,1)S(1)} %copy-done.12), custom_call_target="tpu_custom_call" | custom-call | flops 2147483648 | bytes 4194304 | tf_op jit(solution)/shard_map/pallas_call | solution.py:348
  34.9 3.9 %shard_map.134 = bf16[8,128,128]{2,1,0:T(8,128)(2,1)} custom-call(bf16[2,20,160,128]{3,2,1,0:T(8,128)(2,1)S(1)} %shard_map.133.wide_ref, bf16[20,160,256]{2,1,0:T(8,128)(2,1)S(1)} %copy-done.3, bf16[20,160,256]{2,1,0:T(8,128)(2,1)S(1)} %copy-done.4, bf16[128,160]{1,0:T(8,128)(2,1)S(1)} %copy-done.10, bf16[2,128,256]{2,1,0:T(8,128)(2,1)S(1)} %copy-done.8, ...), custom_call_target="tpu_custom_call" | custom-call | flops 4294967296 | bytes 4194304 | tf_op jit(solution)/shard_map/pallas_call | solution.py:348
  38.8 3.6 %all-to-all-start.1 = ((bf16[8,128,128]{2,1,0:T(8,128)(2,1)}), bf16[8,128,128]{2,1,0:T(8,128)(2,1)S(1)}, u32[]{:S(2)}, u32[]{:S(2)}) async-start(bf16[8,128,128]{2,1,0:T(8,128)(2,1)} %shard_map.134), calls=%async_computation.1 | async-start | bytes 524288 | tf_op jit(solution)/shard_map/all_to_all | solution.py:465
  43.0 0.7 add_reduce_fusion
  43.8 1.9 %shard_map.135 = bf16[128,2,7808]{2,1,0:T(2,128)(2,1)S(1)} custom-call(bf16[64,2,7808]{2,1,0:T(2,128)(2,1)S(1)} %copy-done.2, bf16[64,2,7808]{2,1,0:T(2,128)(2,1)} %collective-permute-done.3.other_ref), custom_call_target="tpu_custom_call" | custom-call | bytes 8388608 | tf_op jit(solution)/shard_map/pallas_call | solution.py:456
  45.7 1.9 %copy-done = bf16[128,2,7808]{2,1,0:T(2,128)(2,1)} copy-done((bf16[128,2,7808]{2,1,0:T(2,128)(2,1)}, bf16[128,2,7808]{2,1,0:T(2,128)(2,1)S(1)}, u32[]{:S(2)}) %copy-start) | copy-done | bytes 3997720
  47.6 3.9 %all-to-all-done.1.in_ref = bf16[8,128,128]{2,1,0:T(8,128)(2,1)S(1)} async-done(((bf16[8,128,128]{2,1,0:T(8,128)(2,1)}), bf16[8,128,128]{2,1,0:T(8,128)(2,1)S(1)}, u32[]{:S(2)}, u32[]{:S(2)}) %all-to-all-start.1) | async-done | bytes 262176 | tf_op jit(solution)/shard_map/all_to_all | solution.py:465
  51.5 2.7 %shard_map.136 = (bf16[1,2,7808]{2,1,0:T(2,128)(2,1)S(1)}, f32[1,2,7808]{2,1,0:T(2,128)S(1)}) custom-call(bf16[8,128,128]{2,1,0:T(8,128)(2,1)S(1)} %all-to-all-done.1.in_ref, s32[1,7808]{1,0:T(1,128)S(1)} %get-tuple-element.18.row_ref, s32[1,7808]{1,0:T(1,128)S(1)} %get-tuple-element.19.z_ref, bf16[1,2,7808]{2,1,0:T(2,128)(2,1)S(1)} %copy-done.6, ...), custom_call_target="tpu_custom_call" | custom-call | flops 4294967296 | bytes 4194304 | tf_op jit(solution)/shard_map/pallas_call | solution.py:348
  54.3 0.9 %collective-permute-start.4 = (bf16[1,2,7808]{2,1,0:T(2,128)(2,1)S(1)}, bf16[1,2,7808]{2,1,0:T(2,128)(2,1)S(1)}, u32[]{:S(2)}, u32[]{:S(2)}) collective-permute-start(bf16[1,2,7808]{2,1,0:T(2,128)(2,1)S(1)} %get-tuple-element.32), channel_id=1, source_target_pairs={{0,16},{8,24},{16,0},{24,8},{1,17},{9,25},{17,1},{25,9},{2,18},{10... | collective-permute-start | bytes 93704 | tf_op jit(solution)/shard_map/ppermute | solution.py:359
  55.2 3.0 %collective-permute-done.4 = bf16[1,2,7808]{2,1,0:T(2,128)(2,1)S(1)} collective-permute-done((bf16[1,2,7808]{2,1,0:T(2,128)(2,1)S(1)}, bf16[1,2,7808]{2,1,0:T(2,128)(2,1)S(1)}, u32[]{:S(2)}, u32[]{:S(2)}) %collective-permute-start.4) | collective-permute-done | bytes 31264 | tf_op jit(solution)/shard_map/ppermute | solution.py:359
  58.7 1.2 %fusion.5 = f32[2,128,2]{1,2,0:T(2,128)S(1)} fusion(bf16[128,2,7808]{2,1,0:T(2,128)(2,1)S(1)} %copy-done.1, bf16[2,2,2,7808]{3,2,1,0:T(2,128)(2,1)S(1)} %pad_maximum_fusion), kind=kOutput, calls=%fused_computation.8 | convolution fusion | flops 15990784 | bytes 4124672 | tf_op jit(solution)/shard_map/mcj,dncj->dmn/dot_general | solution.py:485
  60.0 1.4 %collective-permute-start.5 = (f32[2,128,2]{1,2,0:T(2,128)S(1)}, f32[2,128,2]{1,2,0:T(2,128)S(1)}, u32[]{:S(2)}, u32[]{:S(2)}) collective-permute-start(f32[2,128,2]{1,2,0:T(2,128)S(1)} %fusion.5), channel_id=1, source_target_pairs={{0,1},{1,0},{2,3},{3,2},{4,5},{5,4},{6,7},{7,6},{8,9},{9,8},{10,11... | collective-permute-start | bytes 6152 | tf_op jit(solution)/shard_map/ppermute | solution.py:359
  61.5 2.0 %collective-permute-start.7 = (f32[2,128,2]{1,2,0:T(2,128)S(1)}, f32[2,128,2]{1,2,0:T(2,128)S(1)}, u32[]{:S(2)}, u32[]{:S(2)}) collective-permute-start(f32[2,128,2]{1,2,0:T(2,128)S(1)} %fusion.5), channel_id=1, source_target_pairs={{0,3},{1,2},{2,1},{3,0},{4,7},{5,6},{6,5},{7,4},{8,11},{9,10},{10,... | collective-permute-start | bytes 6152 | tf_op jit(solution)/shard_map/ppermute | solution.py:359
  63.6 1.4 %collective-permute-done.6 = f32[2,128,2]{1,2,0:T(2,128)S(1)} collective-permute-done((f32[2,128,2]{1,2,0:T(2,128)S(1)}, f32[2,128,2]{1,2,0:T(2,128)S(1)}, u32[]{:S(2)}, u32[]{:S(2)}) %collective-permute-start.6) | collective-permute-done | bytes 2080 | tf_op jit(solution)/shard_map/ppermute | solution.py:359
  65.0 1.0 %collective-permute-done.7 = f32[2,128,2]{1,2,0:T(2,128)S(1)} collective-permute-done((f32[2,128,2]{1,2,0:T(2,128)S(1)}, f32[2,128,2]{1,2,0:T(2,128)S(1)}, u32[]{:S(2)}, u32[]{:S(2)}) %collective-permute-start.7) | collective-permute-done | bytes 2080 | tf_op jit(solution)/shard_map/ppermute | solution.py:359
  66.0 2.0 %collective-permute-start.8 = (f32[2,128,2]{1,2,0:T(2,128)S(1)}, f32[2,128,2]{1,2,0:T(2,128)S(1)}, u32[]{:S(2)}, u32[]{:S(2)}) collective-permute-start(f32[2,128,2]{1,2,0:T(2,128)S(1)} %add_add_fusion), channel_id=1, source_target_pairs={{0,4},{1,5},{2,6},{3,7},{4,0},{5,1},{6,2},{7,3},{8,12},{9,13},{10,... | collective-permute-start | bytes 6152 | tf_op jit(solution)/shard_map/ppermute | solution.py:359
  67.9 2.5 %collective-permute-done.8 = f32[2,128,2]{1,2,0:T(2,128)S(1)} collective-permute-done((f32[2,128,2]{1,2,0:T(2,128)S(1)}, f32[2,128,2]{1,2,0:T(2,128)S(1)}, u32[]{:S(2)}, u32[]{:S(2)}) %collective-permute-start.8) | collective-permute-done | bytes 2080 | tf_op jit(solution)/shard_map/ppermute | solution.py:359
  70.5 0.6 convolution_bitcast_fusion
  71.2 0.9 %collective-permute-start.9 = (bf16[1,2,7808]{2,1,0:T(2,128)(2,1)S(1)}, bf16[1,2,7808]{2,1,0:T(2,128)(2,1)S(1)}, u32[]{:S(2)}, u32[]{:S(2)}) collective-permute-start(bf16[1,2,7808]{2,1,0:T(2,128)(2,1)S(1)} %slice.43), channel_id=1, source_target_pairs={{0,16},{8,24},{16,0},{24,8},{1,17},{9,25},{17,1},{25,9},{2,18},{10... | collective-permute-start | bytes 93704 | tf_op jit(solution)/shard_map/ppermute | solution.py:359
  72.1 3.1 %collective-permute-done.9 = bf16[1,2,7808]{2,1,0:T(2,128)(2,1)S(1)} collective-permute-done((bf16[1,2,7808]{2,1,0:T(2,128)(2,1)S(1)}, bf16[1,2,7808]{2,1,0:T(2,128)(2,1)S(1)}, u32[]{:S(2)}, u32[]{:S(2)}) %collective-permute-start.9) | collective-permute-done | bytes 31264 | tf_op jit(solution)/shard_map/ppermute | solution.py:359
  75.1 0.7 fusion.10
  (46 shorter events, 3.4 us)
Async XLA Ops:
  2.3 5.1 %collective-permute-start = (bf16[1,2,7808]{2,1,0:T(2,128)(2,1)S(1)}, bf16[1,2,7808]{2,1,0:T(2,128)(2,1)S(1)}, u32[]{:S(2)}, u32[]{:S(2)}) collective-permute-start(bf16[1,2,7808]{2,1,0:T(2,128)(2,1)S(1)} %get-tuple-element.36), channel_id=1, source_target_pairs={{0,8},{8,0},{16,24},{24,16},{1,9},{9,1},{17,25},{25,17},{2,10},{10... | collective-permute-start | bytes 93704 | tf_op jit(solution)/shard_map/ppermute | solution.py:359
  2.8 4.6 %collective-permute-start.1 = (bf16[1,2,7808]{2,1,0:T(2,128)(2,1)S(1)}, bf16[1,2,7808]{2,1,0:T(2,128)(2,1)S(1)}, u32[]{:S(2)}, u32[]{:S(2)}) collective-permute-start(bf16[1,2,7808]{2,1,0:T(2,128)(2,1)S(1)} %get-tuple-element.35), channel_id=1, source_target_pairs={{0,16},{8,24},{16,0},{24,8},{1,17},{9,25},{17,1},{25,9},{2,18},{10... | collective-permute-start | bytes 93704 | tf_op jit(solution)/shard_map/ppermute | solution.py:359
  5.4 3.3 %collective-permute-start.2 = (bf16[1,2,7808]{2,1,0:T(2,128)(2,1)S(1)}, bf16[1,2,7808]{2,1,0:T(2,128)(2,1)S(1)}, u32[]{:S(2)}, u32[]{:S(2)}) collective-permute-start(bf16[1,2,7808]{2,1,0:T(2,128)(2,1)S(1)} %get-tuple-element.34), channel_id=1, source_target_pairs={{0,24},{8,16},{16,8},{24,0},{1,25},{9,17},{17,9},{25,1},{2,26},{10... | collective-permute-start | bytes 93704 | tf_op jit(solution)/shard_map/ppermute | solution.py:359
  5.5 0.8 copy-start.5
  6.2 0.8 copy-start.7
  8.7 3.3 %copy-start.2 = (bf16[64,2,7808]{2,1,0:T(2,128)(2,1)S(1)}, bf16[64,2,7808]{2,1,0:T(2,128)(2,1)}, u32[]{:S(2)}) copy-start(bf16[64,2,7808]{2,1,0:T(2,128)(2,1)} %mine_ref) | copy-start | bytes 5996548
  12.0 26.8 %collective-permute-start.3 = (bf16[64,2,7808]{2,1,0:T(2,128)(2,1)S(1)}, bf16[64,2,7808]{2,1,0:T(2,128)(2,1)}, u32[]{:S(2)}, u32[]{:S(2)}) collective-permute-start(bf16[64,2,7808]{2,1,0:T(2,128)(2,1)S(1)} %copy-done.2), channel_id=1, source_target_pairs={{0,8},{8,0},{16,24},{24,16},{1,9},{9,1},{17,25},{25,17},{2,10},{10... | collective-permute-start | bytes 5996552 | tf_op jit(solution)/shard_map/ppermute | solution.py:359
  12.2 20.8 %all-to-all-start = ((bf16[8,128,256]{2,1,0:T(8,128)(2,1)}), bf16[8,128,256]{2,1,0:T(8,128)(2,1)S(1)}, u32[]{:S(2)}, u32[]{:S(2)}) async-start(bf16[8,128,256]{2,1,0:T(8,128)(2,1)} %shard_map.132), calls=%async_computation | async-start | bytes 1048576 | tf_op jit(solution)/shard_map/all_to_all | solution.py:429
  21.4 11.6 %copy-start.12 = (bf16[160,128]{1,0:T(8,128)(2,1)S(1)}, bf16[160,128]{1,0:T(8,128)(2,1)}, u32[]{:S(2)}) copy-start(bf16[160,128]{1,0:T(8,128)(2,1)} %constant.50.clone.up_x_ref) | copy-start | bytes 122884
  24.4 9.6 %copy-start.8 = (bf16[2,128,256]{2,1,0:T(8,128)(2,1)S(1)}, bf16[2,128,256]{2,1,0:T(8,128)(2,1)}, u32[]{:S(2)}) copy-start(bf16[2,128,256]{2,1,0:T(8,128)(2,1)} %constant.52.clone.up_z_ref) | copy-start | bytes 393220
  24.4 9.6 %copy-start.9 = (bf16[512,128]{1,0:T(8,128)(2,1)S(1)}, bf16[512,128]{1,0:T(8,128)(2,1)}, u32[]{:S(2)}) copy-start(bf16[512,128]{1,0:T(8,128)(2,1)} %constant.53.clone.down_z_ref) | copy-start | bytes 393220
  24.4 9.6 %copy-start.10 = (bf16[128,160]{1,0:T(8,128)(2,1)S(1)}, bf16[128,160]{1,0:T(8,128)(2,1)}, u32[]{:S(2)}) copy-start(bf16[128,160]{1,0:T(8,128)(2,1)} %constant.51.clone.down_x_ref) | copy-start | bytes 122884
  33.0 1.4 %copy-start.3 = (bf16[20,160,256]{2,1,0:T(8,128)(2,1)S(1)}, bf16[20,160,256]{2,1,0:T(8,128)(2,1)}, u32[]{:S(2)}) copy-start(bf16[20,160,256]{2,1,0:T(8,128)(2,1)} %pad.7.pot_ref) | copy-start | bytes 4915204
  33.0 1.9 %copy-start.4 = (bf16[20,160,256]{2,1,0:T(8,128)(2,1)S(1)}, bf16[20,160,256]{2,1,0:T(8,128)(2,1)}, u32[]{:S(2)}) copy-start(bf16[20,160,256]{2,1,0:T(8,128)(2,1)} %pad.8.con_ref) | copy-start | bytes 4915204
  34.9 7.5 %copy-start.13 = (f32[256]{0:T(256)S(1)}, f32[256]{0:T(256)}, u32[]{:S(2)}) copy-start(f32[256]{0:T(256)} %param.14) | copy-start | bytes 3076
  38.8 12.7 %all-to-all-start.1 = ((bf16[8,128,128]{2,1,0:T(8,128)(2,1)}), bf16[8,128,128]{2,1,0:T(8,128)(2,1)S(1)}, u32[]{:S(2)}, u32[]{:S(2)}) async-start(bf16[8,128,128]{2,1,0:T(8,128)(2,1)} %shard_map.134), calls=%async_computation.1 | async-start | bytes 524288 | tf_op jit(solution)/shard_map/all_to_all | solution.py:465
  43.8 7.8 %copy-start.6 = (bf16[1,2,7808]{2,1,0:T(2,128)(2,1)S(1)}, bf16[1,2,7808]{2,1,0:T(2,128)(2,1)}, u32[]{:S(2)}) copy-start(bf16[1,2,7808]{2,1,0:T(2,128)(2,1)} %resp_ref.3) | copy-start | bytes 93700
  43.8 7.8 %copy-start.11 = (bf16[112,160]{1,0:T(8,128)(2,1)S(1)}, bf16[112,160]{1,0:T(8,128)(2,1)}, u32[]{:S(2)}) copy-start(bf16[112,160]{1,0:T(8,128)(2,1)} %constant.49.clone.down_y_ref) | copy-start | bytes 107524
  45.7 1.9 %copy-start = (bf16[128,2,7808]{2,1,0:T(2,128)(2,1)}, bf16[128,2,7808]{2,1,0:T(2,128)(2,1)S(1)}, u32[]{:S(2)}) copy-start(bf16[128,2,7808]{2,1,0:T(2,128)(2,1)S(1)} %shard_map.135) | copy-start | bytes 11993092
  51.5 7.2 %copy-start.1 = (bf16[128,2,7808]{2,1,0:T(2,128)(2,1)S(1)}, bf16[128,2,7808]{2,1,0:T(2,128)(2,1)}, u32[]{:S(2)}) copy-start(bf16[128,2,7808]{2,1,0:T(2,128)(2,1)} %copy-done) | copy-start | bytes 11993092
  54.3 4.0 %collective-permute-start.4 = (bf16[1,2,7808]{2,1,0:T(2,128)(2,1)S(1)}, bf16[1,2,7808]{2,1,0:T(2,128)(2,1)S(1)}, u32[]{:S(2)}, u32[]{:S(2)}) collective-permute-start(bf16[1,2,7808]{2,1,0:T(2,128)(2,1)S(1)} %get-tuple-element.32), channel_id=1, source_target_pairs={{0,16},{8,24},{16,0},{24,8},{1,17},{9,25},{17,1},{25,9},{2,18},{10... | collective-permute-start | bytes 93704 | tf_op jit(solution)/shard_map/ppermute | solution.py:359
  60.0 3.6 %collective-permute-start.5 = (f32[2,128,2]{1,2,0:T(2,128)S(1)}, f32[2,128,2]{1,2,0:T(2,128)S(1)}, u32[]{:S(2)}, u32[]{:S(2)}) collective-permute-start(f32[2,128,2]{1,2,0:T(2,128)S(1)} %fusion.5), channel_id=1, source_target_pairs={{0,1},{1,0},{2,3},{3,2},{4,5},{5,4},{6,7},{7,6},{8,9},{9,8},{10,11... | collective-permute-start | bytes 6152 | tf_op jit(solution)/shard_map/ppermute | solution.py:359
  61.4 3.6 %collective-permute-start.6 = (f32[2,128,2]{1,2,0:T(2,128)S(1)}, f32[2,128,2]{1,2,0:T(2,128)S(1)}, u32[]{:S(2)}, u32[]{:S(2)}) collective-permute-start(f32[2,128,2]{1,2,0:T(2,128)S(1)} %fusion.5), channel_id=1, source_target_pairs={{0,2},{1,3},{2,0},{3,1},{4,6},{5,7},{6,4},{7,5},{8,10},{9,11},{10,... | collective-permute-start | bytes 6152 | tf_op jit(solution)/shard_map/ppermute | solution.py:359
  61.5 4.5 %collective-permute-start.7 = (f32[2,128,2]{1,2,0:T(2,128)S(1)}, f32[2,128,2]{1,2,0:T(2,128)S(1)}, u32[]{:S(2)}, u32[]{:S(2)}) collective-permute-start(f32[2,128,2]{1,2,0:T(2,128)S(1)} %fusion.5), channel_id=1, source_target_pairs={{0,3},{1,2},{2,1},{3,0},{4,7},{5,6},{6,5},{7,4},{8,11},{9,10},{10,... | collective-permute-start | bytes 6152 | tf_op jit(solution)/shard_map/ppermute | solution.py:359
  66.0 4.5 %collective-permute-start.8 = (f32[2,128,2]{1,2,0:T(2,128)S(1)}, f32[2,128,2]{1,2,0:T(2,128)S(1)}, u32[]{:S(2)}, u32[]{:S(2)}) collective-permute-start(f32[2,128,2]{1,2,0:T(2,128)S(1)} %add_add_fusion), channel_id=1, source_target_pairs={{0,4},{1,5},{2,6},{3,7},{4,0},{5,1},{6,2},{7,3},{8,12},{9,13},{10,... | collective-permute-start | bytes 6152 | tf_op jit(solution)/shard_map/ppermute | solution.py:359
  71.2 4.0 %collective-permute-start.9 = (bf16[1,2,7808]{2,1,0:T(2,128)(2,1)S(1)}, bf16[1,2,7808]{2,1,0:T(2,128)(2,1)S(1)}, u32[]{:S(2)}, u32[]{:S(2)}) collective-permute-start(bf16[1,2,7808]{2,1,0:T(2,128)(2,1)S(1)} %slice.43), channel_id=1, source_target_pairs={{0,16},{8,24},{16,0},{24,8},{1,17},{9,25},{17,1},{25,9},{2,18},{10... | collective-permute-start | bytes 93704 | tf_op jit(solution)/shard_map/ppermute | solution.py:359
